TPU v7x, 32 devices: a whole 2x2x4 slice. The times are simulated.
32 devices in a mesh: tok: 16 (over z, x, core), ch: 2 (over y).
Axes of the slice: x: 2, y: 2, z: 4, core: 2. Of those that a mesh axis runs over, the one named last changes fastest.
Arguments:
- tokens: bfloat16 [2, 36864, 320], P(None, ('tok', 'ch')), may hold values from -6 to 6
- grad_output: bfloat16 [2, 36864, 320], P(None, ('tok', 'ch')), may hold values from -6 to 6
- valid_tiles: int32 [2, 64, 9], P(None, ('tok', 'ch')), may hold values 0 or 1
- master_a: float32 [320, 2560], replicated
- master_b: float32 [1280, 640], replicated
- vector_params: float32 [55, 320], replicated
- matrix_first: float32 [32, 51200], P(('tok', 'ch')), may hold values from -29.182657 to 29.182657
- matrix_second: float32 [32, 51200], P(('tok', 'ch')), may hold values from 1.92 to 7.68
- vector_first: float32 [55, 320], replicated, may hold values from -73.826935 to 73.826935
- vector_second: float32 [55, 320], replicated, may hold values from 12.288 to 49.152
- left_a: int32 [4, 320], replicated, may hold values from 0 to 639, as said below
- right_a: int32 [2560], replicated, may hold values from 0 to 5119, as said below
- left_b: int32 [2, 1280], replicated, may hold values from 0 to 2559, as said below
- right_b: int32 [640], replicated, may hold values from 0 to 1279, as said below
- owner_list: int32 [32], replicated, may hold values from 0 to 31, each once
- step_count: int32 [1], replicated, may hold values from 2 to 20
Outputs:
- block_output: bfloat16 [2, 36864, 320], P(None, ('tok', 'ch'))
- input_grad: float32 [2, 36864, 320], P(None, ('tok', 'ch'))
- matrix_grad: float32 [32, 51200], P(('tok', 'ch'))
- matrix_first_new: float32 [32, 51200], P(('tok', 'ch'))
- matrix_second_new: float32 [32, 51200], P(('tok', 'ch'))
- new_master_a: float32 [320, 2560], replicated
- new_master_b: float32 [1280, 640], replicated
- new_copy_a: bfloat16 [320, 2560], replicated
- new_copy_b: bfloat16 [1280, 640], replicated
- vector_grad: float32 [55, 320], replicated
- vector_first_new: float32 [55, 320], replicated
- vector_second_new: float32 [55, 320], replicated
- new_vectors: float32 [55, 320], replicated
Inputs may be any that keep to these rules, and one draw needn't show every extreme that they name: `left_a`: each row holds codes 2 p + s, with p running over a permutation of 0 .. 319 and s in 0, 1. `right_a`: codes 2 p + s, s in 0, 1, where the indices p of each matrix's columns form a permutation of that matrix's own columns. `left_b`: each row holds codes 2 p + s, with p running over a permutation of 0 .. 1279 and s in 0, 1. `right_b`: codes 2 p + s, s in 0, 1, where the indices p of each matrix's columns form a permutation of that matrix's own columns.
All inputs are finite; a program needn't handle non-finite values. No bound on the sum of `valid_tiles` on one device may be relied on, other than what follows from the above.
Results may differ from a plain program's by a relative error of at most 0.014.
Values may be sent and summed in bfloat16 or wider, within the bound.
A program may use at most 192 MiB of HBM per device.

v0:
```python
import jax
import jax.numpy as jnp
from jax import lax
from jax.sharding import PartitionSpec as P

HEADS = 5
HEAD_DIM = 64
SIDE = 24
TILE = 8


beta_one = 0.9
beta_two = 0.999
adam_epsilon = 1e-08
norm_epsilon = 1e-05
matrix_rate = 0.05
vector_rate = 0.2
weight_decay = 0.01


def layer_norm(values, gain_row, shift_row):
    center = values - jnp.mean(values, axis=-1, keepdims=True)
    inverse_std = lax.rsqrt(jnp.mean(center * center, axis=-1, keepdims=True) + norm_epsilon)
    normal_part = center * inverse_std
    return (normal_part * gain_row + shift_row, normal_part, inverse_std)


def norm_backward(upstream, normal_part, inverse_std, gain_row):
    scaled = upstream * gain_row
    inner_term = jnp.mean(scaled * normal_part, axis=-1, keepdims=True)
    result = inverse_std * (
        scaled - jnp.mean(scaled, axis=-1, keepdims=True) - normal_part * inner_term
    )
    return (result, jnp.sum(upstream * normal_part, axis=0), jnp.sum(upstream, axis=0))


def inner_rows(left_side, right_side):
    return lax.dot_general(
        left_side, right_side, (((0,), (0,)), ((), ())), preferred_element_type=jnp.float32
    )


def times_transposed(left_side, right_side):
    return lax.dot_general(
        left_side, right_side, (((1,), (1,)), ((), ())), preferred_element_type=jnp.float32
    )


def tile_numbers():
    position = jnp.arange(SIDE * SIDE)
    grid_row = position // SIDE
    grid_col = position % SIDE
    per_side = SIDE // TILE
    return (grid_row, grid_col, grid_row // TILE * per_side + grid_col // TILE)


def slot_valid(tile_flags):
    grid_row, grid_col, owner_tile = tile_numbers()
    inside = (grid_row % TILE < TILE - 1) & (grid_col % TILE < TILE - 1)
    per_side = SIDE // TILE
    matches = owner_tile[None, :, None] == jnp.arange(per_side * per_side)[None, None, :]
    covered = jnp.sum(jnp.where(matches, tile_flags[:, None, :], 0), axis=-1)
    return jnp.where(inside[None, :], covered, 0).astype(jnp.float32)


def attend_mask():
    grid_row, grid_col, owner_tile = tile_numbers()
    reduced_side = SIDE // 2
    reduced_pos = jnp.arange(reduced_side * reduced_side)
    reduced_tile = reduced_pos // reduced_side // (TILE // 2) * (
        SIDE // TILE
    ) + reduced_pos % reduced_side // (TILE // 2)
    return owner_tile[:, None] == reduced_tile[None, :]


def invert_order(order_codes):
    return (
        jnp.zeros(order_codes.shape, jnp.int32)
        .at[order_codes]
        .set(jnp.arange(order_codes.shape[0], dtype=jnp.int32))
    )


def rotate_group(matrix, left_codes, right_codes, span_sizes):
    right_sign = (1 - 2 * (right_codes % 2)).astype(jnp.float32)
    columns_moved = jnp.take(matrix, right_codes // 2, axis=1) * right_sign
    pieces = []
    offset_start = 0
    for number, span_size in enumerate(span_sizes):
        left_sign = (1 - 2 * (left_codes[number] % 2)).astype(jnp.float32)
        block_part = jnp.take(
            columns_moved[:, offset_start : offset_start + span_size],
            left_codes[number] // 2,
            axis=0,
        )
        pieces.append(block_part * left_sign[:, None])
        offset_start = offset_start + span_size
    return jnp.concatenate(pieces, axis=1)


def restore_group(rotated, left_codes, right_codes, span_sizes):
    pieces = []
    offset_start = 0
    for number, span_size in enumerate(span_sizes):
        left_sign = (1 - 2 * (left_codes[number] % 2)).astype(jnp.float32)
        block_part = rotated[:, offset_start : offset_start + span_size] * left_sign[:, None]
        pieces.append(jnp.take(block_part, invert_order(left_codes[number] // 2), axis=0))
        offset_start = offset_start + span_size
    right_sign = (1 - 2 * (right_codes % 2)).astype(jnp.float32)
    joined = jnp.concatenate(pieces, axis=1) * right_sign
    return jnp.take(joined, invert_order(right_codes // 2), axis=1)


def patch_halves(rows_low, grid_count):
    half_side = SIDE // 2
    model_width = rows_low.shape[1]
    shaped = rows_low.reshape(grid_count * half_side, 2, half_side * 2 * model_width)
    return [
        shaped[:, offset_row].reshape(grid_count * half_side * half_side, 2 * model_width)
        for offset_row in range(2)
    ]


def halves_to_slots(half_rows, grid_count, model_width):
    half_side = SIDE // 2
    shaped = [
        piece.reshape(grid_count * half_side, half_side * 2 * model_width) for piece in half_rows
    ]
    return jnp.stack(shaped, axis=1).reshape(grid_count * SIDE * SIDE, model_width)


def head_scores(query_head, key_head, attend, score_scale):
    raw_scores = (
        jnp.einsum("gqd,gkd->gqk", query_head, key_head, preferred_element_type=jnp.float32)
        * score_scale
    )
    return jnp.where(attend[None], raw_scores, -1000000000.0)


def depthwise(grid_values, tap_rows):
    side_cells = grid_values.shape[1]
    padded = jnp.pad(grid_values, ((0, 0), (1, 1), (1, 1), (0, 0)))
    running = jnp.zeros(grid_values.shape, jnp.float32)
    for offset_row in range(3):
        for offset_col in range(3):
            running = (
                running
                + padded[
                    :, offset_row : offset_row + side_cells, offset_col : offset_col + side_cells
                ]
                * tap_rows[offset_row * 3 + offset_col]
            )
    return running


def depthwise_backward(grad_mixed, grid_values, tap_rows):
    side_cells = grid_values.shape[1]
    padded_values = jnp.pad(grid_values, ((0, 0), (1, 1), (1, 1), (0, 0)))
    padded_grads = jnp.pad(grad_mixed, ((0, 0), (1, 1), (1, 1), (0, 0)))
    tap_grads = []
    running = jnp.zeros(grid_values.shape, jnp.float32)
    for offset_row in range(3):
        for offset_col in range(3):
            window = padded_values[
                :, offset_row : offset_row + side_cells, offset_col : offset_col + side_cells
            ]
            tap_grads.append(jnp.sum(window * grad_mixed, axis=(0, 1, 2)))
            back_window = padded_grads[
                :,
                2 - offset_row : 2 - offset_row + side_cells,
                2 - offset_col : 2 - offset_col + side_cells,
            ]
            running = running + back_window * tap_rows[offset_row * 3 + offset_col]
    return (jnp.stack(tap_grads), running)


def gelu_exact(values):
    return 0.5 * values * (1.0 + lax.erf(values * 0.7071067811865476))


def gelu_slope(values):
    return (
        0.5 * (1.0 + lax.erf(values * 0.7071067811865476))
        + values * jnp.exp(-0.5 * values * values) * 0.3989422804014327
    )


def on_device(
    tokens,
    grad_output,
    valid_tiles,
    master_a,
    master_b,
    vector_params,
    matrix_first,
    matrix_second,
    vector_first,
    vector_second,
    left_a,
    right_a,
    left_b,
    right_b,
    owner_list,
    step_count,
):
    model_width = tokens.shape[2]
    hidden_width = master_b.shape[0]
    ratio_rows = hidden_width // model_width
    weights_a = master_a.astype(jnp.bfloat16)
    weights_b = master_b.astype(jnp.bfloat16)
    w_query = weights_a[:, :model_width]
    w_keyval = weights_a[:, model_width : 3 * model_width]
    w_output = weights_a[:, 3 * model_width : 4 * model_width]
    w_upward = weights_a[:, 4 * model_width :]
    w_reduce = weights_b[:, :model_width]
    reduce_halves = [w_reduce[: 2 * model_width], w_reduce[2 * model_width :]]
    w_downward = weights_b[:, model_width:]
    gain_one = vector_params[0]
    shift_one = vector_params[1]
    bias_query = vector_params[2]
    bias_value = vector_params[3]
    bias_reduce = vector_params[4]
    gain_kv = vector_params[5]
    shift_kv = vector_params[6]
    bias_output = vector_params[7]
    gain_two = vector_params[8]
    shift_two = vector_params[9]
    bias_down = vector_params[10]
    bias_up = vector_params[11 : 11 + ratio_rows].reshape(hidden_width)
    bias_depth = vector_params[11 + ratio_rows : 11 + 2 * ratio_rows].reshape(hidden_width)
    taps_depth = vector_params[11 + 2 * ratio_rows :].reshape(9, hidden_width)
    hidden_share = hidden_width // lax.axis_size("ch")
    offset_start = lax.axis_index("ch") * hidden_share
    up_local = lax.dynamic_slice_in_dim(w_upward, offset_start, hidden_share, 1)
    down_local = lax.dynamic_slice_in_dim(w_downward, offset_start, hidden_share, 0)
    bias_up_local = lax.dynamic_slice_in_dim(bias_up, offset_start, hidden_share, 0)
    bias_depth_local = lax.dynamic_slice_in_dim(bias_depth, offset_start, hidden_share, 0)
    taps_local = lax.dynamic_slice_in_dim(taps_depth, offset_start, hidden_share, 1)
    attend = attend_mask()
    score_scale = HEAD_DIM ** (-0.5)
    keys_count = (SIDE // 2) ** 2
    owner_count = owner_list.shape[0]
    spans_a = (model_width, 2 * model_width, model_width, hidden_width)
    spans_b = (model_width, model_width)
    output_list = []
    input_list = []
    total_vectors = jnp.zeros(vector_params.shape, jnp.float32)
    owned_sum = jnp.zeros(matrix_first.shape, jnp.float32)
    for batch_number in range(tokens.shape[0]):
        tokens_part = tokens[batch_number]
        tiles_part = valid_tiles[batch_number]
        grid_count = tiles_part.shape[0]
        token_rows = tokens_part.shape[0]
        valid_rows = slot_valid(tiles_part).reshape(token_rows, 1)
        source = tokens_part.astype(jnp.float32)
        normed, normal_one, inverse_one = layer_norm(source, gain_one, shift_one)
        normed_low = normed.astype(jnp.bfloat16)
        query_low = (
            jnp.dot(normed_low, w_query, preferred_element_type=jnp.float32) + bias_query
        ).astype(jnp.bfloat16)
        patch_rows = patch_halves(normed_low * valid_rows.astype(jnp.bfloat16), grid_count)
        reduced = jnp.dot(patch_rows[0], reduce_halves[0], preferred_element_type=jnp.float32)
        reduced = (
            reduced
            + jnp.dot(patch_rows[1], reduce_halves[1], preferred_element_type=jnp.float32)
            + bias_reduce
        )
        kv_normed, normal_kv, inverse_kv = layer_norm(reduced, gain_kv, shift_kv)
        kv_low = kv_normed.astype(jnp.bfloat16)
        keyval = jnp.dot(kv_low, w_keyval, preferred_element_type=jnp.float32)
        keys_low = keyval[:, :model_width].astype(jnp.bfloat16)
        values_low = (keyval[:, model_width:] + bias_value).astype(jnp.bfloat16)

        def head_parts(head_number):
            low_col = head_number * HEAD_DIM
            query_head = query_low[:, low_col : low_col + HEAD_DIM].reshape(
                grid_count, SIDE * SIDE, HEAD_DIM
            )
            key_head = keys_low[:, low_col : low_col + HEAD_DIM].reshape(
                grid_count, keys_count, HEAD_DIM
            )
            value_head = values_low[:, low_col : low_col + HEAD_DIM].reshape(
                grid_count, keys_count, HEAD_DIM
            )
            return (query_head, key_head, value_head)

        log_totals = []
        context_parts = []
        for head_number in range(HEADS):
            query_head, key_head, value_head = head_parts(head_number)
            scores = head_scores(query_head, key_head, attend, score_scale)
            row_peak = jnp.max(scores, axis=-1, keepdims=True)
            log_total = row_peak + jnp.log(
                jnp.sum(jnp.exp(scores - row_peak), axis=-1, keepdims=True)
            )
            probs_low = jnp.exp(scores - log_total).astype(jnp.bfloat16)
            context_head = jnp.einsum(
                "gqk,gkd->gqd", probs_low, value_head, preferred_element_type=jnp.float32
            )
            context_parts.append(context_head.reshape(token_rows, HEAD_DIM))
            log_totals.append(log_total)
        context_low = jnp.concatenate(context_parts, axis=1).astype(jnp.bfloat16)
        attn_out = jnp.dot(context_low, w_output, preferred_element_type=jnp.float32) + bias_output
        middle = source + valid_rows * attn_out
        normed_two, normal_two, inverse_two = layer_norm(middle, gain_two, shift_two)
        normed_two_low = normed_two.astype(jnp.bfloat16)
        rows_all = lax.all_gather(normed_two_low, "ch", axis=0, tiled=True)
        valid_low_all = lax.all_gather(valid_rows.astype(jnp.bfloat16), "ch", axis=0, tiled=True)
        valid_all = valid_low_all.astype(jnp.float32)
        grids_all = rows_all.shape[0] // (SIDE * SIDE)
        upward = jnp.dot(rows_all, up_local, preferred_element_type=jnp.float32) + bias_up_local
        conv_input = (upward * valid_all).reshape(grids_all, SIDE, SIDE, hidden_share)
        mixed_conv = depthwise(conv_input, taps_local) + bias_depth_local
        hidden_low = (
            gelu_exact(mixed_conv)
            .astype(jnp.bfloat16)
            .reshape(grids_all * SIDE * SIDE, hidden_share)
        )
        branch = lax.psum_scatter(
            jnp.dot(hidden_low, down_local, preferred_element_type=jnp.float32).astype(
                jnp.bfloat16
            ),
            "ch",
            scatter_dimension=0,
            tiled=True,
        ).astype(jnp.float32)
        branch = branch + bias_down
        output_rows = (middle + valid_rows * branch).astype(jnp.bfloat16)
        upstream = grad_output[batch_number].astype(jnp.float32)
        branch_grad = (upstream * valid_rows).astype(jnp.bfloat16)
        branch_grad_all = lax.all_gather(branch_grad, "ch", axis=0, tiled=True)
        grad_down = inner_rows(hidden_low, branch_grad_all)
        grad_bias_down = jnp.sum(branch_grad.astype(jnp.float32), axis=0)
        grad_hidden = times_transposed(branch_grad_all, down_local)
        grad_mixed = (grad_hidden * gelu_slope(mixed_conv.reshape(-1, hidden_share))).reshape(
            grids_all, SIDE, SIDE, hidden_share
        )
        grad_taps, grad_conv = depthwise_backward(grad_mixed, conv_input, taps_local)
        grad_bias_depth = jnp.sum(grad_mixed, axis=(0, 1, 2))
        grad_up_low = (grad_conv.reshape(-1, hidden_share) * valid_all).astype(jnp.bfloat16)
        grad_bias_up = jnp.sum(grad_up_low.astype(jnp.float32), axis=0)
        grad_up = inner_rows(rows_all, grad_up_low)
        grad_normed_two = lax.psum_scatter(
            times_transposed(grad_up_low, up_local).astype(jnp.bfloat16),
            "ch",
            scatter_dimension=0,
            tiled=True,
        ).astype(jnp.float32)
        grad_middle_norm, grad_gain_two, grad_shift_two = norm_backward(
            grad_normed_two, normal_two, inverse_two, gain_two
        )
        grad_middle = upstream + grad_middle_norm
        grad_attn = (grad_middle * valid_rows).astype(jnp.bfloat16)
        grad_bias_output = jnp.sum(grad_attn.astype(jnp.float32), axis=0)
        grad_output_w = inner_rows(context_low, grad_attn)
        grad_context_all = times_transposed(grad_attn, w_output).astype(jnp.bfloat16)
        query_grad_parts = []
        key_grad_parts = []
        value_grad_parts = []
        for head_number in range(HEADS):
            query_head, key_head, value_head = head_parts(head_number)
            low_col = head_number * HEAD_DIM
            grad_context = grad_context_all[:, low_col : low_col + HEAD_DIM].reshape(
                grid_count, SIDE * SIDE, HEAD_DIM
            )
            probs_again = jnp.exp(
                head_scores(query_head, key_head, attend, score_scale) - log_totals[head_number]
            )
            probs_again_low = probs_again.astype(jnp.bfloat16)
            grad_values = jnp.einsum(
                "gqk,gqd->gkd", probs_again_low, grad_context, preferred_element_type=jnp.float32
            )
            grad_probs = jnp.einsum(
                "gqd,gkd->gqk", grad_context, value_head, preferred_element_type=jnp.float32
            )
            grad_scores = (
                probs_again
                * (grad_probs - jnp.sum(grad_probs * probs_again, axis=-1, keepdims=True))
            ).astype(jnp.bfloat16)
            grad_query = (
                jnp.einsum(
                    "gqk,gkd->gqd", grad_scores, key_head, preferred_element_type=jnp.float32
                )
                * score_scale
            )
            grad_keys = (
                jnp.einsum(
                    "gqk,gqd->gkd", grad_scores, query_head, preferred_element_type=jnp.float32
                )
                * score_scale
            )
            query_grad_parts.append(grad_query.reshape(token_rows, HEAD_DIM).astype(jnp.bfloat16))
            key_grad_parts.append(
                grad_keys.reshape(grid_count * keys_count, HEAD_DIM).astype(jnp.bfloat16)
            )
            value_grad_parts.append(
                grad_values.reshape(grid_count * keys_count, HEAD_DIM).astype(jnp.bfloat16)
            )
        grad_query_low = jnp.concatenate(query_grad_parts, axis=1)
        grad_values_low = jnp.concatenate(value_grad_parts, axis=1)
        grad_bias_value = jnp.sum(grad_values_low.astype(jnp.float32), axis=0)
        grad_keyval_low = jnp.concatenate(key_grad_parts + value_grad_parts, axis=1)
        grad_keyval_w = inner_rows(kv_low, grad_keyval_low)
        grad_kv_normed = times_transposed(grad_keyval_low, w_keyval)
        grad_reduced_norm, grad_gain_kv, grad_shift_kv = norm_backward(
            grad_kv_normed, normal_kv, inverse_kv, gain_kv
        )
        grad_reduced_low = grad_reduced_norm.astype(jnp.bfloat16)
        grad_bias_reduce = jnp.sum(grad_reduced_low.astype(jnp.float32), axis=0)
        grad_reduce_w = jnp.concatenate(
            [
                inner_rows(patch_rows[0], grad_reduced_low),
                inner_rows(patch_rows[1], grad_reduced_low),
            ],
            axis=0,
        )
        back_halves = [
            times_transposed(grad_reduced_low, reduce_halves[0]),
            times_transposed(grad_reduced_low, reduce_halves[1]),
        ]
        grad_slots = halves_to_slots(back_halves, grid_count, model_width) * valid_rows
        grad_bias_query = jnp.sum(grad_query_low.astype(jnp.float32), axis=0)
        grad_query_w = inner_rows(normed_low, grad_query_low)
        grad_normed = times_transposed(grad_query_low, w_query) + grad_slots
        grad_source_norm, grad_gain_one, grad_shift_one = norm_backward(
            grad_normed, normal_one, inverse_one, gain_one
        )
        grad_input = grad_middle + grad_source_norm
        grad_up_full = lax.dynamic_update_slice_in_dim(
            jnp.zeros((model_width, hidden_width), jnp.float32), grad_up, offset_start, 1
        )
        grad_down_full = lax.dynamic_update_slice_in_dim(
            jnp.zeros((hidden_width, model_width), jnp.float32), grad_down, offset_start, 0
        )
        bias_up_full = lax.dynamic_update_slice_in_dim(
            jnp.zeros((hidden_width,), jnp.float32), grad_bias_up, offset_start, 0
        )
        bias_depth_full = lax.dynamic_update_slice_in_dim(
            jnp.zeros((hidden_width,), jnp.float32), grad_bias_depth, offset_start, 0
        )
        taps_full = lax.dynamic_update_slice_in_dim(
            jnp.zeros((9, hidden_width), jnp.float32), grad_taps, offset_start, 1
        )
        group_grad_a = jnp.concatenate(
            [grad_query_w, grad_keyval_w, grad_output_w, grad_up_full], axis=1
        )
        group_grad_b = jnp.concatenate([grad_reduce_w, grad_down_full], axis=1)
        small_rows = jnp.stack(
            [
                grad_gain_one,
                grad_shift_one,
                grad_bias_query,
                grad_bias_value,
                grad_bias_reduce,
                grad_gain_kv,
                grad_shift_kv,
                grad_bias_output,
                grad_gain_two,
                grad_shift_two,
                grad_bias_down,
            ]
        )
        vector_rows = jnp.concatenate(
            [
                small_rows,
                bias_up_full.reshape(ratio_rows, model_width),
                bias_depth_full.reshape(ratio_rows, model_width),
                taps_full.reshape(9 * ratio_rows, model_width),
            ],
            axis=0,
        )
        results = (output_rows, grad_input, group_grad_a, group_grad_b, vector_rows)
        output_list.append(results[0])
        input_list.append(results[1])
        total_vectors = total_vectors + results[4]
        rotated_a = rotate_group(results[2], left_a, right_a, spans_a)
        rotated_b = rotate_group(results[3], left_b, right_b, spans_b)
        flat_values = jnp.concatenate([rotated_a.reshape(-1), rotated_b.reshape(-1)]).reshape(
            owner_count, -1
        )
        owned_sum = owned_sum + lax.psum_scatter(
            jnp.take(flat_values, owner_list, axis=0),
            ("tok", "ch"),
            scatter_dimension=0,
            tiled=True,
        )
    vector_grad = lax.psum(total_vectors, ("tok", "ch"))
    steps_done = step_count[0].astype(jnp.float32)
    first_new = beta_one * matrix_first + (1.0 - beta_one) * owned_sum
    second_new = beta_two * matrix_second + (1.0 - beta_two) * owned_sum * owned_sum
    direction = (
        first_new
        / (1.0 - beta_one**steps_done)
        / (jnp.sqrt(second_new / (1.0 - beta_two**steps_done)) + adam_epsilon)
    )
    every_block = lax.all_gather(direction, ("tok", "ch"), axis=0, tiled=True)
    ordered = jnp.take(every_block, invert_order(owner_list), axis=0).reshape(-1)
    split_point = model_width * (4 * model_width + hidden_width)
    step_a = restore_group(
        ordered[:split_point].reshape(model_width, 4 * model_width + hidden_width),
        left_a,
        right_a,
        spans_a,
    )
    step_b = restore_group(
        ordered[split_point:].reshape(hidden_width, 2 * model_width), left_b, right_b, spans_b
    )
    new_master_a = master_a - matrix_rate * (step_a + weight_decay * master_a)
    new_master_b = master_b - matrix_rate * (step_b + weight_decay * master_b)
    vec_first_new = beta_one * vector_first + (1.0 - beta_one) * vector_grad
    vec_second_new = beta_two * vector_second + (1.0 - beta_two) * vector_grad * vector_grad
    vec_direction = (
        vec_first_new
        / (1.0 - beta_one**steps_done)
        / (jnp.sqrt(vec_second_new / (1.0 - beta_two**steps_done)) + adam_epsilon)
    )
    new_vectors = vector_params - vector_rate * (vec_direction + weight_decay * vector_params)
    return (
        jnp.stack(output_list),
        jnp.stack(input_list),
        owned_sum,
        first_new,
        second_new,
        new_master_a,
        new_master_b,
        new_master_a.astype(jnp.bfloat16),
        new_master_b.astype(jnp.bfloat16),
        vector_grad,
        vec_first_new,
        vec_second_new,
        new_vectors,
    )


def solution(mesh):
    in_specs = (
        P(None, ("tok", "ch"), None),
        P(None, ("tok", "ch"), None),
        P(None, ("tok", "ch"), None),
        P(),
        P(),
        P(),
        P(("tok", "ch"), None),
        P(("tok", "ch"), None),
        P(),
        P(),
        P(),
        P(),
        P(),
        P(),
        P(),
        P(),
    )
    out_specs = (
        P(None, ("tok", "ch"), None),
        P(None, ("tok", "ch"), None),
        P(("tok", "ch"), None),
        P(("tok", "ch"), None),
        P(("tok", "ch"), None),
        P(),
        P(),
        P(),
        P(),
        P(),
        P(),
        P(),
        P(),
    )
    return jax.shard_map(
        on_device, mesh=mesh, in_specs=in_specs, out_specs=out_specs, check_vma=False
    )
```

profile of v0, /device:TPU:0, one launch (start us, length us, event | category | flops | bytes accessed | tf_op | source)
XLA Modules:
  0.0 1246.0 jit_solution(14126852287643391888)
XLA Ops:
  66.1 8.4 slice_reduce_fusion
  150.4 5.4 all_gather.22
  170.4 5.9 add_multiply_fusion.1
  176.3 22.3 %all-gather.9.cloned.1.call-done = bf16[2304,320]{0,1:T(8,128)(2,1)} async-done(((bf16[1152,320]{0,1:T(8,128)(2,1)}), bf16[2304,320]{0,1:T(8,128)(2,1)}) %all-gather.9.cloned.1.call-update) | async-done | bytes 1474576 | tf_op jit(solution)/shard_map/all_gather | solution.py:307
  198.6 5.9 add_multiply_fusion
  204.5 43.7 %multiply_convert_fusion.3 = (bf16[4,24,24,640]{3,2,1,0:T(8,128)(2,1)}, f32[4,24,24,640]{3,2,1,0:T(8,128)}, bf16[4,24,24,640]{3,2,1,0:T(8,128)(2,1)}, f32[4,24,24,640]{3,2,1,0:T(8,128)}) fusion(f32[640]{0:T(1024)S(1)} %copy-done.333, f32[640]{0:T(1024)S(1)} %copy-done.272, f32[640]{0:T(1024)S(1)} %get-tuple-element.138, f32[640]{0:T(1024)S(1)} %get-tuple-element.139, ...), kind=kLoop, calls=%fused_computation.153 | loop fusion | flops 67829760 | bytes 29516800 | tf_op jit(solution)/shard_map/convert_element_type | solution.py:316
  248.3 9.3 multiply_reduce_fusion.13
  257.6 21.9 %convert_reduce_fusion.1 = (f32[640]{0:T(1024)S(1)}, f32[4,24,24,640]{3,2,1,0:T(8,128)}) fusion(f32[4,24,24]{2,1,0:T(8,128)S(1)} %mul.1618, f32[640]{0:T(1024)S(1)} %copy-done.272, f32[640]{0:T(1024)S(1)} %get-tuple-element.138, f32[640]{0:T(1024)S(1)} %get-tuple-element.139, f32[640]{0:T(1024)S(1)} %copy-done.262, f32[4,24,24,640]{3,2,1,0:T(8,128)} %bitcast.471, ...), kind=kLoop, calls=%fused_computation.148 | loop fusion | flops 30965120 | bytes 11831296 | tf_op jit(solution)/shard_map/reduce_sum | solution.py:341
  325.6 23.8 %reduce-scatter.13.cloned.1.call-done = bf16[1152,320]{1,0:T(8,128)(2,1)} async-done(((bf16[2304,320]{1,0:T(8,128)(2,1)}), bf16[1152,320]{1,0:T(8,128)(2,1)}) %reduce-scatter.13.cloned.1.call-update) | async-done | bytes 737296
  356.5 25.4 %multiply_reduce_fusion.9 = (f32[640]{0:T(1024)S(1)}, f32[640]{0:T(1024)S(1)}, f32[640]{0:T(1024)S(1)}, f32[640]{0:T(1024)S(1)}, f32[640]{0:T(1024)S(1)}, /*inde...) fusion(f32[4,24,24,640]{3,2,1,0:T(8,128)} %bitcast.472, f32[4,24,24,640]{3,2,1,0:T(8,128)} %bitcast.470), kind=kLoop, calls=%fused_computation.139 | loop fusion | flops 23587840 | bytes 11816960 | tf_op jit(solution)/shard_map/reduce_sum | solution.py:167
  461.6 9.8 multiply_reduce_fusion.4
  471.5 22.3 %convert_reduce_fusion = (f32[640]{0:T(1024)S(1)}, f32[4,24,24,640]{3,2,1,0:T(8,128)}) fusion(f32[4,24,24]{2,1,0:T(8,128)S(1)} %copy-done.170, f32[640]{0:T(1024)S(1)} %copy-done.273, f32[640]{0:T(1024)S(1)} %copy-done.259, f32[640]{0:T(1024)S(1)} %copy-done.261, f32[640]{0:T(1024)S(1)} %copy-done.263, f32[4,24,24,640]{3,2,1,0:T(8,128)} %bitcast.473, ...), kind=kLoop, calls=%fused_computation.137 | loop fusion | flops 30965120 | bytes 11831296 | tf_op jit(solution)/shard_map/reduce_sum | solution.py:341
  511.9 10.1 gather_fusion
  525.3 24.2 %multiply_reduce_fusion = (f32[640]{0:T(1024)S(1)}, f32[640]{0:T(1024)S(1)}, f32[640]{0:T(1024)S(1)}, f32[640]{0:T(1024)S(1)}, f32[640]{0:T(1024)S(1)}, /*index=...) fusion(f32[4,24,24,640]{3,2,1,0:T(8,128)} %bitcast.474, f32[4,24,24,640]{3,2,1,0:T(8,128)} %bitcast.468), kind=kLoop, calls=%fused_computation.128 | loop fusion | flops 23587840 | bytes 11816960 | tf_op jit(solution)/shard_map/reduce_sum | solution.py:167
  677.7 10.0 gather_fusion.9
  787.5 5.2 bitcast_multiply_fusion.7
  807.4 6.2 gather_fusion.15
  822.5 6.2 gather_fusion.7
  847.7 6.1 pad_maximum_fusion
  853.8 10.9 gather_fusion.8
  869.9 10.9 gather_fusion.17
  882.4 8.3 select_add_fusion
  891.7 159.6 %all-reduce.8.cloned.1.call-done = (f32[32,51200]{1,0:T(8,128)}, f32[55,320]{1,0:T(8,128)}) async-done(((f32[32,51200]{1,0:T(8,128)}, f32[55,320]{1,0:T(8,128)}), (f32[32,51200]{1,0:T(8,128)}, f32[55,320]{1,0:T(8,128)})) %all-reduce.8.cloned.1.call-update) | async-done | bytes 6624016
  1068.3 10.1 scatter_custom_fusion.5
  1078.5 5.2 scatter_custom_fusion.7
  1083.8 5.2 scatter_custom_fusion.6
  1112.5 12.7 %all-gather.15.cloned.1.call-done = f32[32,1,51200]{2,1,0:T(1,128)} async-done(((f32[1,1,51200]{2,1,0:T(1,128)}), f32[32,1,51200]{2,1,0:T(1,128)}) %all-gather.15.cloned.1.call-update) | async-done | bytes 6553616 | tf_op jit(solution)/shard_map/all_gather | solution.py:496
  1125.2 7.7 copy.809
  1132.9 10.6 gather_fusion.18
  1164.1 6.1 gather_fusion.25
  1214.5 10.0 gather_fusion.23
  1224.5 5.3 fusion.340
  (1447 shorter events, 690.2 us)
Async XLA Ops:
  7.2 163.2 %all-gather.7.cloned.1.call-start = ((), (), s32[]{:S(2)}) async-start(), calls=%async_computation.4 | async-start | bytes 2211840 | tf_op jit(solution)/shard_map/all_gather | solution.py:307
  116.3 452.2 %copy-start.4 = (f32[1152,320]{0,1:T(8,128)}, f32[1152,320]{0,1:T(8,128)S(1)}, u32[]{:S(2)}) copy-start(f32[1152,320]{0,1:T(8,128)S(1)} %get-tuple-element.360) | copy-start | bytes 4423684
  139.3 212.3 %copy-start.6 = (f32[1152,320]{0,1:T(8,128)}, f32[1152,320]{0,1:T(8,128)S(1)}, u32[]{:S(2)}) copy-start(f32[1152,320]{0,1:T(8,128)S(1)} %get-tuple-element.346) | copy-start | bytes 4423684
  139.3 212.3 %copy-start.136 = (f32[1152]{0:T(1024)}, f32[1152]{0:T(1024)S(1)}, u32[]{:S(2)}) copy-start(f32[1152]{0:T(1024)S(1)} %broadcast_multiply_fusion.10) | copy-start | bytes 13828
  141.2 57.4 %all-gather.9.cloned.1.call-start = ((), (), s32[]{:S(2)}) async-start(), calls=%async_computation.5 | async-start | bytes 2211840 | tf_op jit(solution)/shard_map/all_gather | solution.py:307
  141.9 106.3 %all-gather.11.cloned.1.call-start = ((), (), s32[]{:S(2)}) async-start(), calls=%async_computation.6 | async-start | bytes 2211840 | tf_op jit(solution)/shard_map/all_gather | solution.py:331
  144.8 176.3 %reduce-scatter.17.cloned.1.call-start = ((), (), s32[]{:S(2)}) async-start(), calls=%async_computation.11 | async-start | bytes 2654208
  166.2 91.3 %copy-start.256 = (f32[640]{0:T(1024)}, f32[640]{0:T(1024)S(1)}, u32[]{:S(2)}) copy-start(f32[640]{0:T(1024)S(1)} %get-tuple-element.137) | copy-start | bytes 7684
  166.2 91.3 %copy-start.258 = (f32[640]{0:T(1024)}, f32[640]{0:T(1024)S(1)}, u32[]{:S(2)}) copy-start(f32[640]{0:T(1024)S(1)} %get-tuple-element.138) | copy-start | bytes 7684
  166.3 91.3 %copy-start.260 = (f32[640]{0:T(1024)}, f32[640]{0:T(1024)S(1)}, u32[]{:S(2)}) copy-start(f32[640]{0:T(1024)S(1)} %get-tuple-element.139) | copy-start | bytes 7684
  166.3 32.3 %copy-start.224 = (f32[2304]{0:T(1024)S(1)}, f32[2304]{0:T(1024)}, u32[]{:S(2)}) copy-start(f32[2304]{0:T(1024)} %convert_reduce_fusion.16) | copy-start | bytes 27652
  166.3 32.3 %copy-start.370 = (f32[640]{0:T(1024)S(1)}, f32[640]{0:T(1024)}, u32[]{:S(2)}) copy-start(f32[640]{0:T(1024)} %dynamic_slice.16) | copy-start | bytes 7684
  290.5 58.9 %reduce-scatter.13.cloned.1.call-start = ((), (), s32[]{:S(2)}) async-start(), calls=%async_computation.9 | async-start | bytes 2654208
  307.3 154.2 %all-gather.13.cloned.1.call-start = ((), (), s32[]{:S(2)}) async-start(), calls=%async_computation.7 | async-start | bytes 2211840 | tf_op jit(solution)/shard_map/all_gather | solution.py:331
  323.2 28.4 %copy-start.241 = (f32[1152]{0:T(1024)S(1)}, f32[1152]{0:T(1024)}, u32[]{:S(2)}) copy-start(f32[1152]{0:T(1024)} %copy-done.240) | copy-start | bytes 13828
  325.6 30.8 %copy-start.232 = (f32[1152]{0:T(1024)}, f32[1152]{0:T(1024)S(1)}, u32[]{:S(2)}) copy-start(f32[1152]{0:T(1024)S(1)} %broadcast_multiply_fusion.6) | copy-start | bytes 13828
  325.6 30.8 %copy-start.234 = (f32[1152]{0:T(1024)}, f32[1152]{0:T(1024)S(1)}, u32[]{:S(2)}) copy-start(f32[1152]{0:T(1024)S(1)} %broadcast_multiply_fusion.7) | copy-start | bytes 13828
  356.5 165.5 %reduce-scatter.15.cloned.1.call-start = ((), (), s32[]{:S(2)}) async-start(), calls=%async_computation.10 | async-start | bytes 2654208
  384.5 179.2 %reduce-scatter.19.cloned.1.call-start = ((), (), s32[]{:S(2)}) async-start(), calls=%async_computation.12 | async-start | bytes 2654208
  504.8 546.4 %all-reduce.8.cloned.1.call-start = ((), (), s32[]{:S(2)}) async-start(), calls=%async_computation.13 | async-start | bytes 13279232
  890.7 160.6 %copy-start.168 = (f32[1,51200]{1,0:T(1,128)S(1)}, f32[1,51200]{1,0:T(1,128)}, u32[]{:S(2)}) copy-start(f32[1,51200]{1,0:T(1,128)} %param.37) | copy-start | bytes 614404
  890.7 160.6 %copy-start.169 = (f32[1,51200]{1,0:T(1,128)S(1)}, f32[1,51200]{1,0:T(1,128)}, u32[]{:S(2)}) copy-start(f32[1,51200]{1,0:T(1,128)} %param.36) | copy-start | bytes 614404
  890.7 234.5 %all-gather.15.cloned.1.call-start = ((), (), s32[]{:S(2)}) async-start(), calls=%async_computation.8 | async-start | bytes 6758400 | tf_op jit(solution)/shard_map/all_gather | solution.py:496
  1059.6 29.5 %copy-start.308 = (s32[4,320]{1,0:T(4,128)S(1)}, s32[4,320]{1,0:T(4,128)}, u32[]{:S(2)}) copy-start(s32[4,320]{1,0:T(4,128)} %param.40) | copy-start | bytes 15364
  1059.6 43.1 %copy-start.354 = (f32[1152]{0:T(1024)S(1)}, f32[1152]{0:T(1024)}, u32[]{:S(2)}) copy-start(f32[1152]{0:T(1024)} %get-tuple-element.95) | copy-start | bytes 13828
  1062.9 42.3 %copy-start.5 = (f32[1152,320]{0,1:T(8,128)S(1)}, f32[1152,320]{0,1:T(8,128)}, u32[]{:S(2)}) copy-start(f32[1152,320]{0,1:T(8,128)} %copy-done.4) | copy-start | bytes 4423684
  1062.9 42.3 %copy-start.13 = (bf16[2,1152,320]{1,2,0:T(8,128)(2,1)S(1)}, bf16[2,1152,320]{1,2,0:T(8,128)(2,1)}, u32[]{:S(2)}) copy-start(bf16[2,1152,320]{1,2,0:T(8,128)(2,1)} %param.30) | copy-start | bytes 4423684
  1063.0 42.3 %copy-start.135 = (f32[1152]{0:T(1024)S(1)}, f32[1152]{0:T(1024)}, u32[]{:S(2)}) copy-start(f32[1152]{0:T(1024)} %copy-done.133) | copy-start | bytes 13828
  1063.0 42.3 %copy-start.164 = (f32[1152]{0:T(1024)S(1)}, f32[1152]{0:T(1024)}, u32[]{:S(2)}) copy-start(f32[1152]{0:T(1024)} %copy-done.162) | copy-start | bytes 13828
  1063.0 42.3 %copy-start.191 = (f32[320]{0:T(512)S(1)}, f32[320]{0:T(512)}, u32[]{:S(2)}) copy-start(f32[320]{0:T(512)} %get-tuple-element.128) | copy-start | bytes 3844
  1063.0 42.3 %copy-start.237 = (f32[1152]{0:T(1024)S(1)}, f32[1152]{0:T(1024)}, u32[]{:S(2)}) copy-start(f32[1152]{0:T(1024)} %copy-done.236) | copy-start | bytes 13828
  1063.0 42.3 %copy-start.239 = (f32[1152]{0:T(1024)S(1)}, f32[1152]{0:T(1024)}, u32[]{:S(2)}) copy-start(f32[1152]{0:T(1024)} %copy-done.238) | copy-start | bytes 13828
  (375 other events, 2065.9 us)
Sparse Core Ops, SparseCore 0:
  141.3 29.0 all-gather.6
  172.5 26.0 all-gather.8
  200.7 26.0 all-gather.10
  290.6 28.3 reduce-scatter.16
  321.1 28.3 reduce-scatter.12
  356.6 26.0 all-gather.12
  384.9 28.3 reduce-scatter.14
  505.0 28.3 reduce-scatter.18
  890.8 160.3 all-reduce.7
  1054.9 70.2 all-gather.14
where the time goes:
time: 1250 us
  local copies, waits for them, and re-layouts  501 us (40%)
  other arithmetic  308 us (25%)
  waiting for transfers between devices  223 us (18%)
  matrix products  181 us (14%)
  between operations  20.7 us (2%)
    unnamed x15, waiting for transfers between devices  184 us
    unnamed x844, local copies, waits for them, and re-layouts  101 us
    reduce_sum x2, other arithmetic, depthwise_backward(): tap_grads.append(jnp.sum(window * grad_mixed, axis=(0, 1, 2)))  49.6 us
    dot_general x14, matrix products, times_transposed(): lax.dot_general(left_side, right_side, (((1,), (1,)), ((), ())), preferre...  46.2 us
    reduce_sum x2, other arithmetic, on_device(): grad_bias_up = jnp.sum(grad_up_low.astype(jnp.float32), axis=0)  44.2 us
    convert_element_type x1, other arithmetic, on_device(): hidden_low = gelu_exact(mixed_conv).astype(jnp.bfloat16).reshape(grids_al...  43.7 us
    gather x12, local copies, waits for them, and re-layouts, rotate_group(): jnp.take(columns_moved[:, offset_start:offset_start + span_size], left_co...  38.8 us
    scatter x9, local copies, waits for them, and re-layouts, invert_order(): return jnp.zeros(order_codes.shape, jnp.int32).at[order_codes].set(jnp.ar...  37.9 us
  transfers between devices with their start and end apart: 10, of which 5 were waited for; matrix products, arithmetic and copies ran while one was open for 29% of the time, Pallas kernels for 0%

commit v1 on v0

v1 whole, which is shorter than its diff:
```python
import functools

import jax
import jax.numpy as jnp
from jax import lax
from jax.experimental import pallas as pl
from jax.experimental.pallas import tpu as pltpu
from jax.sharding import PartitionSpec as P

HEADS = 5
HEAD_DIM = 64
SIDE = 24
TILE = 8
TILES = 9
SLOTS = 576
KEYS = 144
LANES = 128
KEYS_TILE = 16

beta_one = 0.9
beta_two = 0.999
adam_epsilon = 1e-08
norm_epsilon = 1e-05
matrix_rate = 0.05
vector_rate = 0.2
weight_decay = 0.01

F32 = jnp.float32
BF16 = jnp.bfloat16


def contract(left, right, left_dim, right_dim):
    return lax.dot_general(
        left, right, (((left_dim,), (right_dim,)), ((), ())), preferred_element_type=F32
    )


def normalize(values):
    scale = 1.0 / values.shape[-1]
    center = values - jnp.sum(values, axis=-1, keepdims=True) * scale
    inverse = lax.rsqrt(jnp.sum(center * center, axis=-1, keepdims=True) * scale + norm_epsilon)
    return center * inverse, inverse


def norm_back(upstream, normal, inverse, gain):
    scale = 1.0 / upstream.shape[-1]
    scaled = upstream * gain
    inner = jnp.sum(scaled * normal, axis=-1, keepdims=True) * scale
    mean = jnp.sum(scaled, axis=-1, keepdims=True) * scale
    return inverse * (scaled - mean - normal * inner)


def row_sums(values):
    rows, cols = values.shape
    return jnp.sum(values.reshape(rows // 8, 8, cols), axis=0)


def group_all(values, op):
    lane = lax.broadcasted_iota(jnp.int32, values.shape, 1)
    for step in (1, 2, 4, 8):
        low = pltpu.roll(values, step, 1)
        high = pltpu.roll(values, LANES - step, 1)
        values = op(values, jnp.where((lane & step) != 0, low, high))
    return values


def split_tiles(rows):
    shaped = rows.reshape(TILE, 3, TILE, rows.shape[1])
    return [shaped[:, c].reshape(TILE * TILE, rows.shape[1]) for c in range(3)]


def join_tiles(tiles):
    return jnp.concatenate(
        [tiles[c][i * TILE : (i + 1) * TILE] for i in range(TILE) for c in range(3)], axis=0
    )


def gelu_parts(e):
    gauss = jnp.exp(-0.5 * e * e)
    size = jnp.abs(e)
    t = 1.0 / (1.0 + (0.3275911 * 0.7071067811865476) * size)
    poly = t * (
        0.5 * 0.254829592
        + t
        * (
            0.5 * -0.284496736
            + t * (0.5 * 1.421413741 + t * (0.5 * -1.453152027 + t * (0.5 * 1.061405429)))
        )
    )
    tail = poly * gauss
    phi = jnp.where(e >= 0.0, 1.0 - tail, tail)
    return phi, gauss * 0.3989422804014327


def block_kernel(
    flags,
    x_ref,
    dy_ref,
    wq,
    wk,
    wv,
    wo,
    wup,
    wr,
    wdn,
    vec,
    wide,
    pick,
    hmask,
    out_ref,
    gin_ref,
    gq,
    gk,
    gv,
    go,
    gup,
    gr,
    gdn,
    gsm,
    gwd,
    msk,
    xs,
    n1s,
    r1s,
    h1s,
    hms,
    qs,
    pats,
    kin,
    nks,
    rks,
    ks,
    vs,
    ps,
    ctxs,
    tmp,
    m1s,
    n2s,
    r2s,
    h2s,
    us,
    dhs,
    hids,
    dus,
    dms,
    das,
    dcs,
    dqs,
    dks,
    dvs,
    dps,
):
    g = pl.program_id(0)
    width = x_ref.shape[2]
    hidden = wup.shape[1]

    @pl.when(g == 0)
    def _():
        for ref in (gq, gk, gv, go, gup, gr, gdn, gsm, gwd):
            ref[...] = jnp.zeros(ref.shape, F32)

    row = lax.broadcasted_iota(jnp.int32, (TILE * TILE, width), 0)
    inside = jnp.where((row % TILE < TILE - 1) & (row < TILE * (TILE - 1)), 1.0, 0.0)
    for t in range(TILES):
        msk[t * 64 : (t + 1) * 64, :] = inside * flags[g, t].astype(F32)

    def vrow(number):
        return vec[number : number + 1, :]

    def add_small(number, sums):
        gsm[number : number + 1, :] += jnp.sum(sums, axis=0, keepdims=True)

    zero_rows = jnp.zeros((8, width), F32)

    def first_norm(big, carry):
        base = pl.multiple_of(big * 192, 64)
        tiles = split_tiles(x_ref[0, pl.ds(base, 192), :].astype(F32))
        grads = split_tiles(dy_ref[0, pl.ds(base, 192), :].astype(F32))
        for c in range(3):
            rows = pl.ds(base + c * 64, 64)
            normal, inverse = normalize(tiles[c])
            xs[rows, :] = tiles[c]
            n1s[rows, :] = normal
            r1s[rows, :] = inverse
            low = (normal * vrow(0) + vrow(1)).astype(BF16)
            h1s[rows, :] = low
            mask = msk[rows, :]
            hms[rows, :] = (low.astype(F32) * mask).astype(BF16)
            dms[rows, :] = (grads[c] * mask).astype(BF16)
        return carry

    lax.fori_loop(0, 3, first_norm, 0)
    qs[...] = (jnp.dot(h1s[...], wq[...], preferred_element_type=F32) + vrow(2)).astype(BF16)
    pats[...] = jnp.dot(pick[...], hms[...], preferred_element_type=F32).astype(BF16)
    reduced = vrow(4)
    for d in range(4):
        reduced = reduced + jnp.dot(
            pats[d * KEYS : (d + 1) * KEYS, :],
            wr[d * width : (d + 1) * width, :],
            preferred_element_type=F32,
        )
    normal, inverse = normalize(reduced)
    nks[...] = normal
    rks[...] = inverse
    kin[...] = (normal * vrow(5) + vrow(6)).astype(BF16)
    ks[...] = jnp.dot(kin[...], wk[...], preferred_element_type=F32).astype(BF16)
    vs[...] = (jnp.dot(kin[...], wv[...], preferred_element_type=F32) + vrow(3)).astype(BF16)
    score_scale = HEAD_DIM ** (-0.5)

    def spread(ref, t):
        part = ref[pl.ds(pl.multiple_of(t * KEYS_TILE, KEYS_TILE), KEYS_TILE), :]
        return jnp.concatenate([part] * 8, axis=0) * hmask[...]

    def gather_heads(big):
        big = big * hmask[...].astype(F32)
        total = big[0:KEYS_TILE]
        for h in range(1, HEADS):
            total = total + big[h * KEYS_TILE : (h + 1) * KEYS_TILE]
        return total

    def attend_tile(t, carry):
        rows = pl.ds(pl.multiple_of(t * 64, 64), 64)
        scores = contract(qs[rows, :], spread(ks, t), 1, 1) * score_scale
        exped = jnp.exp(scores - group_all(scores, jnp.maximum))
        probs = exped / group_all(exped, jnp.add)
        ps[rows, :] = probs
        ctxs[rows, :] = jnp.dot(
            probs.astype(BF16), spread(vs, t), preferred_element_type=F32
        ).astype(BF16)
        return carry

    lax.fori_loop(0, TILES, attend_tile, 0)
    tmp[...] = jnp.dot(ctxs[...], wo[...], preferred_element_type=F32)

    def second_norm(t, carry):
        rows = pl.ds(pl.multiple_of(t * 64, 64), 64)
        middle = xs[rows, :] + msk[rows, :] * (tmp[rows, :] + vrow(7))
        m1s[rows, :] = middle
        normal, inverse = normalize(middle)
        n2s[rows, :] = normal
        r2s[rows, :] = inverse
        h2s[rows, :] = (normal * vrow(8) + vrow(9)).astype(BF16)
        return carry

    lax.fori_loop(0, TILES, second_norm, 0)
    for c in range(hidden // 256):
        cols = slice(c * 256, (c + 1) * 256)
        us[:, cols] = jnp.dot(h2s[...], wup[:, cols], preferred_element_type=F32)
        dhs[:, cols] = contract(dms[...], wdn[cols, :], 1, 1)

    def mix_lanes(lane, carry):
        cols = pl.ds(pl.multiple_of(lane * LANES, LANES), LANES)
        bias_up = wide[0:1, cols]
        bias_dw = wide[1:2, cols]
        taps = [wide[2 + k : 3 + k, cols] for k in range(9)]

        def mix_tile(t, sums):
            sums = list(sums)
            rows = pl.ds(pl.multiple_of(t * 64, 64), 64)
            mask = msk[rows, 0:LANES]
            ups = (us[rows, cols] + bias_up) * mask
            mid = [ups[i * 8 : (i + 1) * 8] for i in range(7)]
            shifted = [
                [pltpu.roll(v, 1, 0) for v in mid],
                mid,
                [pltpu.roll(v, 7, 0) for v in mid],
            ]
            grads = dhs[rows, cols]
            hid_rows = []
            de_rows = []
            for i in range(7):
                e = bias_dw
                for a in range(3):
                    if 0 <= i + a - 1 < 7:
                        for b in range(3):
                            e = e + taps[3 * a + b] * shifted[b][i + a - 1]
                phi, gauss = gelu_parts(e)
                hid_rows.append(e * phi)
                de = grads[i * 8 : (i + 1) * 8] * (phi + e * gauss)
                de_rows.append(de)
                sums[1] = sums[1] + de
                for a in range(3):
                    if 0 <= i + a - 1 < 7:
                        for b in range(3):
                            k = 2 + 3 * a + b
                            sums[k] = sums[k] + de * shifted[b][i + a - 1]
            zero = jnp.zeros((8, LANES), F32)
            hids[rows, cols] = jnp.concatenate(hid_rows + [zero], axis=0).astype(BF16)
            back = [
                [pltpu.roll(v, 7, 0) for v in de_rows],
                de_rows,
                [pltpu.roll(v, 1, 0) for v in de_rows],
            ]
            du_rows = []
            for i in range(7):
                du = None
                for a in range(3):
                    if 0 <= i - a + 1 < 7:
                        for b in range(3):
                            term = taps[3 * a + b] * back[b][i - a + 1]
                            du = term if du is None else du + term
                du_rows.append(du * mask[i * 8 : (i + 1) * 8])
            du_low = jnp.concatenate(du_rows + [zero], axis=0).astype(BF16)
            dus[rows, cols] = du_low
            sums[0] = sums[0] + row_sums(du_low.astype(F32))
            return tuple(sums)

        zero = jnp.zeros((8, LANES), F32)
        sums = lax.fori_loop(0, TILES, mix_tile, (zero,) * 11)
        for k in range(11):
            gwd[k : k + 1, cols] += jnp.sum(sums[k], axis=0, keepdims=True)
        return carry

    lax.fori_loop(0, hidden // LANES, mix_lanes, 0)
    tmp[...] = jnp.dot(hids[...], wdn[...], preferred_element_type=F32)
    gdn[...] += contract(dms[...], hids[...], 0, 0)
    gup[...] += contract(h2s[...], dus[...], 0, 0)
    xs[...] = contract(dus[...], wup[...], 1, 1)

    def middle_rows(big, sums):
        sums = list(sums)
        base = pl.multiple_of(big * 192, 64)
        grads = split_tiles(dy_ref[0, pl.ds(base, 192), :].astype(F32))
        outs = []
        for c in range(3):
            rows = pl.ds(base + c * 64, 64)
            mask = msk[rows, :]
            outs.append(m1s[rows, :] + mask * (tmp[rows, :] + vrow(10)))
            dout = xs[rows, :]
            normal = n2s[rows, :]
            dmid = grads[c] + norm_back(dout, normal, r2s[rows, :], vrow(8))
            m1s[rows, :] = dmid
            low = (dmid * mask).astype(BF16)
            das[rows, :] = low
            sums[0] = sums[0] + row_sums(dout * normal)
            sums[1] = sums[1] + row_sums(dout)
            sums[2] = sums[2] + row_sums(low.astype(F32))
            sums[3] = sums[3] + row_sums(dms[rows, :].astype(F32))
        out_ref[0, pl.ds(base, 192), :] = join_tiles(outs).astype(BF16)
        return tuple(sums)

    sums = lax.fori_loop(0, 3, middle_rows, (zero_rows,) * 4)
    add_small(8, sums[0])
    add_small(9, sums[1])
    add_small(7, sums[2])
    add_small(10, sums[3])
    go[...] += contract(ctxs[...], das[...], 0, 0)
    dcs[...] = contract(das[...], wo[...], 1, 1).astype(BF16)

    def attend_back(t, sums):
        rows = pl.ds(pl.multiple_of(t * 64, 64), 64)
        keys = pl.ds(pl.multiple_of(t * KEYS_TILE, KEYS_TILE), KEYS_TILE)
        probs = ps[rows, :]
        upper = dcs[rows, :]
        dprobs = contract(upper, spread(vs, t), 1, 1)
        inner = group_all(dprobs * probs, jnp.add)
        dz = (probs * (dprobs - inner)).astype(BF16)
        dq = (
            jnp.dot(dz, spread(ks, t), preferred_element_type=F32) * score_scale
        ).astype(BF16)
        dqs[rows, :] = dq
        dk = gather_heads(contract(dz, qs[rows, :], 0, 0)) * score_scale
        dks[keys, :] = dk.astype(BF16)
        dv = gather_heads(contract(probs.astype(BF16), upper, 0, 0)).astype(BF16)
        dvs[keys, :] = dv
        return (sums[0] + row_sums(dq.astype(F32)), sums[1] + row_sums(dv.astype(F32)))

    sums = lax.fori_loop(0, TILES, attend_back, (zero_rows,) * 2)
    add_small(2, sums[0])
    add_small(3, sums[1])
    gq[...] += contract(h1s[...], dqs[...], 0, 0)
    gk[...] += contract(kin[...], dks[...], 0, 0)
    gv[...] += contract(kin[...], dvs[...], 0, 0)
    dout = contract(dks[...], wk[...], 1, 1) + contract(dvs[...], wv[...], 1, 1)
    normal = nks[...]
    ds = norm_back(dout, normal, rks[...], vrow(5)).astype(BF16)
    add_small(5, row_sums(dout * normal))
    add_small(6, row_sums(dout))
    add_small(4, row_sums(ds.astype(F32)))
    for d in range(4):
        rows = slice(d * KEYS, (d + 1) * KEYS)
        wide_rows = slice(d * width, (d + 1) * width)
        gr[wide_rows, :] += contract(pats[rows, :], ds, 0, 0)
        dps[rows, :] = contract(ds, wr[wide_rows, :], 1, 1).astype(BF16)
    tmp[...] = contract(pick[...], dps[...], 0, 0)
    xs[...] = contract(dqs[...], wq[...], 1, 1)

    def last_rows(big, sums):
        sums = list(sums)
        base = pl.multiple_of(big * 192, 64)
        outs = []
        for c in range(3):
            rows = pl.ds(base + c * 64, 64)
            dout = xs[rows, :] + msk[rows, :] * tmp[rows, :]
            normal = n1s[rows, :]
            outs.append(m1s[rows, :] + norm_back(dout, normal, r1s[rows, :], vrow(0)))
            sums[0] = sums[0] + row_sums(dout * normal)
            sums[1] = sums[1] + row_sums(dout)
        gin_ref[0, pl.ds(base, 192), :] = join_tiles(outs)
        return tuple(sums)

    sums = lax.fori_loop(0, 3, last_rows, (zero_rows,) * 2)
    add_small(0, sums[0])
    add_small(1, sums[1])


def pick_matrix():
    spot = jnp.arange(SLOTS)
    part = spot // KEYS
    key = spot % KEYS
    tile = key // KEYS_TILE
    inner = key % KEYS_TILE
    slot = tile * 64 + (2 * (inner // 4) + part // 2) * TILE + 2 * (inner % 4) + part % 2
    return (slot[:, None] == spot[None, :]).astype(BF16)


def head_mask(width):
    row = jnp.arange(8 * KEYS_TILE) // KEYS_TILE
    col = jnp.arange(width) // HEAD_DIM
    return (row[:, None] == col[None, :]).astype(BF16)


def run_block(tokens, grad_output, valid_tiles, master_a, master_b, vector_params):
    width = tokens.shape[2]
    hidden = master_b.shape[0]
    grids = tokens.shape[0] * tokens.shape[1] // SLOTS
    x = tokens.reshape(grids, SLOTS, width)
    dy = grad_output.reshape(grids, SLOTS, width)
    flags = valid_tiles.reshape(grids, TILES)
    low_a = master_a.astype(BF16)
    low_b = master_b.astype(BF16)
    weights = (
        low_a[:, :width],
        low_a[:, width : 2 * width],
        low_a[:, 2 * width : 3 * width],
        low_a[:, 3 * width : 4 * width],
        low_a[:, 4 * width :],
        low_b[:, :width],
        low_b[:, width:],
    )
    wide = vector_params[11:].reshape(11, hidden)
    consts = weights + (vector_params[:11], wide, pick_matrix(), head_mask(width))
    grid_spec = pl.BlockSpec((1, SLOTS, width), lambda g: (g, 0, 0))

    def whole(shape):
        return pl.BlockSpec(shape, lambda g: (0,) * len(shape), pipeline_mode=pl.Buffered(1))

    grad_shapes = [(width, width)] * 4 + [
        (width, hidden),
        (hidden, width),
        (width, hidden),
        (16, width),
        (16, hidden),
    ]
    tall = (SLOTS, width)
    keys = (KEYS, width)
    scratch = [
        (tall, F32),
        (tall, F32),
        (tall, F32),
        ((SLOTS, 1), F32),
        (tall, BF16),
        (tall, BF16),
        (tall, BF16),
        (tall, BF16),
        (keys, BF16),
        (keys, F32),
        ((KEYS, 1), F32),
        (keys, BF16),
        (keys, BF16),
        ((SLOTS, LANES), F32),
        (tall, BF16),
        (tall, F32),
        (tall, F32),
        (tall, F32),
        ((SLOTS, 1), F32),
        (tall, BF16),
        ((SLOTS, hidden), F32),
        ((SLOTS, hidden), F32),
        ((SLOTS, hidden), BF16),
        ((SLOTS, hidden), BF16),
        (tall, BF16),
        (tall, BF16),
        (tall, BF16),
        (tall, BF16),
        (keys, BF16),
        (keys, BF16),
        (tall, BF16),
    ]
    return pl.pallas_call(
        block_kernel,
        name="block_step",
        grid=(grids,),
        in_specs=[pl.BlockSpec(memory_space=pltpu.SMEM), grid_spec, grid_spec]
        + [whole(c.shape) for c in consts],
        out_specs=[grid_spec, grid_spec] + [whole(s) for s in grad_shapes],
        out_shape=[
            jax.ShapeDtypeStruct((grids, SLOTS, width), BF16),
            jax.ShapeDtypeStruct((grids, SLOTS, width), F32),
        ]
        + [jax.ShapeDtypeStruct(s, F32) for s in grad_shapes],
        scratch_shapes=[pltpu.VMEM(s, d) for s, d in scratch],
        compiler_params=pltpu.CompilerParams(vmem_limit_bytes=60 << 20),
    )(flags, x, dy, *consts)

SPANS_A = ((0, 1), (1, 2), (3, 1), (4, 4))
VECTOR_ROWS = 143
EXTRA = 16


def fill_codes(la, ra, lb, rb, codes, width):
    hidden = lb.shape[1]
    codes[...] = jnp.full(codes.shape, -2, jnp.int32)
    codes[0:4, 0:width] = la[...]
    codes[4:6, 0:hidden] = lb[...]
    for k, (first, count) in enumerate(SPANS_A):
        start = first * width
        span = count * width
        codes[6 + k : 7 + k, 0:span] = ra[:, start : start + span] - 2 * start
    for k in range(2):
        codes[10 + k : 11 + k, 0:width] = rb[:, k * width : (k + 1) * width] - 2 * k * width


def lane_matrix(codes, k, size):
    code = codes[k : k + 1, 0:size]
    sign = (1 - 2 * (code & 1)).astype(F32)
    spot = lax.broadcasted_iota(jnp.int32, (size, size), 0)
    return jnp.where(spot == (code >> 1), sign, 0.0).astype(BF16)


def row_matrix(codes, k, out, size):
    for start in range(0, size, LANES):
        code = codes[k : k + 1, start : start + LANES]
        spot = jnp.transpose(jnp.broadcast_to((code >> 1).astype(F32), (LANES, LANES)))
        sign = jnp.transpose(
            jnp.broadcast_to((1 - 2 * (code & 1)).astype(F32), (LANES, LANES))
        )
        for col in range(0, size, LANES):
            lane = lax.broadcasted_iota(jnp.int32, (LANES, LANES), 1).astype(F32) + col
            part = jnp.where(spot == lane, sign, 0.0).astype(BF16)
            out[start : start + LANES, col : col + LANES] = part


def vector_spots(width, hidden):
    spots = []
    for k in range(11):
        for col in range(0, width, LANES):
            spots.append((0, k, col, min(LANES, width - col)))
    for k in range(11):
        for col in range(0, hidden, LANES):
            spots.append((1, k, col, LANES))
    return spots


def rotate_kernel(
    gq, gk, gv, go, gup, gr, gdn, gsm, gwd, la, ra, lb, rb, flat_ref, vec_ref,
    codes, rows_m, ras, rbs, flat, per_block,
):
    width, hidden = gup.shape
    fill_codes(la, ra, lb, rb, codes, width)

    def dot(left, right):
        return jnp.dot(left, right, preferred_element_type=F32)

    for k, parts in enumerate(((gq,), (gk, gv), (go,), (gup,))):
        first, count = SPANS_A[k]
        right = lane_matrix(codes, 6 + k, count * width)
        total = None
        depth = right.shape[0] // len(parts)
        for p, part in enumerate(parts):
            piece = dot(part[...].astype(BF16), right[p * depth : (p + 1) * depth])
            total = piece if total is None else total + piece
        row_matrix(codes, k, rows_m, width)
        ras[:, first * width : (first + count) * width] = dot(rows_m[0:width, 0:width], total.astype(BF16))
    row_matrix(codes, 4, rows_m, hidden)
    part = dot(rows_m[...], gr[...].astype(BF16)).astype(BF16)
    rbs[:, 0:width] = dot(part, lane_matrix(codes, 10, width))
    row_matrix(codes, 5, rows_m, hidden)
    part = contract(rows_m[...], gdn[...].astype(BF16), 1, 1).astype(BF16)
    rbs[:, width : 2 * width] = dot(part, lane_matrix(codes, 11, width))
    per_row = ras.shape[1] // LANES
    for j in range(per_row):
        flat[pl.ds(j, width, stride=per_row), :] = ras[:, j * LANES : (j + 1) * LANES]
    base = width * per_row
    per_row = rbs.shape[1] // LANES
    for j in range(per_row):
        flat[pl.ds(base + j, hidden, stride=per_row), :] = rbs[:, j * LANES : (j + 1) * LANES]
    flat_ref[...] = flat[...].astype(BF16)
    vec_ref[...] = jnp.zeros(vec_ref.shape, BF16)
    for number, (kind, k, col, size) in enumerate(vector_spots(width, hidden)):
        block, row = number // per_block, number % per_block
        source = (gsm, gwd)[kind]
        vec_ref[block, row : row + 1, 0:size] = source[k : k + 1, col : col + size].astype(BF16)


def restore_kernel(
    blocks, vecs, order, la, ra, lb, rb, steps, ma, mb, vp, vf, vsec,
    na, nb, ca, cb, vg, vfn, vsn, nv,
    codes, rows_m, das, dbs, flat, wide_s, per_block,
):
    width = ma.shape[0]
    hidden = mb.shape[0]
    fill_codes(la, ra, lb, rb, codes, width)
    count, depth, _ = blocks.shape
    if depth % 8 == 0:
        for t in range(count):
            spot = pl.multiple_of(order[t] * depth, 8)
            flat[pl.ds(spot, depth), :] = blocks[t].astype(F32)
    else:
        for t in range(count):
            flat[t * depth : (t + 1) * depth, :] = blocks[t].astype(F32)
    per_row = ma.shape[1] // LANES
    for j in range(per_row):
        das[:, j * LANES : (j + 1) * LANES] = flat[pl.ds(j, width, stride=per_row), :]
    base = width * per_row
    per_row = mb.shape[1] // LANES
    for j in range(per_row):
        dbs[:, j * LANES : (j + 1) * LANES] = flat[pl.ds(base + j, hidden, stride=per_row), :]

    def dot(left, right):
        return jnp.dot(left, right, preferred_element_type=F32)

    def update(master, step, new, copy, cols):
        old = master[:, cols]
        value = old - matrix_rate * (step + weight_decay * old)
        new[:, cols] = value
        copy[:, cols] = value.astype(BF16)

    for k, (first, span) in enumerate(SPANS_A):
        size = span * width
        cols = slice(first * width, first * width + size)
        part = dot(lane_matrix(codes, k, width), das[:, cols].astype(BF16)).astype(BF16)
        row_matrix(codes, 6 + k, rows_m, size)
        update(ma, dot(part, rows_m[0:size, 0:size]), na, ca, cols)
    for k in range(2):
        cols = slice(k * width, (k + 1) * width)
        part = dot(lane_matrix(codes, 4 + k, hidden), dbs[:, cols].astype(BF16)).astype(BF16)
        row_matrix(codes, 10 + k, rows_m, width)
        update(mb, dot(part, rows_m[0:width, 0:width]), nb, cb, cols)
    for number, (kind, k, col, size) in enumerate(vector_spots(width, hidden)):
        block, row = number // per_block, number % per_block
        value = vecs[block, row : row + 1, 0:size].astype(F32)
        if kind == 0:
            vg[k : k + 1, col : col + size] = value
        else:
            wide_s[k : k + 1, col : col + size] = value
    ratio = hidden // width
    for k in range(11):
        for q in range(ratio):
            row = 11 + ratio * k + q
            vg[row : row + 1, :] = wide_s[k : k + 1, q * width : (q + 1) * width]
    grad = vg[...]
    first_new = beta_one * vf[...] + (1.0 - beta_one) * grad
    second_new = beta_two * vsec[...] + (1.0 - beta_two) * grad * grad
    vfn[...] = first_new
    vsn[...] = second_new
    move = direction_of(first_new, second_new, steps[0])
    old = vp[...]
    nv[...] = old - vector_rate * (move + weight_decay * old)


def direction_of(first_new, second_new, steps):
    count = jnp.full((1, LANES), steps, jnp.int32).astype(F32)
    log_one = -0.10536051565782628
    log_two = -0.0010005003335835335
    one = (1.0 / (1.0 - jnp.exp(count * log_one)))[:, 0:1]
    two = (1.0 / (1.0 - jnp.exp(count * log_two)))[:, 0:1]
    return first_new * one / (jnp.sqrt(second_new * two) + adam_epsilon)


def vmem_spec():
    return pl.BlockSpec(memory_space=pltpu.VMEM)


def rotate_blocks(grads, la, ra, lb, rb, blocks):
    width, hidden = grads[4].shape
    per_block = -(-VECTOR_ROWS // blocks)
    total = (width * 8 * width + hidden * 2 * width) // LANES
    return pl.pallas_call(
        functools.partial(rotate_kernel, per_block=per_block),
        name="rotate",
        in_specs=[vmem_spec()] * 13,
        out_specs=[vmem_spec()] * 2,
        out_shape=[
            jax.ShapeDtypeStruct((total, LANES), BF16),
            jax.ShapeDtypeStruct((blocks, EXTRA, LANES), BF16),
        ],
        scratch_shapes=[
            pltpu.VMEM((16, hidden), jnp.int32),
            pltpu.VMEM((hidden, hidden), BF16),
            pltpu.VMEM((width, 8 * width), F32),
            pltpu.VMEM((hidden, 2 * width), F32),
            pltpu.VMEM((total, LANES), F32),
        ],
        compiler_params=pltpu.CompilerParams(vmem_limit_bytes=60 << 20),
    )(*grads, la, ra.reshape(1, -1), lb, rb.reshape(1, -1))


def restore_blocks(blocks, vecs, order, la, ra, lb, rb, steps, ma, mb, vp, vf, vsec):
    width = ma.shape[0]
    hidden = mb.shape[0]
    per_block = -(-VECTOR_ROWS // blocks.shape[0])
    total = blocks.shape[0] * blocks.shape[1]
    smem = pl.BlockSpec(memory_space=pltpu.SMEM)
    return pl.pallas_call(
        functools.partial(restore_kernel, per_block=per_block),
        name="restore",
        in_specs=[vmem_spec()] * 2 + [smem] + [vmem_spec()] * 4 + [smem] + [vmem_spec()] * 5,
        out_specs=[vmem_spec()] * 8,
        out_shape=[
            jax.ShapeDtypeStruct(ma.shape, F32),
            jax.ShapeDtypeStruct(mb.shape, F32),
            jax.ShapeDtypeStruct(ma.shape, BF16),
            jax.ShapeDtypeStruct(mb.shape, BF16),
        ]
        + [jax.ShapeDtypeStruct(vp.shape, F32)] * 4,
        scratch_shapes=[
            pltpu.VMEM((16, hidden), jnp.int32),
            pltpu.VMEM((hidden, hidden), BF16),
            pltpu.VMEM((width, 8 * width), F32),
            pltpu.VMEM((hidden, 2 * width), F32),
            pltpu.VMEM((total, LANES), F32),
            pltpu.VMEM((16, hidden), F32),
        ],
        compiler_params=pltpu.CompilerParams(vmem_limit_bytes=60 << 20),
    )(blocks, vecs, order, la, ra.reshape(1, -1), lb, rb.reshape(1, -1), steps, ma, mb, vp, vf, vsec)


def on_device(
    tokens, grad_output, valid_tiles, master_a, master_b, vector_params, matrix_first,
    matrix_second, vector_first, vector_second, left_a, right_a, left_b, right_b,
    owner_list, step_count,
):
    out, grad_in, *grads = run_block(
        tokens, grad_output, valid_tiles, master_a, master_b, vector_params
    )
    count = owner_list.shape[0]
    flat, vecs = rotate_blocks(grads, left_a, right_a, left_b, right_b, count)
    depth = flat.shape[0] // count
    axes = ("tok", "ch")
    wire = jnp.concatenate(
        [jnp.take(flat.reshape(count, depth, LANES), owner_list, axis=0), vecs], axis=1
    )
    owned = lax.psum_scatter(wire, axes, scatter_dimension=0, tiled=True)
    matrix_grad = owned[:, :depth].astype(F32).reshape(matrix_first.shape)
    steps = step_count[0].astype(F32)
    first_new = beta_one * matrix_first + (1.0 - beta_one) * matrix_grad
    second_new = beta_two * matrix_second + (1.0 - beta_two) * matrix_grad * matrix_grad
    direction = (
        first_new
        / (1.0 - beta_one**steps)
        / (jnp.sqrt(second_new / (1.0 - beta_two**steps)) + adam_epsilon)
    )
    sent = jnp.concatenate(
        [direction.astype(BF16).reshape(1, depth, LANES), owned[:, depth:]], axis=1
    )
    every = lax.all_gather(sent, axes, axis=0, tiled=True)
    blocks = every[:, :depth]
    if depth % 8:
        order = jnp.zeros_like(owner_list).at[owner_list].set(jnp.arange(count, dtype=jnp.int32))
        blocks = jnp.take(blocks, order, axis=0)
    new_a, new_b, copy_a, copy_b, vec_grad, vec_first, vec_second, new_vec = restore_blocks(
        blocks, every[:, depth:], owner_list, left_a, right_a, left_b, right_b, step_count,
        master_a, master_b, vector_params, vector_first, vector_second,
    )
    return (
        out.reshape(tokens.shape),
        grad_in.reshape(tokens.shape),
        matrix_grad,
        first_new,
        second_new,
        new_a,
        new_b,
        copy_a,
        copy_b,
        vec_grad,
        vec_first,
        vec_second,
        new_vec,
    )


def solution(mesh):
    part = P(None, ("tok", "ch"), None)
    owned = P(("tok", "ch"), None)
    in_specs = (part,) * 3 + (P(),) * 3 + (owned,) * 2 + (P(),) * 8
    out_specs = (part,) * 2 + (owned,) * 3 + (P(),) * 8
    return jax.shard_map(
        on_device, mesh=mesh, in_specs=in_specs, out_specs=out_specs, check_vma=False
    )
```

time: 1250 us -> 435 us (0.35)
  local copies, waits for them, and re-layouts: 501 us -> 28.1 us
  other arithmetic: 308 us -> 11.1 us
  Pallas kernels: 0 us -> 187 us
  matrix products: 181 us -> 0 us
  waiting for transfers between devices: 223 us -> 193 us
    pallas_call x0 -> x3, Pallas kernels: none -> 187 us  [the longest x1 156 us: run_block(): pl.pallas_call(block_kernel, name='block_step', grid=(grids,), in_specs=[...]
    unnamed x15 -> x2, waiting for transfers between devices: 184 us -> 0.03 us
    dot_general x102 -> x0, matrix products: 181 us -> none  [the longest x14 46.2 us: times_transposed(): lax.dot_general(left_side, right_side, (((1,), (1,)), ((), ())), preferre...]
    reduce_scatter x0 -> x1, waiting for transfers between devices: none -> 143 us  [on_device(): owned = lax.psum_scatter(wire, axes, scatter_dimension=0, tiled=True)]
    gather x33 -> x1, local copies, waits for them, and re-layouts: 141 us -> 3.11 us  [on_device(): jnp.take(flat.reshape(count, depth, LANES), owner_list, axis=0)]
    reduce_sum x31 -> x0, other arithmetic: 118 us -> none  [the longest x2 49.6 us: depthwise_backward(): tap_grads.append(jnp.sum(window * grad_mixed, axis=(0, 1, 2)))]
    unnamed x844 -> x24, local copies, waits for them, and re-layouts: 101 us -> 12.4 us
    convert_element_type x29 -> x5, other arithmetic: 81.8 us -> 7.08 us  [the longest x1 2.89 us: on_device(): direction.astype(BF16).reshape(1, depth, LANES)]
  transfers between devices with their start and end apart: 10 -> 2, of which waited for: 5 -> 2; matrix products, arithmetic and copies ran while one was open for 29% -> 2% of each run, Pallas kernels for 0% -> 0%
where the time goes in v1:
time: 435 us; the launch traced here: 434 us
  waiting for transfers between devices  193 us (44%)
  Pallas kernels  187 us (43%)
  local copies, waits for them, and re-layouts  28.1 us (6%)
  between operations  15.1 us (3%)
  other arithmetic  11.1 us (3%)
    pallas_call x1, Pallas kernels, run_block(): pl.pallas_call(block_kernel, name='block_step', grid=(grids,), in_specs=[...  156 us
    reduce_scatter x1, waiting for transfers between devices, on_device(): owned = lax.psum_scatter(wire, axes, scatter_dimension=0, tiled=True)  143 us
    all_gather x1, waiting for transfers between devices, on_device(): every = lax.all_gather(sent, axes, axis=0, tiled=True)  50.1 us
    pallas_call x1, Pallas kernels, restore_blocks(): pl.pallas_call(functools.partial(restore_kernel, per_block=per_block), na...  16.2 us
    pallas_call x1, Pallas kernels, rotate_blocks(): pl.pallas_call(functools.partial(rotate_kernel, per_block=per_block), nam...  14.2 us
    unnamed x24, local copies, waits for them, and re-layouts  12.4 us
  transfers between devices with their start and end apart: 2, of which 2 were waited for; matrix products, arithmetic and copies ran while one was open for 2% of the time, Pallas kernels for 0%

profile of v1, /device:TPU:0, one launch (start us, length us, event | category | flops | bytes accessed | tf_op | source)
XLA Modules:
  0.0 434.3 jit_solution(14927241208756810227)
XLA Ops:
  7.3 2.2 convert_element_type.20
  9.5 1.2 fusion.35
  10.7 1.0 slice.58.wup
  11.8 0.6 slice.46.vec
  12.4 0.2 convert_element_type.21
  12.6 1.7 fusion.34
  14.4 2.2 copy.33
  16.6 2.2 copy.34
  18.9 1.1 fusion.pick
  19.9 0.7 reshape.246.wide
  20.6 0.6 reshape.249.ra
  21.2 0.6 reshape.250.rb
  21.8 0.7 compare_convert_fusion.hmask
  22.6 156.1 %block_step.1 = (bf16[4,576,320]{2,1,0:T(8,128)(2,1)}, f32[4,576,320]{2,1,0:T(8,128)}, f32[320,320]{1,0:T(8,128)}, f32[320,320]{1,0:T(8,128)}, f32[320,320]{1,0:...) custom-call(s32[4,9]{1,0:T(4,128)} %bitcast.18, ...), custom_call_target="tpu_custom_call" | custom-call | tf_op jit(solution)/shard_map/block_step/pallas_call | solution.py:490
  178.7 14.2 %rotate.1 = (bf16[12800,128]{1,0:T(8,128)(2,1)}, bf16[32,16,128]{2,1,0:T(8,128)(2,1)}) custom-call(f32[320,320]{1,0:T(8,128)} %get-tuple-element.36.gq, f32[320,320]{1,0:T(8,128)} %get-tuple-element.37.gk, f32[320,320]{1,0:T(8,128)} %get-tuple-element.38.gv, f32[320,320]{1,0:T(8,128)} %get-tuple-element.39.go, f32[320,1280]{1,0:T(8,128)} %get-tuple-element.40.gup, ...), custom_call_target="tpu_custom_call" | custom-call | tf_op jit(solution)/shard_map/rotate/pallas_call | solution.py:679
  192.9 3.1 gather_fusion
  196.0 0.4 broadcast_select_fusion
  196.4 0.5 copy-done.6
  196.9 2.0 pad_maximum_fusion
  198.9 0.0 all-gather.2.cloned.1.call-start
  199.9 143.3 %reduce-scatter.2.cloned.1.call-done = bf16[1,416,128]{2,1,0:T(8,128)(2,1)} async-done(((bf16[32,416,128]{2,1,0:T(8,128)(2,1)}), bf16[1,416,128]{2,1,0:T(8,128)(2,1)}) %reduce-scatter.2.cloned.1.call-update) | async-done | bytes 106512 | tf_op jit(solution)/shard_map/reduce_scatter | solution.py:744
  343.2 0.9 slice_convert_fusion
  344.1 0.7 copy-done.4
  344.8 2.9 convert_reduce_fusion
  347.6 0.7 slice.62
  348.3 0.7 pad_maximum_fusion.1
  349.0 3.0 copy.36
  352.0 3.7 copy.35
  355.7 50.1 %all-gather.2.cloned.1.call-done = bf16[32,416,128]{2,1,0:T(8,128)(2,1)} async-done(((bf16[1,416,128]{2,1,0:T(8,128)(2,1)}), bf16[32,416,128]{2,1,0:T(8,128)(2,1)}) %all-gather.2.cloned.1.call-update) | async-done | bytes 3407888 | tf_op jit(solution)/shard_map/all_gather | solution.py:757
  405.9 3.8 slice.63.blocks
  409.7 1.6 slice.64.vecs
  411.2 16.2 %restore.1 = (f32[320,2560]{1,0:T(8,128)}, f32[1280,640]{1,0:T(8,128)}, bf16[320,2560]{1,0:T(8,128)(2,1)}, bf16[1280,640]{1,0:T(8,128)(2,1)}, f32[55,320]{1,0:T(...) custom-call(bf16[32,400,128]{2,1,0:T(8,128)(2,1)} %slice.63.blocks, ...), custom_call_target="tpu_custom_call" | custom-call | tf_op jit(solution)/shard_map/restore/pallas_call | solution.py:705
  (28 shorter events, 0.2 us)
Async XLA Ops:
  7.2 4.6 %copy-start.5 = (f32[55,320]{1,0:T(8,128)S(1)}, f32[55,320]{1,0:T(8,128)}, u32[]{:S(2)}) copy-start(f32[55,320]{1,0:T(8,128)} %vp.1) | copy-start | bytes 211204
  7.2 5.2 %copy-start.9 = (s32[32]{0:T(128)S(1)}, s32[32]{0:T(128)}, u32[]{:S(2)}) copy-start(s32[32]{0:T(128)} %order.1) | copy-start | bytes 388
  7.2 5.2 %copy-start = (f32[1280,640]{1,0:T(8,128)S(1)}, f32[1280,640]{1,0:T(8,128)}, u32[]{:S(2)}) copy-start(f32[1280,640]{1,0:T(8,128)} %mb.1) | copy-start | bytes 9830404
  7.2 335.9 %reduce-scatter.2.cloned.1.call-start = ((), (), s32[]{:S(2)}) async-start(), calls=%async_computation.1 | async-start | bytes 3514368 | tf_op jit(solution)/shard_map/reduce_scatter | solution.py:744
  12.6 1.8 copy-start.2
  12.6 4.0 copy-start.3
  14.4 6.2 %copy-start.7 = (s32[2560]{0:T(1024)S(1)}, s32[2560]{0:T(1024)}, u32[]{:S(2)}) copy-start(s32[2560]{0:T(1024)} %param.27) | copy-start | bytes 30724
  14.4 6.8 %copy-start.8 = (s32[640]{0:T(1024)S(1)}, s32[640]{0:T(1024)}, u32[]{:S(2)}) copy-start(s32[640]{0:T(1024)} %param.29) | copy-start | bytes 7684
  196.0 0.9 copy-start.6
  198.9 150.1 %copy-start.1 = (f32[4,576,320]{2,1,0:T(8,128)S(1)}, f32[4,576,320]{2,1,0:T(8,128)}, u32[]{:S(2)}) copy-start(f32[4,576,320]{2,1,0:T(8,128)} %get-tuple-element.35) | copy-start | bytes 8847364
  198.9 206.9 %all-gather.2.cloned.1.call-start = ((), (), s32[]{:S(2)}) async-start(), calls=%async_computation.2 | async-start | bytes 3514368 | tf_op jit(solution)/shard_map/all_gather | solution.py:757
  344.1 0.7 copy-start.4
Sparse Core Ops, SparseCore 0:
  199.1 144.0 reduce-scatter.1
  349.1 56.6 all-gather.1

commit v2 on v1

--- a/solution.py
+++ b/solution.py
@@ -505,7 +505,6 @@
 
 SPANS_A = ((0, 1), (1, 2), (3, 1), (4, 4))
 VECTOR_ROWS = 143
-EXTRA = 16
 
 
 def fill_codes(la, ra, lb, rb, codes, width):
@@ -553,7 +552,7 @@
 
 
 def rotate_kernel(
-    gq, gk, gv, go, gup, gr, gdn, gsm, gwd, la, ra, lb, rb, flat_ref, vec_ref,
+    order, gq, gk, gv, go, gup, gr, gdn, gsm, gwd, la, ra, lb, rb, wire,
     codes, rows_m, ras, rbs, flat, per_block,
 ):
     width, hidden = gup.shape
@@ -585,30 +584,37 @@
     per_row = rbs.shape[1] // LANES
     for j in range(per_row):
         flat[pl.ds(base + j, hidden, stride=per_row), :] = rbs[:, j * LANES : (j + 1) * LANES]
-    flat_ref[...] = flat[...].astype(BF16)
-    vec_ref[...] = jnp.zeros(vec_ref.shape, BF16)
+    count, tall, _ = wire.shape
+    depth = flat.shape[0] // count
+
+    def place(t, carry):
+        wire[t, 0:depth, :] = flat[pl.ds(order[t] * depth, depth), :].astype(BF16)
+        wire[t, depth:tall, :] = jnp.zeros((tall - depth, LANES), BF16)
+        return carry
+
+    lax.fori_loop(0, count, place, 0)
     for number, (kind, k, col, size) in enumerate(vector_spots(width, hidden)):
-        block, row = number // per_block, number % per_block
+        block, row = number // per_block, depth + number % per_block
         source = (gsm, gwd)[kind]
-        vec_ref[block, row : row + 1, 0:size] = source[k : k + 1, col : col + size].astype(BF16)
+        wire[block, row : row + 1, 0:size] = source[k : k + 1, col : col + size].astype(BF16)
 
 
 def restore_kernel(
-    blocks, vecs, order, la, ra, lb, rb, steps, ma, mb, vp, vf, vsec,
+    blocks, order, la, ra, lb, rb, steps, ma, mb, vp, vf, vsec,
     na, nb, ca, cb, vg, vfn, vsn, nv,
     codes, rows_m, das, dbs, flat, wide_s, per_block,
 ):
     width = ma.shape[0]
     hidden = mb.shape[0]
     fill_codes(la, ra, lb, rb, codes, width)
-    count, depth, _ = blocks.shape
-    if depth % 8 == 0:
-        for t in range(count):
-            spot = pl.multiple_of(order[t] * depth, 8)
-            flat[pl.ds(spot, depth), :] = blocks[t].astype(F32)
-    else:
-        for t in range(count):
-            flat[t * depth : (t + 1) * depth, :] = blocks[t].astype(F32)
+    count = blocks.shape[0]
+    depth = flat.shape[0] // count
+
+    def place(t, carry):
+        flat[pl.ds(order[t] * depth, depth), :] = blocks[t, 0:depth, :].astype(F32)
+        return carry
+
+    lax.fori_loop(0, count, place, 0)
     per_row = ma.shape[1] // LANES
     for j in range(per_row):
         das[:, j * LANES : (j + 1) * LANES] = flat[pl.ds(j, width, stride=per_row), :]
@@ -638,8 +644,8 @@
         row_matrix(codes, 10 + k, rows_m, width)
         update(mb, dot(part, rows_m[0:width, 0:width]), nb, cb, cols)
     for number, (kind, k, col, size) in enumerate(vector_spots(width, hidden)):
-        block, row = number // per_block, number % per_block
-        value = vecs[block, row : row + 1, 0:size].astype(F32)
+        block, row = number // per_block, depth + number % per_block
+        value = blocks[block, row : row + 1, 0:size].astype(F32)
         if kind == 0:
             vg[k : k + 1, col : col + size] = value
         else:
@@ -672,19 +678,19 @@
     return pl.BlockSpec(memory_space=pltpu.VMEM)
 
 
-def rotate_blocks(grads, la, ra, lb, rb, blocks):
+def rotate_blocks(order, grads, la, ra, lb, rb):
     width, hidden = grads[4].shape
+    blocks = order.shape[0]
     per_block = -(-VECTOR_ROWS // blocks)
     total = (width * 8 * width + hidden * 2 * width) // LANES
+    tall = -(-(total // blocks + per_block) // 32) * 32
+    smem = pl.BlockSpec(memory_space=pltpu.SMEM)
     return pl.pallas_call(
         functools.partial(rotate_kernel, per_block=per_block),
         name="rotate",
-        in_specs=[vmem_spec()] * 13,
-        out_specs=[vmem_spec()] * 2,
-        out_shape=[
-            jax.ShapeDtypeStruct((total, LANES), BF16),
-            jax.ShapeDtypeStruct((blocks, EXTRA, LANES), BF16),
-        ],
+        in_specs=[smem] + [vmem_spec()] * 13,
+        out_specs=vmem_spec(),
+        out_shape=jax.ShapeDtypeStruct((blocks, tall, LANES), BF16),
         scratch_shapes=[
             pltpu.VMEM((16, hidden), jnp.int32),
             pltpu.VMEM((hidden, hidden), BF16),
@@ -693,19 +699,19 @@
             pltpu.VMEM((total, LANES), F32),
         ],
         compiler_params=pltpu.CompilerParams(vmem_limit_bytes=60 << 20),
-    )(*grads, la, ra.reshape(1, -1), lb, rb.reshape(1, -1))
-
-
-def restore_blocks(blocks, vecs, order, la, ra, lb, rb, steps, ma, mb, vp, vf, vsec):
+    )(order, *grads, la, ra.reshape(1, -1), lb, rb.reshape(1, -1))
+
+
+def restore_blocks(blocks, order, la, ra, lb, rb, steps, ma, mb, vp, vf, vsec):
     width = ma.shape[0]
     hidden = mb.shape[0]
     per_block = -(-VECTOR_ROWS // blocks.shape[0])
-    total = blocks.shape[0] * blocks.shape[1]
+    total = (ma.size + mb.size) // LANES
     smem = pl.BlockSpec(memory_space=pltpu.SMEM)
     return pl.pallas_call(
         functools.partial(restore_kernel, per_block=per_block),
         name="restore",
-        in_specs=[vmem_spec()] * 2 + [smem] + [vmem_spec()] * 4 + [smem] + [vmem_spec()] * 5,
+        in_specs=[vmem_spec(), smem] + [vmem_spec()] * 4 + [smem] + [vmem_spec()] * 5,
         out_specs=[vmem_spec()] * 8,
         out_shape=[
             jax.ShapeDtypeStruct(ma.shape, F32),
@@ -723,68 +729,184 @@
             pltpu.VMEM((16, hidden), F32),
         ],
         compiler_params=pltpu.CompilerParams(vmem_limit_bytes=60 << 20),
-    )(blocks, vecs, order, la, ra.reshape(1, -1), lb, rb.reshape(1, -1), steps, ma, mb, vp, vf, vsec)
+    )(blocks, order, la, ra.reshape(1, -1), lb, rb.reshape(1, -1), steps, ma, mb, vp, vf, vsec)
+
+
+def exchange_kernel(wire, first, second, steps, grad, first_new, second_new, every, *scratch,
+                    plan, bits, depth):
+    buffers = []
+    spot = 0
+    for _, _, order in plan:
+        buffers.append(scratch[spot : spot + len(order)])
+        spot += len(order)
+    rs_send, rs_recv, ag_send, ag_recv = scratch[spot:]
+    tok = lax.axis_index("tok")
+    side = lax.axis_index("ch")
+
+    def mine(axis):
+        return side if axis == "ch" else lax.rem(lax.div(tok, 2**axis), 2)
+
+    def peer(axis):
+        if axis == "ch":
+            return {"ch": 1 - side}
+        return {"tok": tok + 2**axis - 2 ** (axis + 1) * mine(axis)}
+
+    axes = [*reversed(range(bits)), "ch"]
+    barrier = pltpu.get_barrier_semaphore()
+    for axis in axes:
+        pl.semaphore_signal(barrier, inc=1, device_id=peer(axis), device_id_type=pl.DeviceIdType.MESH)
+    pl.semaphore_wait(barrier, len(axes))
+
+    chunks = range(len(plan))
+    left = [list(axes) for _ in chunks]
+    held = [wire for _ in chunks]
+    pending = []
+
+    def region(c, choice):
+        index = tuple(choice(axis) for axis in left[c])
+        start, size, _ = plan[c]
+        rows = pl.ds(start, size) if held[c] is wire else slice(None)
+        return index + (rows, slice(None))
+
+    def scatter_start(c, s):
+        axis = plan[c][2][s]
+        index = region(c, lambda a: 1 - mine(a) if a == axis else slice(None))
+        copy = pltpu.make_async_remote_copy(
+            held[c].at[index], buffers[c][s], rs_send.at[c, s], rs_recv.at[c, s],
+            device_id=peer(axis), device_id_type=pl.DeviceIdType.MESH,
+        )
+        copy.start()
+        pending.append(copy)
+        return copy
+
+    def scatter_keep(c, s):
+        axis = plan[c][2][s]
+        return held[c][region(c, lambda a: mine(a) if a == axis else slice(None))]
+
+    def gather_start(c, s):
+        start, size, order = plan[c]
+        axis = order[len(order) - 1 - s]
+        done = order[len(order) - s :]
+        index = tuple(slice(None) if a in done else mine(a) for a in axes)
+        piece = every.at[index + (pl.ds(start, size), slice(None))]
+        copy = pltpu.make_async_remote_copy(
+            piece, piece, ag_send.at[c, s], ag_recv.at[c, s],
+            device_id=peer(axis), device_id_type=pl.DeviceIdType.MESH,
+        )
+        copy.start()
+        pending.append(copy)
+        return copy
+
+    stages = len(axes)
+    flying = [scatter_start(c, 0) for c in chunks]
+    for s in range(stages):
+        for c in chunks:
+            start, size, order = plan[c]
+            flying[c].wait_recv()
+            kept = scatter_keep(c, s)
+            buffer = buffers[c][s]
+            if s < stages - 1:
+                buffer[...] = buffer[...] + kept
+                left[c].remove(order[s])
+                held[c] = buffer
+                flying[c] = scatter_start(c, s + 1)
+                continue
+            total = buffer[...].astype(F32) + kept.astype(F32)
+            count = max(0, min(depth - start, size))
+            parts = []
+            if count:
+                rows = slice(start, start + count)
+                owned = total[:count]
+                grad[rows, :] = owned
+                one = beta_one * first[rows, :] + (1.0 - beta_one) * owned
+                two = beta_two * second[rows, :] + (1.0 - beta_two) * owned * owned
+                first_new[rows, :] = one
+                second_new[rows, :] = two
+                parts.append(direction_of(one, two, steps[0]))
+            if count < size:
+                parts.append(total[count:])
+            ready = parts[0] if len(parts) == 1 else jnp.concatenate(parts, axis=0)
+            own = tuple(mine(a) for a in axes)
+            every[own + (slice(start, start + size), slice(None))] = ready.astype(BF16)
+            flying[c] = gather_start(c, 0)
+    for s in range(stages):
+        for c in chunks:
+            flying[c].wait_recv()
+            if s < stages - 1:
+                flying[c] = gather_start(c, s + 1)
+    for copy in pending:
+        copy.wait_send()
+
+
+def exchange_blocks(wire, first, second, steps, bits):
+    count, tall, _ = wire.shape
+    depth = first.shape[0]
+    units = tall // 16
+    small = max(1, units * 6 // 26)
+    large = (units - small + 1) // 2
+    rest = list(range(2, bits))
+    sizes = (small, large, units - small - large)
+    orders = ([0] + rest + ["ch", 1], [0, "ch", 1] + rest, [0, 1, "ch"] + rest)
+    plan = []
+    start = 0
+    for size, order in zip(sizes, orders):
+        plan.append((start, size * 16, order))
+        start += size * 16
+    scratch = []
+    for _, size, order in plan:
+        for s in range(len(order)):
+            scratch.append(pltpu.VMEM((2,) * (len(order) - 1 - s) + (size, LANES), BF16))
+    for _ in range(4):
+        scratch.append(pltpu.SemaphoreType.DMA((len(plan), bits + 1)))
+    shape = (2,) * (bits + 1) + (tall, LANES)
+    block = jax.ShapeDtypeStruct((depth, LANES), F32)
+    grad, first_new, second_new, every = pl.pallas_call(
+        functools.partial(exchange_kernel, plan=plan, bits=bits, depth=depth),
+        name="exchange",
+        in_specs=[vmem_spec()] * 3 + [pl.BlockSpec(memory_space=pltpu.SMEM)],
+        out_specs=[vmem_spec()] * 4,
+        out_shape=[block, block, block, jax.ShapeDtypeStruct(shape, BF16)],
+        scratch_shapes=scratch,
+        compiler_params=pltpu.CompilerParams(
+            vmem_limit_bytes=60 << 20, collective_id=0, has_side_effects=True
+        ),
+    )(wire.reshape(shape), first, second, steps)
+    return grad, first_new, second_new, every.reshape(wire.shape)
 
 
 def on_device(
     tokens, grad_output, valid_tiles, master_a, master_b, vector_params, matrix_first,
     matrix_second, vector_first, vector_second, left_a, right_a, left_b, right_b,
-    owner_list, step_count,
+    owner_list, step_count, bits,
 ):
     out, grad_in, *grads = run_block(
         tokens, grad_output, valid_tiles, master_a, master_b, vector_params
     )
-    count = owner_list.shape[0]
-    flat, vecs = rotate_blocks(grads, left_a, right_a, left_b, right_b, count)
-    depth = flat.shape[0] // count
-    axes = ("tok", "ch")
-    wire = jnp.concatenate(
-        [jnp.take(flat.reshape(count, depth, LANES), owner_list, axis=0), vecs], axis=1
+    wire = rotate_blocks(owner_list, grads, left_a, right_a, left_b, right_b)
+    shape = matrix_first.shape
+    grad, first_new, second_new, every = exchange_blocks(
+        wire, matrix_first.reshape(-1, LANES), matrix_second.reshape(-1, LANES), step_count, bits
     )
-    owned = lax.psum_scatter(wire, axes, scatter_dimension=0, tiled=True)
-    matrix_grad = owned[:, :depth].astype(F32).reshape(matrix_first.shape)
-    steps = step_count[0].astype(F32)
-    first_new = beta_one * matrix_first + (1.0 - beta_one) * matrix_grad
-    second_new = beta_two * matrix_second + (1.0 - beta_two) * matrix_grad * matrix_grad
-    direction = (
-        first_new
-        / (1.0 - beta_one**steps)
-        / (jnp.sqrt(second_new / (1.0 - beta_two**steps)) + adam_epsilon)
-    )
-    sent = jnp.concatenate(
-        [direction.astype(BF16).reshape(1, depth, LANES), owned[:, depth:]], axis=1
-    )
-    every = lax.all_gather(sent, axes, axis=0, tiled=True)
-    blocks = every[:, :depth]
-    if depth % 8:
-        order = jnp.zeros_like(owner_list).at[owner_list].set(jnp.arange(count, dtype=jnp.int32))
-        blocks = jnp.take(blocks, order, axis=0)
-    new_a, new_b, copy_a, copy_b, vec_grad, vec_first, vec_second, new_vec = restore_blocks(
-        blocks, every[:, depth:], owner_list, left_a, right_a, left_b, right_b, step_count,
+    restored = restore_blocks(
+        every, owner_list, left_a, right_a, left_b, right_b, step_count,
         master_a, master_b, vector_params, vector_first, vector_second,
     )
     return (
         out.reshape(tokens.shape),
         grad_in.reshape(tokens.shape),
-        matrix_grad,
-        first_new,
-        second_new,
-        new_a,
-        new_b,
-        copy_a,
-        copy_b,
-        vec_grad,
-        vec_first,
-        vec_second,
-        new_vec,
+        grad.reshape(shape),
+        first_new.reshape(shape),
+        second_new.reshape(shape),
+        *restored,
     )
 
 
 def solution(mesh):
+    bits = mesh.shape["tok"].bit_length() - 1
     part = P(None, ("tok", "ch"), None)
     owned = P(("tok", "ch"), None)
     in_specs = (part,) * 3 + (P(),) * 3 + (owned,) * 2 + (P(),) * 8
     out_specs = (part,) * 2 + (owned,) * 3 + (P(),) * 8
     return jax.shard_map(
-        on_device, mesh=mesh, in_specs=in_specs, out_specs=out_specs, check_vma=False
+        functools.partial(on_device, bits=bits), mesh=mesh, in_specs=in_specs, out_specs=out_specs, check_vma=False
     )

time: 435 us -> 272 us (0.63)
  waiting for transfers between devices: 193 us -> 0 us
  Pallas kernels: 187 us -> 246 us
  between operations: 15.1 us -> 1.37 us
  local copies, waits for them, and re-layouts: 28.1 us -> 20.2 us
  other arithmetic: 11.1 us -> 4.27 us
    reduce_scatter x1 -> x0, waiting for transfers between devices: 143 us -> none  [on_device(): owned = lax.psum_scatter(wire, axes, scatter_dimension=0, tiled=True)]
    pallas_call x0 -> x1, Pallas kernels: none -> 57.4 us  [exchange_blocks(): pl.pallas_call(functools.partial(exchange_kernel, plan=plan, bits=bits, d...]
    all_gather x1 -> x0, waiting for transfers between devices: 50.1 us -> none  [on_device(): every = lax.all_gather(sent, axes, axis=0, tiled=True)]
    slice x3 -> x0, local copies, waits for them, and re-layouts: 6.05 us -> none  [the longest x1 3.8 us: on_device(): blocks = every[:, :depth]]
    unnamed x24 -> x27, local copies, waits for them, and re-layouts: 12.4 us -> 13.8 us
  transfers between devices with their start and end apart: 2 -> 0, of which waited for: 2 -> 0; matrix products, arithmetic and copies ran while one was open for 2% -> 0% of each run, Pallas kernels for 0% -> 0%
where the time goes in v2:
time: 272 us
  Pallas kernels  246 us (90%)
  local copies, waits for them, and re-layouts  20.2 us (7%)
  other arithmetic  4.27 us (2%)
    pallas_call x1, Pallas kernels, run_block(): pl.pallas_call(block_kernel, name='block_step', grid=(grids,), in_specs=[...  156 us
    pallas_call x1, Pallas kernels, exchange_blocks(): pl.pallas_call(functools.partial(exchange_kernel, plan=plan, bits=bits, d...  57.4 us
    pallas_call x1, Pallas kernels, restore_blocks(): pl.pallas_call(functools.partial(restore_kernel, per_block=per_block), na...  17.9 us
    pallas_call x1, Pallas kernels, rotate_blocks(): pl.pallas_call(functools.partial(rotate_kernel, per_block=per_block), nam...  14.6 us
    unnamed x27, local copies, waits for them, and re-layouts  13.8 us

profile of v2, /device:TPU:0, one launch (start us, length us, event | category | flops | bytes accessed | tf_op | source)
XLA Modules:
  0.0 271.9 jit_solution(7227584663079835036)
XLA Ops:
  0.6 0.0 copy-start
  0.7 2.2 convert_element_type.12
  2.9 1.2 fusion.33
  4.1 0.0 copy-done
  4.1 0.2 convert_element_type.13
  4.3 1.7 fusion.32
  6.0 1.0 slice.40.wup
  7.0 0.7 copy-done.2
  7.7 2.2 copy.29
  9.9 0.0 copy-done.3
  9.9 2.2 copy.30
  12.2 1.1 fusion.pick
  13.3 0.0 copy-done.4
  13.3 0.7 reshape.205.wide
  14.0 0.7 compare_convert_fusion.hmask
  14.8 0.6 slice.34.vec
  15.4 156.1 %block_step.1 = (bf16[4,576,320]{2,1,0:T(8,128)(2,1)}, f32[4,576,320]{2,1,0:T(8,128)}, f32[320,320]{1,0:T(8,128)}, f32[320,320]{1,0:T(8,128)}, f32[320,320]{1,0:...) custom-call(s32[4,9]{1,0:T(4,128)} %bitcast.23, ...), custom_call_target="tpu_custom_call" | custom-call | tf_op jit(solution)/shard_map/block_step/pallas_call | solution.py:490
  171.5 0.0 copy-done.8
  171.5 0.6 reshape.208.ra
  172.1 0.0 copy-done.9
  172.1 0.6 reshape.209.rb
  172.7 14.6 %rotate.1 = bf16[32,416,128]{2,1,0:T(8,128)(2,1)} custom-call(s32[32]{0:T(128)} %order.3, f32[320,320]{1,0:T(8,128)} %get-tuple-element.38.gq, f32[320,320]{1,0:T(8,128)} %get-tuple-element.39.gk, f32[320,320]{1,0:T(8,128)} %get-tuple-element.40.gv, f32[320,320]{1,0:T(8,128)} %get-tuple-element.41.go, f32[320,1280]{1,0:T(8,128)} %get-tuple-element.42.gup, ...), custom_call_target="tpu_custom_call" | custom-call | tf_op jit(solution)/shard_map/rotate/pallas_call | solution.py:688
  187.9 57.4 %exchange.1 = (f32[400,128]{1,0:T(8,128)}, f32[400,128]{1,0:T(8,128)}, f32[400,128]{1,0:T(8,128)}, bf16[2,2,2,2,2,416,128]{6,5,4,3,2,1,0:T(8,128)(2,1)}) custom-call(bf16[2,2,2,2,2,416,128]{6,5,4,3,2,1,0:T(8,128)(2,1)} %bitcast.12, f32[400,128]{1,0:T(8,128)} %bitcast.21, f32[400,128]{1,0:T(8,128)} %bitcast.22, s32[1]{0:T(128)S(6)} %copy.36.steps), custom_call_target="tpu_custom_call" | custom-call | tf_op jit(solution)/shard_map/exchange/pallas_call | solution.py:863
  245.3 0.0 copy-start.1
  245.4 17.9 %restore.1 = (f32[320,2560]{1,0:T(8,128)}, f32[1280,640]{1,0:T(8,128)}, bf16[320,2560]{1,0:T(8,128)(2,1)}, bf16[1280,640]{1,0:T(8,128)(2,1)}, f32[55,320]{1,0:T(...) custom-call(bf16[32,416,128]{2,1,0:T(8,128)(2,1)} %bitcast.16, s32[32]{0:T(128)} %order.3, ...), custom_call_target="tpu_custom_call" | custom-call | tf_op jit(solution)/shard_map/restore/pallas_call | solution.py:711
  263.2 0.0 copy-done.1
  263.2 2.8 %copy.32 = f32[2,1152,320]{1,2,0:T(8,128)} copy(f32[2,1152,320]{2,1,0:T(8,128)S(1)} %bitcast.15) | data formatting | bytes 5898240
  266.0 3.8 %copy.31 = bf16[2,1152,320]{1,2,0:T(8,128)(2,1)} copy(bf16[2,1152,320]{2,1,0:T(8,128)(2,1)} %bitcast.17) | data formatting | bytes 2949120
  269.8 0.0 copy-done.7
  269.8 0.7 copy.37
  270.5 0.7 copy.38
  271.2 0.7 copy.39
  (14 shorter events, 0.1 us)
Async XLA Ops:
  0.6 3.5 %copy-start = (f32[1280,640]{1,0:T(8,128)S(1)}, f32[1280,640]{1,0:T(8,128)}, u32[]{:S(2)}) copy-start(f32[1280,640]{1,0:T(8,128)} %mb.1) | copy-start | bytes 9830404
  6.0 1.7 copy-start.2
  7.7 2.2 copy-start.3
  9.9 3.3 %copy-start.4 = (f32[55,320]{1,0:T(8,128)S(1)}, f32[55,320]{1,0:T(8,128)}, u32[]{:S(2)}) copy-start(f32[55,320]{1,0:T(8,128)} %vp.1) | copy-start | bytes 211204
  15.4 156.1 %copy-start.8 = (s32[2560]{0:T(1024)S(1)}, s32[2560]{0:T(1024)}, u32[]{:S(2)}) copy-start(s32[2560]{0:T(1024)} %param.27) | copy-start | bytes 30724
  15.4 156.7 %copy-start.9 = (s32[640]{0:T(1024)S(1)}, s32[640]{0:T(1024)}, u32[]{:S(2)}) copy-start(s32[640]{0:T(1024)} %param.29) | copy-start | bytes 7684
  245.3 17.9 %copy-start.1 = (f32[4,576,320]{2,1,0:T(8,128)S(1)}, f32[4,576,320]{2,1,0:T(8,128)}, u32[]{:S(2)}) copy-start(f32[4,576,320]{2,1,0:T(8,128)} %get-tuple-element.37) | copy-start | bytes 8847364
  266.0 3.8 %copy-start.7 = (f32[400,128]{1,0:T(8,128)S(1)}, f32[400,128]{1,0:T(8,128)}, u32[]{:S(2)}) copy-start(f32[400,128]{1,0:T(8,128)} %get-tuple-element.47) | copy-start | bytes 614404
  266.0 4.5 %copy-start.6 = (f32[400,128]{1,0:T(8,128)S(1)}, f32[400,128]{1,0:T(8,128)}, u32[]{:S(2)}) copy-start(f32[400,128]{1,0:T(8,128)} %get-tuple-element.48) | copy-start | bytes 614404
  266.0 5.2 %copy-start.5 = (f32[400,128]{1,0:T(8,128)S(1)}, f32[400,128]{1,0:T(8,128)}, u32[]{:S(2)}) copy-start(f32[400,128]{1,0:T(8,128)} %get-tuple-element.49) | copy-start | bytes 614404

commit v3 on v2

--- a/solution.py
+++ b/solution.py
@@ -76,7 +76,7 @@
 
 
 def gelu_parts(e):
-    gauss = jnp.exp(-0.5 * e * e)
+    gauss = jnp.exp2((-0.5 * 1.4426950408889634) * (e * e))
     size = jnp.abs(e)
     t = 1.0 / (1.0 + (0.3275911 * 0.7071067811865476) * size)
     poly = t * (
@@ -94,8 +94,19 @@
 
 def block_kernel(
     flags,
+    order,
     x_ref,
     dy_ref,
+    ma,
+    mb,
+    vec,
+    la,
+    ra,
+    lb,
+    rb,
+    out_ref,
+    gin_ref,
+    wire,
     wq,
     wk,
     wv,
@@ -103,12 +114,9 @@
     wup,
     wr,
     wdn,
-    vec,
     wide,
     pick,
     hmask,
-    out_ref,
-    gin_ref,
     gq,
     gk,
     gv,
@@ -118,6 +126,16 @@
     gdn,
     gsm,
     gwd,
+    mas,
+    mbs,
+    sems,
+    xrow,
+    dyrow,
+    orow,
+    grow,
+    codes,
+    rows_m,
+    flat,
     msk,
     xs,
     n1s,
@@ -149,15 +167,39 @@
     dks,
     dvs,
     dps,
+    *,
+    per,
+    per_block,
 ):
     g = pl.program_id(0)
-    width = x_ref.shape[2]
+    part = lax.rem(g, per)
+    width = x_ref.shape[1]
     hidden = wup.shape[1]
+    spans = x_ref.shape[2] // LANES
+    base_row = part * SLOTS
+    load_a = pltpu.make_async_copy(ma, mas, sems.at[0])
+    load_b = pltpu.make_async_copy(mb, mbs, sems.at[1])
 
     @pl.when(g == 0)
     def _():
+        load_a.start()
+        load_b.start()
+        pick[...] = pick_matrix()
+        hmask[...] = head_mask(width)
+        ratio = hidden // width
+        for k in range(11):
+            for q in range(ratio):
+                row = 11 + ratio * k + q
+                wide[k : k + 1, q * width : (q + 1) * width] = vec[row : row + 1, :]
         for ref in (gq, gk, gv, go, gup, gr, gdn, gsm, gwd):
             ref[...] = jnp.zeros(ref.shape, F32)
+
+    @pl.when(part == 0)
+    def _():
+        for c in range(spans):
+            cols = slice(c * LANES, (c + 1) * LANES)
+            xrow[cols, :] = jnp.transpose(x_ref[0, :, cols].astype(F32)).astype(BF16)
+            dyrow[cols, :] = jnp.transpose(dy_ref[0, :, cols].astype(F32)).astype(BF16)
 
     row = lax.broadcasted_iota(jnp.int32, (TILE * TILE, width), 0)
     inside = jnp.where((row % TILE < TILE - 1) & (row < TILE * (TILE - 1)), 1.0, 0.0)
@@ -174,8 +216,8 @@
 
     def first_norm(big, carry):
         base = pl.multiple_of(big * 192, 64)
-        tiles = split_tiles(x_ref[0, pl.ds(base, 192), :].astype(F32))
-        grads = split_tiles(dy_ref[0, pl.ds(base, 192), :].astype(F32))
+        tiles = split_tiles(xrow[pl.ds(base_row + base, 192), :].astype(F32))
+        grads = split_tiles(dyrow[pl.ds(base_row + base, 192), :].astype(F32))
         for c in range(3):
             rows = pl.ds(base + c * 64, 64)
             normal, inverse = normalize(tiles[c])
@@ -190,6 +232,17 @@
         return carry
 
     lax.fori_loop(0, 3, first_norm, 0)
+
+    @pl.when(g == 0)
+    def _():
+        load_a.wait()
+        for k, ref in enumerate((wq, wk, wv, wo)):
+            ref[...] = mas[:, k * width : (k + 1) * width].astype(BF16)
+        wup[...] = mas[:, 4 * width :].astype(BF16)
+        load_b.wait()
+        wr[...] = mbs[:, :width].astype(BF16)
+        wdn[...] = mbs[:, width:].astype(BF16)
+
     qs[...] = (jnp.dot(h1s[...], wq[...], preferred_element_type=F32) + vrow(2)).astype(BF16)
     pats[...] = jnp.dot(pick[...], hms[...], preferred_element_type=F32).astype(BF16)
     reduced = vrow(4)
@@ -229,7 +282,7 @@
         ).astype(BF16)
         return carry
 
-    lax.fori_loop(0, TILES, attend_tile, 0)
+    lax.fori_loop(0, TILES, attend_tile, 0, unroll=3)
     tmp[...] = jnp.dot(ctxs[...], wo[...], preferred_element_type=F32)
 
     def second_norm(t, carry):
@@ -242,7 +295,7 @@
         h2s[rows, :] = (normal * vrow(8) + vrow(9)).astype(BF16)
         return carry
 
-    lax.fori_loop(0, TILES, second_norm, 0)
+    lax.fori_loop(0, TILES, second_norm, 0, unroll=3)
     for c in range(hidden // 256):
         cols = slice(c * 256, (c + 1) * 256)
         us[:, cols] = jnp.dot(h2s[...], wup[:, cols], preferred_element_type=F32)
@@ -320,7 +373,7 @@
     def middle_rows(big, sums):
         sums = list(sums)
         base = pl.multiple_of(big * 192, 64)
-        grads = split_tiles(dy_ref[0, pl.ds(base, 192), :].astype(F32))
+        grads = split_tiles(dyrow[pl.ds(base_row + base, 192), :].astype(F32))
         outs = []
         for c in range(3):
             rows = pl.ds(base + c * 64, 64)
@@ -336,7 +389,7 @@
             sums[1] = sums[1] + row_sums(dout)
             sums[2] = sums[2] + row_sums(low.astype(F32))
             sums[3] = sums[3] + row_sums(dms[rows, :].astype(F32))
-        out_ref[0, pl.ds(base, 192), :] = join_tiles(outs).astype(BF16)
+        orow[pl.ds(base_row + base, 192), :] = join_tiles(outs).astype(BF16)
         return tuple(sums)
 
     sums = lax.fori_loop(0, 3, middle_rows, (zero_rows,) * 4)
@@ -365,7 +418,7 @@
         dvs[keys, :] = dv
         return (sums[0] + row_sums(dq.astype(F32)), sums[1] + row_sums(dv.astype(F32)))
 
-    sums = lax.fori_loop(0, TILES, attend_back, (zero_rows,) * 2)
+    sums = lax.fori_loop(0, TILES, attend_back, (zero_rows,) * 2, unroll=3)
     add_small(2, sums[0])
     add_small(3, sums[1])
     gq[...] += contract(h1s[...], dqs[...], 0, 0)
@@ -396,162 +449,29 @@
             outs.append(m1s[rows, :] + norm_back(dout, normal, r1s[rows, :], vrow(0)))
             sums[0] = sums[0] + row_sums(dout * normal)
             sums[1] = sums[1] + row_sums(dout)
-        gin_ref[0, pl.ds(base, 192), :] = join_tiles(outs)
+        grow[pl.ds(base_row + base, 192), :] = join_tiles(outs)
         return tuple(sums)
 
     sums = lax.fori_loop(0, 3, last_rows, (zero_rows,) * 2)
     add_small(0, sums[0])
     add_small(1, sums[1])
 
-
-def pick_matrix():
-    spot = jnp.arange(SLOTS)
-    part = spot // KEYS
-    key = spot % KEYS
-    tile = key // KEYS_TILE
-    inner = key % KEYS_TILE
-    slot = tile * 64 + (2 * (inner // 4) + part // 2) * TILE + 2 * (inner % 4) + part % 2
-    return (slot[:, None] == spot[None, :]).astype(BF16)
-
-
-def head_mask(width):
-    row = jnp.arange(8 * KEYS_TILE) // KEYS_TILE
-    col = jnp.arange(width) // HEAD_DIM
-    return (row[:, None] == col[None, :]).astype(BF16)
-
-
-def run_block(tokens, grad_output, valid_tiles, master_a, master_b, vector_params):
-    width = tokens.shape[2]
-    hidden = master_b.shape[0]
-    grids = tokens.shape[0] * tokens.shape[1] // SLOTS
-    x = tokens.reshape(grids, SLOTS, width)
-    dy = grad_output.reshape(grids, SLOTS, width)
-    flags = valid_tiles.reshape(grids, TILES)
-    low_a = master_a.astype(BF16)
-    low_b = master_b.astype(BF16)
-    weights = (
-        low_a[:, :width],
-        low_a[:, width : 2 * width],
-        low_a[:, 2 * width : 3 * width],
-        low_a[:, 3 * width : 4 * width],
-        low_a[:, 4 * width :],
-        low_b[:, :width],
-        low_b[:, width:],
-    )
-    wide = vector_params[11:].reshape(11, hidden)
-    consts = weights + (vector_params[:11], wide, pick_matrix(), head_mask(width))
-    grid_spec = pl.BlockSpec((1, SLOTS, width), lambda g: (g, 0, 0))
-
-    def whole(shape):
-        return pl.BlockSpec(shape, lambda g: (0,) * len(shape), pipeline_mode=pl.Buffered(1))
-
-    grad_shapes = [(width, width)] * 4 + [
-        (width, hidden),
-        (hidden, width),
-        (width, hidden),
-        (16, width),
-        (16, hidden),
-    ]
-    tall = (SLOTS, width)
-    keys = (KEYS, width)
-    scratch = [
-        (tall, F32),
-        (tall, F32),
-        (tall, F32),
-        ((SLOTS, 1), F32),
-        (tall, BF16),
-        (tall, BF16),
-        (tall, BF16),
-        (tall, BF16),
-        (keys, BF16),
-        (keys, F32),
-        ((KEYS, 1), F32),
-        (keys, BF16),
-        (keys, BF16),
-        ((SLOTS, LANES), F32),
-        (tall, BF16),
-        (tall, F32),
-        (tall, F32),
-        (tall, F32),
-        ((SLOTS, 1), F32),
-        (tall, BF16),
-        ((SLOTS, hidden), F32),
-        ((SLOTS, hidden), F32),
-        ((SLOTS, hidden), BF16),
-        ((SLOTS, hidden), BF16),
-        (tall, BF16),
-        (tall, BF16),
-        (tall, BF16),
-        (tall, BF16),
-        (keys, BF16),
-        (keys, BF16),
-        (tall, BF16),
-    ]
-    return pl.pallas_call(
-        block_kernel,
-        name="block_step",
-        grid=(grids,),
-        in_specs=[pl.BlockSpec(memory_space=pltpu.SMEM), grid_spec, grid_spec]
-        + [whole(c.shape) for c in consts],
-        out_specs=[grid_spec, grid_spec] + [whole(s) for s in grad_shapes],
-        out_shape=[
-            jax.ShapeDtypeStruct((grids, SLOTS, width), BF16),
-            jax.ShapeDtypeStruct((grids, SLOTS, width), F32),
-        ]
-        + [jax.ShapeDtypeStruct(s, F32) for s in grad_shapes],
-        scratch_shapes=[pltpu.VMEM(s, d) for s, d in scratch],
-        compiler_params=pltpu.CompilerParams(vmem_limit_bytes=60 << 20),
-    )(flags, x, dy, *consts)
-
-SPANS_A = ((0, 1), (1, 2), (3, 1), (4, 4))
-VECTOR_ROWS = 143
-
-
-def fill_codes(la, ra, lb, rb, codes, width):
-    hidden = lb.shape[1]
-    codes[...] = jnp.full(codes.shape, -2, jnp.int32)
-    codes[0:4, 0:width] = la[...]
-    codes[4:6, 0:hidden] = lb[...]
-    for k, (first, count) in enumerate(SPANS_A):
-        start = first * width
-        span = count * width
-        codes[6 + k : 7 + k, 0:span] = ra[:, start : start + span] - 2 * start
-    for k in range(2):
-        codes[10 + k : 11 + k, 0:width] = rb[:, k * width : (k + 1) * width] - 2 * k * width
-
-
-def lane_matrix(codes, k, size):
-    code = codes[k : k + 1, 0:size]
-    sign = (1 - 2 * (code & 1)).astype(F32)
-    spot = lax.broadcasted_iota(jnp.int32, (size, size), 0)
-    return jnp.where(spot == (code >> 1), sign, 0.0).astype(BF16)
-
-
-def row_matrix(codes, k, out, size):
-    for start in range(0, size, LANES):
-        code = codes[k : k + 1, start : start + LANES]
-        spot = jnp.transpose(jnp.broadcast_to((code >> 1).astype(F32), (LANES, LANES)))
-        sign = jnp.transpose(
-            jnp.broadcast_to((1 - 2 * (code & 1)).astype(F32), (LANES, LANES))
+    @pl.when(part == per - 1)
+    def _():
+        for c in range(spans):
+            cols = slice(c * LANES, (c + 1) * LANES)
+            out_ref[0, :, cols] = jnp.transpose(orow[cols, :].astype(F32)).astype(BF16)
+            gin_ref[0, :, cols] = jnp.transpose(grow[cols, :])
+
+    @pl.when(g == pl.num_programs(0) - 1)
+    def _():
+        rotate(
+            order, gq, gk, gv, go, gup, gr, gdn, gsm, gwd, la, ra, lb, rb, wire,
+            codes, rows_m, mas, mbs, flat, per_block,
         )
-        for col in range(0, size, LANES):
-            lane = lax.broadcasted_iota(jnp.int32, (LANES, LANES), 1).astype(F32) + col
-            part = jnp.where(spot == lane, sign, 0.0).astype(BF16)
-            out[start : start + LANES, col : col + LANES] = part
-
-
-def vector_spots(width, hidden):
-    spots = []
-    for k in range(11):
-        for col in range(0, width, LANES):
-            spots.append((0, k, col, min(LANES, width - col)))
-    for k in range(11):
-        for col in range(0, hidden, LANES):
-            spots.append((1, k, col, LANES))
-    return spots
-
-
-def rotate_kernel(
+
+
+def rotate(
     order, gq, gk, gv, go, gup, gr, gdn, gsm, gwd, la, ra, lb, rb, wire,
     codes, rows_m, ras, rbs, flat, per_block,
 ):
@@ -577,26 +497,204 @@
     row_matrix(codes, 5, rows_m, hidden)
     part = contract(rows_m[...], gdn[...].astype(BF16), 1, 1).astype(BF16)
     rbs[:, width : 2 * width] = dot(part, lane_matrix(codes, 11, width))
-    per_row = ras.shape[1] // LANES
-    for j in range(per_row):
-        flat[pl.ds(j, width, stride=per_row), :] = ras[:, j * LANES : (j + 1) * LANES]
-    base = width * per_row
-    per_row = rbs.shape[1] // LANES
-    for j in range(per_row):
-        flat[pl.ds(base + j, hidden, stride=per_row), :] = rbs[:, j * LANES : (j + 1) * LANES]
     count, tall, _ = wire.shape
-    depth = flat.shape[0] // count
-
-    def place(t, carry):
-        wire[t, 0:depth, :] = flat[pl.ds(order[t] * depth, depth), :].astype(BF16)
-        wire[t, depth:tall, :] = jnp.zeros((tall - depth, LANES), BF16)
-        return carry
-
-    lax.fori_loop(0, count, place, 0)
+    half = count // 2
+    depth = 2 * flat.shape[0] // count
+    for first, (source, rows) in enumerate(((ras, width), (rbs, hidden))):
+        per_row = source.shape[1] // LANES
+        for j in range(per_row):
+            cols = slice(j * LANES, (j + 1) * LANES)
+            flat[pl.ds(j, rows, stride=per_row), :] = source[:, cols]
+
+        def place(t, carry, first=first):
+            spot = order[t] - first * half
+
+            @pl.when((spot >= 0) & (spot < half))
+            def _():
+                wire[t, 0:depth, :] = flat[pl.ds(spot * depth, depth), :].astype(BF16)
+                wire[t, depth:tall, :] = jnp.zeros((tall - depth, LANES), BF16)
+
+            return carry
+
+        lax.fori_loop(0, count, place, 0)
     for number, (kind, k, col, size) in enumerate(vector_spots(width, hidden)):
         block, row = number // per_block, depth + number % per_block
         source = (gsm, gwd)[kind]
         wire[block, row : row + 1, 0:size] = source[k : k + 1, col : col + size].astype(BF16)
+
+
+def pick_matrix():
+    spot = lax.broadcasted_iota(jnp.int32, (SLOTS, SLOTS), 0)
+    lane = lax.broadcasted_iota(jnp.int32, (SLOTS, SLOTS), 1)
+    part = spot // KEYS
+    key = spot - part * KEYS
+    tile = key >> 4
+    inner = key & 15
+    row = 2 * (inner >> 2) + (part >> 1)
+    col = 2 * (inner & 3) + (part & 1)
+    return jnp.where(tile * 64 + row * TILE + col == lane, 1.0, 0.0).astype(BF16)
+
+
+def head_mask(width):
+    row = lax.broadcasted_iota(jnp.int32, (8 * KEYS_TILE, width), 0) >> 4
+    col = lax.broadcasted_iota(jnp.int32, (8 * KEYS_TILE, width), 1) >> 6
+    return jnp.where(row == col, 1.0, 0.0).astype(BF16)
+
+
+def run_block(
+    tokens, grad_output, valid_tiles, master_a, master_b, vector_params, order, la, ra, lb, rb
+):
+    width = tokens.shape[2]
+    hidden = master_b.shape[0]
+    rows = tokens.shape[1]
+    per = rows // SLOTS
+    grids = tokens.shape[0] * per
+    flags = valid_tiles.reshape(grids, TILES)
+    blocks = order.shape[0]
+    per_block = -(-VECTOR_ROWS // blocks)
+    total = (master_a.size + master_b.size) // LANES
+    tall_block = -(-(total // blocks + per_block) // 32) * 32
+    flip = pl.BlockSpec((1, width, rows), lambda g: (g // per, 0, 0))
+    tall = (SLOTS, width)
+    keys = (KEYS, width)
+    scratch = [((width, width), BF16)] * 4 + [
+        ((width, hidden), BF16),
+        ((hidden, width), BF16),
+        ((hidden, width), BF16),
+        ((16, hidden), F32),
+        ((SLOTS, SLOTS), BF16),
+        ((8 * KEYS_TILE, width), BF16),
+    ]
+    scratch += [((width, width), F32)] * 4 + [
+        ((width, hidden), F32),
+        ((hidden, width), F32),
+        ((width, hidden), F32),
+        ((16, width), F32),
+        ((16, hidden), F32),
+        (master_a.shape, F32),
+        (master_b.shape, F32),
+        None,
+        ((rows, width), BF16),
+        ((rows, width), BF16),
+        ((rows, width), BF16),
+        ((rows, width), F32),
+        ((16, hidden), jnp.int32),
+        ((hidden, hidden), BF16),
+        ((total // 2, LANES), F32),
+    ]
+    scratch += [
+        (tall, F32),
+        (tall, F32),
+        (tall, F32),
+        ((SLOTS, 1), F32),
+        (tall, BF16),
+        (tall, BF16),
+        (tall, BF16),
+        (tall, BF16),
+        (keys, BF16),
+        (keys, F32),
+        ((KEYS, 1), F32),
+        (keys, BF16),
+        (keys, BF16),
+        ((SLOTS, LANES), F32),
+        (tall, BF16),
+        (tall, F32),
+        (tall, F32),
+        (tall, F32),
+        ((SLOTS, 1), F32),
+        (tall, BF16),
+        ((SLOTS, hidden), F32),
+        ((SLOTS, hidden), F32),
+        ((SLOTS, hidden), BF16),
+        ((SLOTS, hidden), BF16),
+        (tall, BF16),
+        (tall, BF16),
+        (tall, BF16),
+        (tall, BF16),
+        (keys, BF16),
+        (keys, BF16),
+        (tall, BF16),
+    ]
+    smem = pl.BlockSpec(memory_space=pltpu.SMEM)
+    anywhere = pl.BlockSpec(memory_space=pl.ANY)
+
+    def whole(shape):
+        return pl.BlockSpec(shape, lambda g: (0,) * len(shape), pipeline_mode=pl.Buffered(1))
+
+    small = (vector_params, la, ra.reshape(1, -1), lb, rb.reshape(1, -1))
+    out, gin, wire = pl.pallas_call(
+        functools.partial(block_kernel, per=per, per_block=per_block),
+        name="block_step",
+        grid=(grids,),
+        in_specs=[smem, smem, flip, flip, anywhere, anywhere] + [whole(c.shape) for c in small],
+        out_specs=[flip, flip, whole((blocks, tall_block, LANES))],
+        out_shape=[
+            jax.ShapeDtypeStruct((tokens.shape[0], width, rows), BF16),
+            jax.ShapeDtypeStruct((tokens.shape[0], width, rows), F32),
+            jax.ShapeDtypeStruct((blocks, tall_block, LANES), BF16),
+        ],
+        scratch_shapes=[
+            pltpu.SemaphoreType.DMA((2,)) if item is None else pltpu.VMEM(*item)
+            for item in scratch
+        ],
+        compiler_params=pltpu.CompilerParams(vmem_limit_bytes=67_000_000),
+    )(
+        flags,
+        order,
+        jnp.transpose(tokens, (0, 2, 1)),
+        jnp.transpose(grad_output, (0, 2, 1)),
+        master_a,
+        master_b,
+        *small,
+    )
+    return jnp.transpose(out, (0, 2, 1)), jnp.transpose(gin, (0, 2, 1)), wire
+
+SPANS_A = ((0, 1), (1, 2), (3, 1), (4, 4))
+VECTOR_ROWS = 143
+
+
+def fill_codes(la, ra, lb, rb, codes, width):
+    hidden = lb.shape[1]
+    codes[...] = jnp.full(codes.shape, -2, jnp.int32)
+    codes[0:4, 0:width] = la[...]
+    codes[4:6, 0:hidden] = lb[...]
+    for k, (first, count) in enumerate(SPANS_A):
+        start = first * width
+        span = count * width
+        codes[6 + k : 7 + k, 0:span] = ra[:, start : start + span] - 2 * start
+    for k in range(2):
+        codes[10 + k : 11 + k, 0:width] = rb[:, k * width : (k + 1) * width] - 2 * k * width
+
+
+def lane_matrix(codes, k, size):
+    code = codes[k : k + 1, 0:size]
+    sign = (1 - 2 * (code & 1)).astype(F32)
+    spot = lax.broadcasted_iota(jnp.int32, (size, size), 0)
+    return jnp.where(spot == (code >> 1), sign, 0.0).astype(BF16)
+
+
+def row_matrix(codes, k, out, size):
+    for start in range(0, size, LANES):
+        code = codes[k : k + 1, start : start + LANES]
+        spot = jnp.transpose(jnp.broadcast_to((code >> 1).astype(F32), (LANES, LANES)))
+        sign = jnp.transpose(
+            jnp.broadcast_to((1 - 2 * (code & 1)).astype(F32), (LANES, LANES))
+        )
+        for col in range(0, size, LANES):
+            lane = lax.broadcasted_iota(jnp.int32, (LANES, LANES), 1).astype(F32) + col
+            part = jnp.where(spot == lane, sign, 0.0).astype(BF16)
+            out[start : start + LANES, col : col + LANES] = part
+
+
+def vector_spots(width, hidden):
+    spots = []
+    for k in range(11):
+        for col in range(0, width, LANES):
+            spots.append((0, k, col, min(LANES, width - col)))
+    for k in range(11):
+        for col in range(0, hidden, LANES):
+            spots.append((1, k, col, LANES))
+    return spots
 
 
 def restore_kernel(
@@ -676,30 +774,6 @@
 
 def vmem_spec():
     return pl.BlockSpec(memory_space=pltpu.VMEM)
-
-
-def rotate_blocks(order, grads, la, ra, lb, rb):
-    width, hidden = grads[4].shape
-    blocks = order.shape[0]
-    per_block = -(-VECTOR_ROWS // blocks)
-    total = (width * 8 * width + hidden * 2 * width) // LANES
-    tall = -(-(total // blocks + per_block) // 32) * 32
-    smem = pl.BlockSpec(memory_space=pltpu.SMEM)
-    return pl.pallas_call(
-        functools.partial(rotate_kernel, per_block=per_block),
-        name="rotate",
-        in_specs=[smem] + [vmem_spec()] * 13,
-        out_specs=vmem_spec(),
-        out_shape=jax.ShapeDtypeStruct((blocks, tall, LANES), BF16),
-        scratch_shapes=[
-            pltpu.VMEM((16, hidden), jnp.int32),
-            pltpu.VMEM((hidden, hidden), BF16),
-            pltpu.VMEM((width, 8 * width), F32),
-            pltpu.VMEM((hidden, 2 * width), F32),
-            pltpu.VMEM((total, LANES), F32),
-        ],
-        compiler_params=pltpu.CompilerParams(vmem_limit_bytes=60 << 20),
-    )(order, *grads, la, ra.reshape(1, -1), lb, rb.reshape(1, -1))
 
 
 def restore_blocks(blocks, order, la, ra, lb, rb, steps, ma, mb, vp, vf, vsec):
@@ -879,10 +953,10 @@
     matrix_second, vector_first, vector_second, left_a, right_a, left_b, right_b,
     owner_list, step_count, bits,
 ):
-    out, grad_in, *grads = run_block(
-        tokens, grad_output, valid_tiles, master_a, master_b, vector_params
+    out, grad_in, wire = run_block(
+        tokens, grad_output, valid_tiles, master_a, master_b, vector_params, owner_list,
+        left_a, right_a, left_b, right_b,
     )
-    wire = rotate_blocks(owner_list, grads, left_a, right_a, left_b, right_b)
     shape = matrix_first.shape
     grad, first_new, second_new, every = exchange_blocks(
         wire, matrix_first.reshape(-1, LANES), matrix_second.reshape(-1, LANES), step_count, bits
@@ -892,8 +966,8 @@
         master_a, master_b, vector_params, vector_first, vector_second,
     )
     return (
-        out.reshape(tokens.shape),
-        grad_in.reshape(tokens.shape),
+        out,
+        grad_in,
         grad.reshape(shape),
         first_new.reshape(shape),
         second_new.reshape(shape),

time: 272 us -> 241 us (0.89)
  local copies, waits for them, and re-layouts: 20.2 us -> 4.63 us
  Pallas kernels: 246 us -> 235 us
  other arithmetic: 4.27 us -> 0 us
    unnamed x27 -> x9, local copies, waits for them, and re-layouts: 13.8 us -> 2.06 us
    pallas_call x2 -> x1, Pallas kernels: 171 us -> 159 us  [run_block(): pl.pallas_call(functools.partial(block_kernel, per=per, per_block=per_blo...]
    slice x5 -> x0, local copies, waits for them, and re-layouts: 4.53 us -> none  [the longest x1 1.75 us: run_block(): low_b[:, width:]]
    convert_element_type x4 -> x0, other arithmetic: 4.23 us -> none  [the longest x1 2.25 us: run_block(): low_a = master_a.astype(BF16)]
where the time goes in v3:
time: 241 us
  Pallas kernels  235 us (98%)
  local copies, waits for them, and re-layouts  4.63 us (2%)
    pallas_call x1, Pallas kernels, run_block(): pl.pallas_call(functools.partial(block_kernel, per=per, per_block=per_blo...  159 us
    pallas_call x1, Pallas kernels, exchange_blocks(): pl.pallas_call(functools.partial(exchange_kernel, plan=plan, bits=bits, d...  58.2 us
    pallas_call x1, Pallas kernels, restore_blocks(): pl.pallas_call(functools.partial(restore_kernel, per_block=per_block), na...  17.6 us

profile of v3, /device:TPU:0, one launch (start us, length us, event | category | flops | bytes accessed | tf_op | source)
XLA Modules:
  0.0 240.8 jit_solution(15644566627701652096)
XLA Ops:
  1.3 1.3 reshape.60.rb
  2.6 1.3 reshape.59.ra
  3.9 159.1 %block_step.1 = (bf16[2,320,1152]{2,1,0:T(8,128)(2,1)}, f32[2,320,1152]{2,1,0:T(8,128)}, bf16[32,416,128]{2,1,0:T(8,128)(2,1)}) custom-call(s32[4,9]{1,0:T(4,128)} %bitcast.21, s32[32]{0:T(128)} %order.3, bf16[2,320,1152]{2,1,0:T(8,128)(2,1)} %bitcast.14, bf16[2,320,1152]{2,1,0:T(8,128)(2,1)} %bitcast.15, f32[320,2560]{1,0:T(8,128)} %ma.3, f32[1280,640]{1,0:T(8,128)} %mb.3, ...), custom_call_target="tpu_custom_call" | custom-call | tf_op jit(solution)/shard_map/block_step/pallas_call | solution.py:625
  163.0 58.2 %exchange.1 = (f32[400,128]{1,0:T(8,128)}, f32[400,128]{1,0:T(8,128)}, f32[400,128]{1,0:T(8,128)}, bf16[2,2,2,2,2,416,128]{6,5,4,3,2,1,0:T(8,128)(2,1)}) custom-call(bf16[2,2,2,2,2,416,128]{6,5,4,3,2,1,0:T(8,128)(2,1)} %bitcast.13, f32[400,128]{1,0:T(8,128)} %bitcast.19, f32[400,128]{1,0:T(8,128)} %bitcast.20, s32[1]{0:T(128)S(6)} %copy.32.steps), custom_call_target="tpu_custom_call" | custom-call | tf_op jit(solution)/shard_map/exchange/pallas_call | solution.py:937
  221.2 0.0 copy-start.2
  221.2 0.0 copy-start.1
  221.2 0.0 copy-start
  221.2 17.6 %restore.1 = (f32[320,2560]{1,0:T(8,128)}, f32[1280,640]{1,0:T(8,128)}, bf16[320,2560]{1,0:T(8,128)(2,1)}, bf16[1280,640]{1,0:T(8,128)(2,1)}, f32[55,320]{1,0:T(...) custom-call(bf16[32,416,128]{2,1,0:T(8,128)(2,1)} %bitcast.12, s32[32]{0:T(128)} %order.3, ...), custom_call_target="tpu_custom_call" | custom-call | tf_op jit(solution)/shard_map/restore/pallas_call | solution.py:785
  238.8 0.0 copy-done.2
  238.8 0.7 copy.33
  239.5 0.0 copy-done.1
  239.5 0.7 copy.34
  240.2 0.0 copy-done
  240.2 0.7 copy.35
Async XLA Ops:
  221.2 17.6 %copy-start.2 = (f32[400,128]{1,0:T(8,128)S(1)}, f32[400,128]{1,0:T(8,128)}, u32[]{:S(2)}) copy-start(f32[400,128]{1,0:T(8,128)} %get-tuple-element.31) | copy-start | bytes 614404
  221.2 18.3 %copy-start.1 = (f32[400,128]{1,0:T(8,128)S(1)}, f32[400,128]{1,0:T(8,128)}, u32[]{:S(2)}) copy-start(f32[400,128]{1,0:T(8,128)} %get-tuple-element.32) | copy-start | bytes 614404
  221.2 18.9 %copy-start = (f32[400,128]{1,0:T(8,128)S(1)}, f32[400,128]{1,0:T(8,128)}, u32[]{:S(2)}) copy-start(f32[400,128]{1,0:T(8,128)} %get-tuple-element.33) | copy-start | bytes 614404

commit v4 on v3

--- a/solution.py
+++ b/solution.py
@@ -55,13 +55,8 @@
     return jnp.sum(values.reshape(rows // 8, 8, cols), axis=0)
 
 
-def group_all(values, op):
-    lane = lax.broadcasted_iota(jnp.int32, values.shape, 1)
-    for step in (1, 2, 4, 8):
-        low = pltpu.roll(values, step, 1)
-        high = pltpu.roll(values, LANES - step, 1)
-        values = op(values, jnp.where((lane & step) != 0, low, high))
-    return values
+def by_head(values):
+    return values.reshape(HEADS, KEYS_TILE, values.shape[1])
 
 
 def split_tiles(rows):
@@ -156,10 +151,17 @@
     n2s,
     r2s,
     h2s,
-    us,
-    dhs,
-    hids,
-    dus,
+    dmt,
+    h2t,
+    acc,
+    u_a,
+    d_a,
+    hid_a,
+    du_a,
+    u_b,
+    d_b,
+    hid_b,
+    du_b,
     dms,
     das,
     dcs,
@@ -191,7 +193,7 @@
             for q in range(ratio):
                 row = 11 + ratio * k + q
                 wide[k : k + 1, q * width : (q + 1) * width] = vec[row : row + 1, :]
-        for ref in (gq, gk, gv, go, gup, gr, gdn, gsm, gwd):
+        for ref in (gq, gk, gv, go, gup, gr, gdn, gsm, acc):
             ref[...] = jnp.zeros(ref.shape, F32)
 
     @pl.when(part == 0)
@@ -262,24 +264,20 @@
 
     def spread(ref, t):
         part = ref[pl.ds(pl.multiple_of(t * KEYS_TILE, KEYS_TILE), KEYS_TILE), :]
-        return jnp.concatenate([part] * 8, axis=0) * hmask[...]
+        return jnp.concatenate([part] * HEADS, axis=0) * hmask[...]
 
     def gather_heads(big):
-        big = big * hmask[...].astype(F32)
-        total = big[0:KEYS_TILE]
-        for h in range(1, HEADS):
-            total = total + big[h * KEYS_TILE : (h + 1) * KEYS_TILE]
-        return total
+        big = by_head(big * hmask[...].astype(F32))
+        return jnp.sum(big, axis=0)
 
     def attend_tile(t, carry):
         rows = pl.ds(pl.multiple_of(t * 64, 64), 64)
-        scores = contract(qs[rows, :], spread(ks, t), 1, 1) * score_scale
-        exped = jnp.exp(scores - group_all(scores, jnp.maximum))
-        probs = exped / group_all(exped, jnp.add)
-        ps[rows, :] = probs
-        ctxs[rows, :] = jnp.dot(
-            probs.astype(BF16), spread(vs, t), preferred_element_type=F32
-        ).astype(BF16)
+        scores = by_head(contract(spread(ks, t), qs[rows, :], 1, 1) * score_scale)
+        exped = jnp.exp(scores - jnp.max(scores, axis=1, keepdims=True))
+        probs = exped * (1.0 / jnp.sum(exped, axis=1, keepdims=True))
+        probs = probs.reshape(HEADS * KEYS_TILE, 64)
+        ps[pl.ds(pl.multiple_of(t * 80, 16), 80), :] = probs
+        ctxs[rows, :] = contract(probs.astype(BF16), spread(vs, t), 0, 0).astype(BF16)
         return carry
 
     lax.fori_loop(0, TILES, attend_tile, 0, unroll=3)
@@ -296,79 +294,145 @@
         return carry
 
     lax.fori_loop(0, TILES, second_norm, 0, unroll=3)
-    for c in range(hidden // 256):
-        cols = slice(c * 256, (c + 1) * 256)
-        us[:, cols] = jnp.dot(h2s[...], wup[:, cols], preferred_element_type=F32)
-        dhs[:, cols] = contract(dms[...], wdn[cols, :], 1, 1)
-
-    def mix_lanes(lane, carry):
-        cols = pl.ds(pl.multiple_of(lane * LANES, LANES), LANES)
-        bias_up = wide[0:1, cols]
-        bias_dw = wide[1:2, cols]
-        taps = [wide[2 + k : 3 + k, cols] for k in range(9)]
-
-        def mix_tile(t, sums):
-            sums = list(sums)
-            rows = pl.ds(pl.multiple_of(t * 64, 64), 64)
-            mask = msk[rows, 0:LANES]
-            ups = (us[rows, cols] + bias_up) * mask
-            mid = [ups[i * 8 : (i + 1) * 8] for i in range(7)]
-            shifted = [
-                [pltpu.roll(v, 1, 0) for v in mid],
-                mid,
-                [pltpu.roll(v, 7, 0) for v in mid],
-            ]
-            grads = dhs[rows, cols]
-            hid_rows = []
-            de_rows = []
-            for i in range(7):
-                e = bias_dw
-                for a in range(3):
-                    if 0 <= i + a - 1 < 7:
-                        for b in range(3):
-                            e = e + taps[3 * a + b] * shifted[b][i + a - 1]
-                phi, gauss = gelu_parts(e)
-                hid_rows.append(e * phi)
-                de = grads[i * 8 : (i + 1) * 8] * (phi + e * gauss)
-                de_rows.append(de)
-                sums[1] = sums[1] + de
-                for a in range(3):
-                    if 0 <= i + a - 1 < 7:
-                        for b in range(3):
-                            k = 2 + 3 * a + b
-                            sums[k] = sums[k] + de * shifted[b][i + a - 1]
-            zero = jnp.zeros((8, LANES), F32)
-            hids[rows, cols] = jnp.concatenate(hid_rows + [zero], axis=0).astype(BF16)
-            back = [
-                [pltpu.roll(v, 7, 0) for v in de_rows],
-                de_rows,
-                [pltpu.roll(v, 1, 0) for v in de_rows],
-            ]
-            du_rows = []
-            for i in range(7):
-                du = None
-                for a in range(3):
-                    if 0 <= i - a + 1 < 7:
-                        for b in range(3):
-                            term = taps[3 * a + b] * back[b][i - a + 1]
-                            du = term if du is None else du + term
-                du_rows.append(du * mask[i * 8 : (i + 1) * 8])
-            du_low = jnp.concatenate(du_rows + [zero], axis=0).astype(BF16)
-            dus[rows, cols] = du_low
-            sums[0] = sums[0] + row_sums(du_low.astype(F32))
-            return tuple(sums)
-
+    for r in range(3):
+        rows = slice(r * 192, (r + 1) * 192)
+        dmt[r] = jnp.transpose(dms[rows, :])
+        h2t[r] = jnp.transpose(h2s[rows, :])
+    for ref in (tmp, xs):
+        ref[...] = jnp.zeros(ref.shape, F32)
+    for ref in (hid_b, du_b):
+        ref[...] = jnp.zeros(ref.shape, BF16)
+
+    def spots(step):
+        group = lax.div(step, 3)
+        big = step - group * 3
+        return big, pl.ds(pl.multiple_of(big * 192, 64), 192), pl.ds(
+            pl.multiple_of(group * 256, 256), 256
+        )
+
+    def feed(step, u_ref, d_ref):
+        big, rows, cols = spots(step)
+
+        def up():
+            u_ref[...] = jnp.dot(h2s[rows, :], wup[:, cols], preferred_element_type=F32)
+
+        def down():
+            d_ref[...] = contract(dms[rows, :], wdn[cols, :], 1, 1)
+
+        return [up, down]
+
+    def drain(step, hid_ref, du_ref):
+        big, rows, cols = spots(step)
+
+        def one():
+            tmp[rows, :] += jnp.dot(hid_ref[...], wdn[cols, :], preferred_element_type=F32)
+
+        def two():
+            xs[rows, :] += contract(du_ref[...], wup[:, cols], 1, 1)
+
+        def three():
+            gdn[:, cols] += jnp.dot(dmt[big], hid_ref[...], preferred_element_type=F32)
+
+        def four():
+            gup[:, cols] += jnp.dot(h2t[big], du_ref[...], preferred_element_type=F32)
+
+        return [one, two, three, four]
+
+    def mix(step, u_ref, d_ref, hid_ref, du_ref, extras):
+        big = lax.rem(step, 3)
+        extras = list(extras)
+        for lane in range(2):
+            local = slice(lane * LANES, (lane + 1) * LANES)
+            cols = pl.ds(
+                pl.multiple_of(lax.div(step, 3) * 256 + lane * LANES, LANES), LANES
+            )
+            bias_up = wide[0:1, cols]
+            bias_dw = wide[1:2, cols]
+            taps = [wide[2 + k : 3 + k, cols] for k in range(9)]
+            sums = [jnp.zeros((8, LANES), F32)] * 11
+            for c in range(3):
+                rows = slice(c * 64, (c + 1) * 64)
+                mask = msk[pl.ds(pl.multiple_of(big * 192 + c * 64, 64), 64), 0:LANES]
+                sums = mix_unit(
+                    u_ref, d_ref, hid_ref, du_ref, rows, local, mask, bias_up, bias_dw, taps, sums
+                )
+                if extras:
+                    extras.pop(0)()
+            for k in range(11):
+                acc[k * 8 : (k + 1) * 8, cols] += sums[k]
+        for extra in extras:
+            extra()
+
+    def mix_unit(
+        u_ref, d_ref, hid_ref, du_ref, rows, local, mask, bias_up, bias_dw, taps, sums
+    ):
+        sums = list(sums)
+        ups = (u_ref[rows, local] + bias_up) * mask
+        mid = [ups[i * 8 : (i + 1) * 8] for i in range(7)]
+        shifted = [
+            [pltpu.roll(v, 1, 0) for v in mid],
+            mid,
+            [pltpu.roll(v, 7, 0) for v in mid],
+        ]
+        grads = d_ref[rows, local]
+        hid_rows = []
+        de_rows = []
+        for i in range(7):
+            e = bias_dw
+            for a in range(3):
+                if 0 <= i + a - 1 < 7:
+                    for b in range(3):
+                        e = e + taps[3 * a + b] * shifted[b][i + a - 1]
+            phi, gauss = gelu_parts(e)
+            hid_rows.append(e * phi)
+            de = grads[i * 8 : (i + 1) * 8] * (phi + e * gauss)
+            de_rows.append(de)
+            sums[1] = sums[1] + de
+            for a in range(3):
+                if 0 <= i + a - 1 < 7:
+                    for b in range(3):
+                        k = 2 + 3 * a + b
+                        sums[k] = sums[k] + de * shifted[b][i + a - 1]
         zero = jnp.zeros((8, LANES), F32)
-        sums = lax.fori_loop(0, TILES, mix_tile, (zero,) * 11)
-        for k in range(11):
-            gwd[k : k + 1, cols] += jnp.sum(sums[k], axis=0, keepdims=True)
+        hid_ref[rows, local] = jnp.concatenate(hid_rows + [zero], axis=0).astype(BF16)
+        back = [
+            [pltpu.roll(v, 7, 0) for v in de_rows],
+            de_rows,
+            [pltpu.roll(v, 1, 0) for v in de_rows],
+        ]
+        du_rows = []
+        for i in range(7):
+            du = None
+            for a in range(3):
+                if 0 <= i - a + 1 < 7:
+                    for b in range(3):
+                        term = taps[3 * a + b] * back[b][i - a + 1]
+                        du = term if du is None else du + term
+            du_rows.append(du * mask[i * 8 : (i + 1) * 8])
+        du_low = jnp.concatenate(du_rows + [zero], axis=0).astype(BF16)
+        du_ref[rows, local] = du_low
+        sums[0] = sums[0] + row_sums(du_low.astype(F32))
+        return sums
+
+    steps = 3 * hidden // 256
+    even = (u_a, d_a, hid_a, du_a)
+    odd = (u_b, d_b, hid_b, du_b)
+    for piece in feed(0, *even[:2]):
+        piece()
+
+    def slot(step, own, other, ahead):
+        extras = feed(step + 1, *other[:2]) if ahead else []
+        mix(step, *own, extras + drain(jnp.maximum(step - 1, 0), *other[2:]))
+
+    def pair(number, carry):
+        slot(2 * number, even, odd, True)
+        slot(2 * number + 1, odd, even, True)
         return carry
 
-    lax.fori_loop(0, hidden // LANES, mix_lanes, 0)
-    tmp[...] = jnp.dot(hids[...], wdn[...], preferred_element_type=F32)
-    gdn[...] += contract(dms[...], hids[...], 0, 0)
-    gup[...] += contract(h2s[...], dus[...], 0, 0)
-    xs[...] = contract(dus[...], wup[...], 1, 1)
+    lax.fori_loop(0, (steps - 1) // 2, pair, 0)
+    slot(steps - 1, even, odd, False)
+    for piece in drain(steps - 1, *even[2:]):
+        piece()
 
     def middle_rows(big, sums):
         sums = list(sums)
@@ -403,18 +467,18 @@
     def attend_back(t, sums):
         rows = pl.ds(pl.multiple_of(t * 64, 64), 64)
         keys = pl.ds(pl.multiple_of(t * KEYS_TILE, KEYS_TILE), KEYS_TILE)
-        probs = ps[rows, :]
+        probs = ps[pl.ds(pl.multiple_of(t * 80, 16), 80), :]
         upper = dcs[rows, :]
-        dprobs = contract(upper, spread(vs, t), 1, 1)
-        inner = group_all(dprobs * probs, jnp.add)
-        dz = (probs * (dprobs - inner)).astype(BF16)
-        dq = (
-            jnp.dot(dz, spread(ks, t), preferred_element_type=F32) * score_scale
+        dprobs = contract(spread(vs, t), upper, 1, 1)
+        inner = jnp.sum(by_head(dprobs * probs), axis=1, keepdims=True)
+        dz = (by_head(probs) * (by_head(dprobs) - inner)).reshape(probs.shape).astype(BF16)
+        dq = (contract(dz, spread(ks, t), 0, 0) * score_scale).astype(BF16)
+        dqs[rows, :] = dq
+        dk = gather_heads(jnp.dot(dz, qs[rows, :], preferred_element_type=F32)) * score_scale
+        dks[keys, :] = dk.astype(BF16)
+        dv = gather_heads(
+            jnp.dot(probs.astype(BF16), upper, preferred_element_type=F32)
         ).astype(BF16)
-        dqs[rows, :] = dq
-        dk = gather_heads(contract(dz, qs[rows, :], 0, 0)) * score_scale
-        dks[keys, :] = dk.astype(BF16)
-        dv = gather_heads(contract(probs.astype(BF16), upper, 0, 0)).astype(BF16)
         dvs[keys, :] = dv
         return (sums[0] + row_sums(dq.astype(F32)), sums[1] + row_sums(dv.astype(F32)))
 
@@ -465,6 +529,8 @@
 
     @pl.when(g == pl.num_programs(0) - 1)
     def _():
+        for k in range(11):
+            gwd[k : k + 1, :] = jnp.sum(acc[k * 8 : (k + 1) * 8, :], axis=0, keepdims=True)
         rotate(
             order, gq, gk, gv, go, gup, gr, gdn, gsm, gwd, la, ra, lb, rb, wire,
             codes, rows_m, mas, mbs, flat, per_block,
@@ -536,8 +602,8 @@
 
 
 def head_mask(width):
-    row = lax.broadcasted_iota(jnp.int32, (8 * KEYS_TILE, width), 0) >> 4
-    col = lax.broadcasted_iota(jnp.int32, (8 * KEYS_TILE, width), 1) >> 6
+    row = lax.broadcasted_iota(jnp.int32, (HEADS * KEYS_TILE, width), 0) >> 4
+    col = lax.broadcasted_iota(jnp.int32, (HEADS * KEYS_TILE, width), 1) >> 6
     return jnp.where(row == col, 1.0, 0.0).astype(BF16)
 
 
@@ -563,7 +629,7 @@
         ((hidden, width), BF16),
         ((16, hidden), F32),
         ((SLOTS, SLOTS), BF16),
-        ((8 * KEYS_TILE, width), BF16),
+        ((HEADS * KEYS_TILE, width), BF16),
     ]
     scratch += [((width, width), F32)] * 4 + [
         ((width, hidden), F32),
@@ -596,17 +662,24 @@
         ((KEYS, 1), F32),
         (keys, BF16),
         (keys, BF16),
-        ((SLOTS, LANES), F32),
+        ((TILES * HEADS * KEYS_TILE, 64), F32),
         (tall, BF16),
         (tall, F32),
         (tall, F32),
         (tall, F32),
         ((SLOTS, 1), F32),
         (tall, BF16),
-        ((SLOTS, hidden), F32),
-        ((SLOTS, hidden), F32),
-        ((SLOTS, hidden), BF16),
-        ((SLOTS, hidden), BF16),
+        ((3, width, 192), BF16),
+        ((3, width, 192), BF16),
+        ((88, hidden), F32),
+        ((192, 256), F32),
+        ((192, 256), F32),
+        ((192, 256), BF16),
+        ((192, 256), BF16),
+        ((192, 256), F32),
+        ((192, 256), F32),
+        ((192, 256), BF16),
+        ((192, 256), BF16),
         (tall, BF16),
         (tall, BF16),
         (tall, BF16),
@@ -913,19 +986,20 @@
 
 
 def exchange_blocks(wire, first, second, steps, bits):
+    units = wire.shape[1] // 16
+    each = -(-units // 9)
+    rest = list(range(2, bits))
+    orders = ([0] + rest + ["ch", 1], [0, "ch", 1] + rest, [0, 1, "ch"] + rest)
+    plan = []
+    for number, start in enumerate(range(0, units, each)):
+        size = min(each, units - start)
+        plan.append((start * 16, size * 16, orders[number % 3]))
+    return exchange_plan(wire, first, second, steps, bits, plan)
+
+
+def exchange_plan(wire, first, second, steps, bits, plan):
     count, tall, _ = wire.shape
     depth = first.shape[0]
-    units = tall // 16
-    small = max(1, units * 6 // 26)
-    large = (units - small + 1) // 2
-    rest = list(range(2, bits))
-    sizes = (small, large, units - small - large)
-    orders = ([0] + rest + ["ch", 1], [0, "ch", 1] + rest, [0, 1, "ch"] + rest)
-    plan = []
-    start = 0
-    for size, order in zip(sizes, orders):
-        plan.append((start, size * 16, order))
-        start += size * 16
     scratch = []
     for _, size, order in plan:
         for s in range(len(order)):

time: 241 us -> 195 us (0.81)
  Pallas kernels: 235 us -> 189 us
    pallas_call x1, Pallas kernels: 159 us -> 123 us  [run_block(): pl.pallas_call(functools.partial(block_kernel, per=per, per_block=per_blo...]
    pallas_call x1, Pallas kernels: 58.2 us -> 48.4 us  [exchange_plan(): pl.pallas_call(functools.partial(exchange_kernel, plan=plan, bits=bits, d...]
where the time goes in v4:
time: 195 us; the launch traced here: 194 us
  Pallas kernels  189 us (97%)
  local copies, waits for them, and re-layouts  4.63 us (2%)
    pallas_call x1, Pallas kernels, run_block(): pl.pallas_call(functools.partial(block_kernel, per=per, per_block=per_blo...  123 us
    pallas_call x1, Pallas kernels, exchange_plan(): pl.pallas_call(functools.partial(exchange_kernel, plan=plan, bits=bits, d...  48.4 us
    pallas_call x1, Pallas kernels, restore_blocks(): pl.pallas_call(functools.partial(restore_kernel, per_block=per_block), na...  17.6 us

profile of v4, /device:TPU:0, one launch (start us, length us, event | category | flops | bytes accessed | tf_op | source)
XLA Modules:
  0.0 194.5 jit_solution(3877701127158297486)
XLA Ops:
  1.3 1.3 reshape.60.rb
  2.6 1.3 reshape.59.ra
  3.9 122.6 %block_step.1 = (bf16[2,320,1152]{2,1,0:T(8,128)(2,1)}, f32[2,320,1152]{2,1,0:T(8,128)}, bf16[32,416,128]{2,1,0:T(8,128)(2,1)}) custom-call(s32[4,9]{1,0:T(4,128)} %bitcast.21, s32[32]{0:T(128)} %order.3, bf16[2,320,1152]{2,1,0:T(8,128)(2,1)} %bitcast.14, bf16[2,320,1152]{2,1,0:T(8,128)(2,1)} %bitcast.15, f32[320,2560]{1,0:T(8,128)} %ma.3, f32[1280,640]{1,0:T(8,128)} %mb.3, ...), custom_call_target="tpu_custom_call" | custom-call | tf_op jit(solution)/shard_map/block_step/pallas_call | solution.py:698
  126.4 48.4 %exchange.1 = (f32[400,128]{1,0:T(8,128)}, f32[400,128]{1,0:T(8,128)}, f32[400,128]{1,0:T(8,128)}, bf16[2,2,2,2,2,416,128]{6,5,4,3,2,1,0:T(8,128)(2,1)}) custom-call(bf16[2,2,2,2,2,416,128]{6,5,4,3,2,1,0:T(8,128)(2,1)} %bitcast.13, f32[400,128]{1,0:T(8,128)} %bitcast.19, f32[400,128]{1,0:T(8,128)} %bitcast.20, s32[1]{0:T(128)S(6)} %copy.32.steps), custom_call_target="tpu_custom_call" | custom-call | tf_op jit(solution)/shard_map/exchange/pallas_call | solution.py:1011
  174.8 0.0 copy-start.2
  174.9 0.0 copy-start.1
  174.9 0.0 copy-start
  174.9 17.6 %restore.1 = (f32[320,2560]{1,0:T(8,128)}, f32[1280,640]{1,0:T(8,128)}, bf16[320,2560]{1,0:T(8,128)(2,1)}, bf16[1280,640]{1,0:T(8,128)(2,1)}, f32[55,320]{1,0:T(...) custom-call(bf16[32,416,128]{2,1,0:T(8,128)(2,1)} %bitcast.12, s32[32]{0:T(128)} %order.3, ...), custom_call_target="tpu_custom_call" | custom-call | tf_op jit(solution)/shard_map/restore/pallas_call | solution.py:858
  192.4 0.0 copy-done.2
  192.4 0.7 copy.33
  193.1 0.0 copy-done.1
  193.1 0.7 copy.34
  193.8 0.0 copy-done
  193.8 0.7 copy.35
Async XLA Ops:
  174.8 17.6 %copy-start.2 = (f32[400,128]{1,0:T(8,128)S(1)}, f32[400,128]{1,0:T(8,128)}, u32[]{:S(2)}) copy-start(f32[400,128]{1,0:T(8,128)} %get-tuple-element.31) | copy-start | bytes 614404
  174.9 18.3 %copy-start.1 = (f32[400,128]{1,0:T(8,128)S(1)}, f32[400,128]{1,0:T(8,128)}, u32[]{:S(2)}) copy-start(f32[400,128]{1,0:T(8,128)} %get-tuple-element.32) | copy-start | bytes 614404
  174.9 18.9 %copy-start = (f32[400,128]{1,0:T(8,128)S(1)}, f32[400,128]{1,0:T(8,128)}, u32[]{:S(2)}) copy-start(f32[400,128]{1,0:T(8,128)} %get-tuple-element.33) | copy-start | bytes 614404

commit v5 on v4

--- a/solution.py
+++ b/solution.py
@@ -233,7 +233,7 @@
             dms[rows, :] = (grads[c] * mask).astype(BF16)
         return carry
 
-    lax.fori_loop(0, 3, first_norm, 0)
+    lax.fori_loop(0, 3, first_norm, 0, unroll=3)
 
     @pl.when(g == 0)
     def _():
@@ -246,7 +246,12 @@
         wdn[...] = mbs[:, width:].astype(BF16)
 
     qs[...] = (jnp.dot(h1s[...], wq[...], preferred_element_type=F32) + vrow(2)).astype(BF16)
-    pats[...] = jnp.dot(pick[...], hms[...], preferred_element_type=F32).astype(BF16)
+    for t in range(TILES):
+        slots = hms[t * 64 : (t + 1) * 64, :]
+        picked = jnp.dot(pick[...], slots, preferred_element_type=F32).astype(BF16)
+        for d in range(4):
+            spot = d * KEYS + t * KEYS_TILE
+            pats[spot : spot + KEYS_TILE, :] = picked[d * KEYS_TILE : (d + 1) * KEYS_TILE]
     reduced = vrow(4)
     for d in range(4):
         reduced = reduced + jnp.dot(
@@ -280,7 +285,7 @@
         ctxs[rows, :] = contract(probs.astype(BF16), spread(vs, t), 0, 0).astype(BF16)
         return carry
 
-    lax.fori_loop(0, TILES, attend_tile, 0, unroll=3)
+    lax.fori_loop(0, TILES, attend_tile, 0, unroll=9)
     tmp[...] = jnp.dot(ctxs[...], wo[...], preferred_element_type=F32)
 
     def second_norm(t, carry):
@@ -293,7 +298,7 @@
         h2s[rows, :] = (normal * vrow(8) + vrow(9)).astype(BF16)
         return carry
 
-    lax.fori_loop(0, TILES, second_norm, 0, unroll=3)
+    lax.fori_loop(0, TILES, second_norm, 0, unroll=9)
     for r in range(3):
         rows = slice(r * 192, (r + 1) * 192)
         dmt[r] = jnp.transpose(dms[rows, :])
@@ -456,7 +461,7 @@
         orow[pl.ds(base_row + base, 192), :] = join_tiles(outs).astype(BF16)
         return tuple(sums)
 
-    sums = lax.fori_loop(0, 3, middle_rows, (zero_rows,) * 4)
+    sums = lax.fori_loop(0, 3, middle_rows, (zero_rows,) * 4, unroll=3)
     add_small(8, sums[0])
     add_small(9, sums[1])
     add_small(7, sums[2])
@@ -482,7 +487,7 @@
         dvs[keys, :] = dv
         return (sums[0] + row_sums(dq.astype(F32)), sums[1] + row_sums(dv.astype(F32)))
 
-    sums = lax.fori_loop(0, TILES, attend_back, (zero_rows,) * 2, unroll=3)
+    sums = lax.fori_loop(0, TILES, attend_back, (zero_rows,) * 2, unroll=9)
     add_small(2, sums[0])
     add_small(3, sums[1])
     gq[...] += contract(h1s[...], dqs[...], 0, 0)
@@ -499,7 +504,10 @@
         wide_rows = slice(d * width, (d + 1) * width)
         gr[wide_rows, :] += contract(pats[rows, :], ds, 0, 0)
         dps[rows, :] = contract(ds, wr[wide_rows, :], 1, 1).astype(BF16)
-    tmp[...] = contract(pick[...], dps[...], 0, 0)
+    for t in range(TILES):
+        spots = [d * KEYS + t * KEYS_TILE for d in range(4)]
+        picked = jnp.concatenate([dps[spot : spot + KEYS_TILE, :] for spot in spots], axis=0)
+        tmp[t * 64 : (t + 1) * 64, :] = contract(pick[...], picked, 0, 0)
     xs[...] = contract(dqs[...], wq[...], 1, 1)
 
     def last_rows(big, sums):
@@ -516,7 +524,7 @@
         grow[pl.ds(base_row + base, 192), :] = join_tiles(outs)
         return tuple(sums)
 
-    sums = lax.fori_loop(0, 3, last_rows, (zero_rows,) * 2)
+    sums = lax.fori_loop(0, 3, last_rows, (zero_rows,) * 2, unroll=3)
     add_small(0, sums[0])
     add_small(1, sums[1])
 
@@ -590,15 +598,13 @@
 
 
 def pick_matrix():
-    spot = lax.broadcasted_iota(jnp.int32, (SLOTS, SLOTS), 0)
-    lane = lax.broadcasted_iota(jnp.int32, (SLOTS, SLOTS), 1)
-    part = spot // KEYS
-    key = spot - part * KEYS
-    tile = key >> 4
-    inner = key & 15
+    spot = lax.broadcasted_iota(jnp.int32, (64, 64), 0)
+    lane = lax.broadcasted_iota(jnp.int32, (64, 64), 1)
+    part = spot >> 4
+    inner = spot & 15
     row = 2 * (inner >> 2) + (part >> 1)
     col = 2 * (inner & 3) + (part & 1)
-    return jnp.where(tile * 64 + row * TILE + col == lane, 1.0, 0.0).astype(BF16)
+    return jnp.where(row * TILE + col == lane, 1.0, 0.0).astype(BF16)
 
 
 def head_mask(width):
@@ -628,7 +634,7 @@
         ((hidden, width), BF16),
         ((hidden, width), BF16),
         ((16, hidden), F32),
-        ((SLOTS, SLOTS), BF16),
+        ((64, 64), BF16),
         ((HEADS * KEYS_TILE, width), BF16),
     ]
     scratch += [((width, width), F32)] * 4 + [
@@ -694,7 +700,7 @@
     def whole(shape):
         return pl.BlockSpec(shape, lambda g: (0,) * len(shape), pipeline_mode=pl.Buffered(1))
 
-    small = (vector_params, la, ra.reshape(1, -1), lb, rb.reshape(1, -1))
+    small = (vector_params, la, ra.reshape(-1, LANES), lb, rb.reshape(-1, LANES))
     out, gin, wire = pl.pallas_call(
         functools.partial(block_kernel, per=per, per_block=per_block),
         name="block_step",
@@ -729,14 +735,16 @@
 def fill_codes(la, ra, lb, rb, codes, width):
     hidden = lb.shape[1]
     codes[...] = jnp.full(codes.shape, -2, jnp.int32)
+    right_a = jnp.concatenate([ra[j : j + 1, :] for j in range(ra.shape[0])], axis=1)
+    right_b = jnp.concatenate([rb[j : j + 1, :] for j in range(rb.shape[0])], axis=1)
     codes[0:4, 0:width] = la[...]
     codes[4:6, 0:hidden] = lb[...]
     for k, (first, count) in enumerate(SPANS_A):
         start = first * width
         span = count * width
-        codes[6 + k : 7 + k, 0:span] = ra[:, start : start + span] - 2 * start
+        codes[6 + k : 7 + k, 0:span] = right_a[:, start : start + span] - 2 * start
     for k in range(2):
-        codes[10 + k : 11 + k, 0:width] = rb[:, k * width : (k + 1) * width] - 2 * k * width
+        codes[10 + k : 11 + k, 0:width] = right_b[:, k * width : (k + 1) * width] - 2 * k * width
 
 
 def lane_matrix(codes, k, size):
@@ -771,12 +779,16 @@
 
 
 def restore_kernel(
-    blocks, order, la, ra, lb, rb, steps, ma, mb, vp, vf, vsec,
-    na, nb, ca, cb, vg, vfn, vsn, nv,
-    codes, rows_m, das, dbs, flat, wide_s, per_block,
+    blocks, order, la, ra, lb, rb, steps, ma, mb, vp, vf, vsec, owned, first, second,
+    na, nb, ca, cb, vg, vfn, vsn, nv, grad, first_new, second_new,
+    codes, rows_m, das, dbs, flat, wide_s, mas, mbs, cas, cbs, sems, per_block,
 ):
     width = ma.shape[0]
     hidden = mb.shape[0]
+    load_a = pltpu.make_async_copy(ma, mas, sems.at[0])
+    load_b = pltpu.make_async_copy(mb, mbs, sems.at[1])
+    load_a.start()
+    load_b.start()
     fill_codes(la, ra, lb, rb, codes, width)
     count = blocks.shape[0]
     depth = flat.shape[0] // count
@@ -788,32 +800,59 @@
     lax.fori_loop(0, count, place, 0)
     per_row = ma.shape[1] // LANES
     for j in range(per_row):
-        das[:, j * LANES : (j + 1) * LANES] = flat[pl.ds(j, width, stride=per_row), :]
+        cols = slice(j * LANES, (j + 1) * LANES)
+        das[:, cols] = flat[pl.ds(j, width, stride=per_row), :].astype(BF16)
     base = width * per_row
     per_row = mb.shape[1] // LANES
     for j in range(per_row):
-        dbs[:, j * LANES : (j + 1) * LANES] = flat[pl.ds(base + j, hidden, stride=per_row), :]
+        cols = slice(j * LANES, (j + 1) * LANES)
+        dbs[:, cols] = flat[pl.ds(base + j, hidden, stride=per_row), :].astype(BF16)
 
     def dot(left, right):
         return jnp.dot(left, right, preferred_element_type=F32)
 
-    def update(master, step, new, copy, cols):
-        old = master[:, cols]
+    def update(master, step, copy, rows, cols):
+        old = master[rows, cols]
         value = old - matrix_rate * (step + weight_decay * old)
-        new[:, cols] = value
-        copy[:, cols] = value.astype(BF16)
-
-    for k, (first, span) in enumerate(SPANS_A):
+        master[rows, cols] = value
+        copy[rows, cols] = value.astype(BF16)
+
+    stores = []
+
+    def send(source, target, rows):
+        copy = pltpu.make_async_copy(
+            source.at[rows, :], target.at[rows, :], sems.at[2 + len(stores)]
+        )
+        copy.start()
+        stores.append(copy)
+
+    load_a.wait()
+    for k, (start, span) in enumerate(SPANS_A):
         size = span * width
-        cols = slice(first * width, first * width + size)
-        part = dot(lane_matrix(codes, k, width), das[:, cols].astype(BF16)).astype(BF16)
+        cols = slice(start * width, start * width + size)
+        part = dot(lane_matrix(codes, k, width), das[:, cols]).astype(BF16)
         row_matrix(codes, 6 + k, rows_m, size)
-        update(ma, dot(part, rows_m[0:size, 0:size]), na, ca, cols)
+        update(mas, dot(part, rows_m[0:size, 0:size]), cas, slice(None), cols)
+    send(mas, na, slice(0, width))
+    send(cas, ca, slice(0, width))
+    parts = []
     for k in range(2):
         cols = slice(k * width, (k + 1) * width)
-        part = dot(lane_matrix(codes, 4 + k, hidden), dbs[:, cols].astype(BF16)).astype(BF16)
-        row_matrix(codes, 10 + k, rows_m, width)
-        update(mb, dot(part, rows_m[0:width, 0:width]), nb, cb, cols)
+        parts.append(dot(lane_matrix(codes, 4 + k, hidden), dbs[:, cols]).astype(BF16))
+        row_matrix(codes, 10 + k, rows_m.at[k * 512 : k * 512 + 512, :], width)
+    load_b.wait()
+    for c in range(hidden // width):
+        rows = slice(c * width, (c + 1) * width)
+        for k in range(2):
+            right = rows_m[k * 512 : k * 512 + width, 0:width]
+            cols = slice(k * width, (k + 1) * width)
+            update(mbs, dot(parts[k][rows], right), cbs, rows, cols)
+        send(mbs, nb, rows)
+        send(cbs, cb, rows)
+    total = owned[...]
+    grad[...] = total
+    first_new[...] = beta_one * first[...] + (1.0 - beta_one) * total
+    second_new[...] = beta_two * second[...] + (1.0 - beta_two) * total * total
     for number, (kind, k, col, size) in enumerate(vector_spots(width, hidden)):
         block, row = number // per_block, depth + number % per_block
         value = blocks[block, row : row + 1, 0:size].astype(F32)
@@ -834,6 +873,8 @@
     move = direction_of(first_new, second_new, steps[0])
     old = vp[...]
     nv[...] = old - vector_rate * (move + weight_decay * old)
+    for copy in stores:
+        copy.wait()
 
 
 def direction_of(first_new, second_new, steps):
@@ -849,37 +890,53 @@
     return pl.BlockSpec(memory_space=pltpu.VMEM)
 
 
-def restore_blocks(blocks, order, la, ra, lb, rb, steps, ma, mb, vp, vf, vsec):
+def restore_blocks(
+    blocks, order, la, ra, lb, rb, steps, ma, mb, vp, vf, vsec, owned, first, second
+):
     width = ma.shape[0]
     hidden = mb.shape[0]
     per_block = -(-VECTOR_ROWS // blocks.shape[0])
     total = (ma.size + mb.size) // LANES
     smem = pl.BlockSpec(memory_space=pltpu.SMEM)
+    anywhere = pl.BlockSpec(memory_space=pl.ANY)
     return pl.pallas_call(
         functools.partial(restore_kernel, per_block=per_block),
         name="restore",
-        in_specs=[vmem_spec(), smem] + [vmem_spec()] * 4 + [smem] + [vmem_spec()] * 5,
-        out_specs=[vmem_spec()] * 8,
+        in_specs=[vmem_spec(), smem]
+        + [vmem_spec()] * 4
+        + [smem]
+        + [anywhere] * 2
+        + [vmem_spec()] * 6,
+        out_specs=[anywhere] * 4 + [vmem_spec()] * 7,
         out_shape=[
             jax.ShapeDtypeStruct(ma.shape, F32),
             jax.ShapeDtypeStruct(mb.shape, F32),
             jax.ShapeDtypeStruct(ma.shape, BF16),
             jax.ShapeDtypeStruct(mb.shape, BF16),
         ]
-        + [jax.ShapeDtypeStruct(vp.shape, F32)] * 4,
+        + [jax.ShapeDtypeStruct(vp.shape, F32)] * 4
+        + [jax.ShapeDtypeStruct(owned.shape, F32)] * 3,
         scratch_shapes=[
             pltpu.VMEM((16, hidden), jnp.int32),
             pltpu.VMEM((hidden, hidden), BF16),
-            pltpu.VMEM((width, 8 * width), F32),
-            pltpu.VMEM((hidden, 2 * width), F32),
+            pltpu.VMEM(ma.shape, BF16),
+            pltpu.VMEM(mb.shape, BF16),
             pltpu.VMEM((total, LANES), F32),
             pltpu.VMEM((16, hidden), F32),
+            pltpu.VMEM(ma.shape, F32),
+            pltpu.VMEM(mb.shape, F32),
+            pltpu.VMEM(ma.shape, BF16),
+            pltpu.VMEM(mb.shape, BF16),
+            pltpu.SemaphoreType.DMA((4 + 2 * (hidden // width),)),
         ],
         compiler_params=pltpu.CompilerParams(vmem_limit_bytes=60 << 20),
-    )(blocks, order, la, ra.reshape(1, -1), lb, rb.reshape(1, -1), steps, ma, mb, vp, vf, vsec)
-
-
-def exchange_kernel(wire, first, second, steps, grad, first_new, second_new, every, *scratch,
+    )(
+        blocks, order, la, ra.reshape(-1, LANES), lb, rb.reshape(-1, LANES), steps,
+        ma, mb, vp, vf, vsec, owned, first, second,
+    )
+
+
+def exchange_kernel(wire, first, second, steps, grad, every, *scratch,
                     plan, bits, depth):
     buffers = []
     spot = 0
@@ -967,8 +1024,6 @@
                 grad[rows, :] = owned
                 one = beta_one * first[rows, :] + (1.0 - beta_one) * owned
                 two = beta_two * second[rows, :] + (1.0 - beta_two) * owned * owned
-                first_new[rows, :] = one
-                second_new[rows, :] = two
                 parts.append(direction_of(one, two, steps[0]))
             if count < size:
                 parts.append(total[count:])
@@ -1008,18 +1063,18 @@
         scratch.append(pltpu.SemaphoreType.DMA((len(plan), bits + 1)))
     shape = (2,) * (bits + 1) + (tall, LANES)
     block = jax.ShapeDtypeStruct((depth, LANES), F32)
-    grad, first_new, second_new, every = pl.pallas_call(
+    grad, every = pl.pallas_call(
         functools.partial(exchange_kernel, plan=plan, bits=bits, depth=depth),
         name="exchange",
         in_specs=[vmem_spec()] * 3 + [pl.BlockSpec(memory_space=pltpu.SMEM)],
-        out_specs=[vmem_spec()] * 4,
-        out_shape=[block, block, block, jax.ShapeDtypeStruct(shape, BF16)],
+        out_specs=[vmem_spec()] * 2,
+        out_shape=[block, jax.ShapeDtypeStruct(shape, BF16)],
         scratch_shapes=scratch,
         compiler_params=pltpu.CompilerParams(
             vmem_limit_bytes=60 << 20, collective_id=0, has_side_effects=True
         ),
     )(wire.reshape(shape), first, second, steps)
-    return grad, first_new, second_new, every.reshape(wire.shape)
+    return grad, every.reshape(wire.shape)
 
 
 def on_device(
@@ -1032,12 +1087,12 @@
         left_a, right_a, left_b, right_b,
     )
     shape = matrix_first.shape
-    grad, first_new, second_new, every = exchange_blocks(
-        wire, matrix_first.reshape(-1, LANES), matrix_second.reshape(-1, LANES), step_count, bits
-    )
-    restored = restore_blocks(
-        every, owner_list, left_a, right_a, left_b, right_b, step_count,
-        master_a, master_b, vector_params, vector_first, vector_second,
+    first = matrix_first.reshape(-1, LANES)
+    second = matrix_second.reshape(-1, LANES)
+    owned, every = exchange_blocks(wire, first, second, step_count, bits)
+    *restored, grad, first_new, second_new = restore_blocks(
+        every, owner_list, left_a, right_a, left_b, right_b, step_count, master_a, master_b,
+        vector_params, vector_first, vector_second, owned, first, second,
     )
     return (
         out,

time: 195 us -> 178 us (0.913)
  Pallas kernels: 189 us -> 177 us
  local copies, waits for them, and re-layouts: 4.63 us -> 0 us
    pallas_call x1, Pallas kernels: 123 us -> 113 us  [run_block(): pl.pallas_call(functools.partial(block_kernel, per=per, per_block=per_blo...]
    reshape x2 -> x0, local copies, waits for them, and re-layouts: 2.58 us -> none  [run_block(): small = (vector_params, la, ra.reshape(1, -1), lb, rb.reshape(1, -1))]
    unnamed x9 -> x0, local copies, waits for them, and re-layouts: 2.06 us -> none
where the time goes in v5:
time: 178 us
  Pallas kernels  177 us (99%)
    pallas_call x1, Pallas kernels, run_block(): pl.pallas_call(functools.partial(block_kernel, per=per, per_block=per_blo...  113 us
    pallas_call x1, Pallas kernels, exchange_plan(): pl.pallas_call(functools.partial(exchange_kernel, plan=plan, bits=bits, d...  48.3 us
    pallas_call x1, Pallas kernels, restore_blocks(): pl.pallas_call(functools.partial(restore_kernel, per_block=per_block), na...  15.9 us

profile of v5, /device:TPU:0, one launch (start us, length us, event | category | flops | bytes accessed | tf_op | source)
XLA Modules:
  0.0 178.2 jit_solution(16192436351626249254)
XLA Ops:
  1.3 112.6 %block_step.1 = (bf16[2,320,1152]{2,1,0:T(8,128)(2,1)}, f32[2,320,1152]{2,1,0:T(8,128)}, bf16[32,416,128]{2,1,0:T(8,128)(2,1)}) custom-call(s32[4,9]{1,0:T(4,128)} %bitcast.26, s32[32]{0:T(128)} %order.3, bf16[2,320,1152]{2,1,0:T(8,128)(2,1)} %bitcast.16, bf16[2,320,1152]{2,1,0:T(8,128)(2,1)} %bitcast.17, f32[320,2560]{1,0:T(8,128)} %ma.3, f32[1280,640]{1,0:T(8,128)} %mb.3, ...), custom_call_target="tpu_custom_call" | custom-call | tf_op jit(solution)/shard_map/block_step/pallas_call | solution.py:704
  113.9 48.3 %exchange.1 = (f32[400,128]{1,0:T(8,128)}, bf16[2,2,2,2,2,416,128]{6,5,4,3,2,1,0:T(8,128)(2,1)}) custom-call(bf16[2,2,2,2,2,416,128]{6,5,4,3,2,1,0:T(8,128)(2,1)} %bitcast.14, f32[400,128]{1,0:T(8,128)} %bitcast.18, f32[400,128]{1,0:T(8,128)} %bitcast.20, s32[1]{0:T(128)S(6)} %copy.29.steps), custom_call_target="tpu_custom_call" | custom-call | tf_op jit(solution)/shard_map/exchange/pallas_call | solution.py:1066
  162.2 15.9 %restore.1 = (f32[320,2560]{1,0:T(8,128)}, f32[1280,640]{1,0:T(8,128)}, bf16[320,2560]{1,0:T(8,128)(2,1)}, bf16[1280,640]{1,0:T(8,128)(2,1)}, f32[55,320]{1,0:T(...) custom-call(bf16[32,416,128]{2,1,0:T(8,128)(2,1)} %bitcast.15, ...), custom_call_target="tpu_custom_call" | custom-call | tf_op jit(solution)/shard_map/restore/pallas_call | solution.py:902

commit v6 on v5

--- a/solution.py
+++ b/solution.py
@@ -130,6 +130,7 @@
     grow,
     codes,
     rows_m,
+    rbt,
     flat,
     msk,
     xs,
@@ -162,6 +163,10 @@
     d_b,
     hid_b,
     du_b,
+    u_c,
+    d_c,
+    hid_c,
+    du_c,
     dms,
     das,
     dcs,
@@ -177,6 +182,7 @@
     part = lax.rem(g, per)
     width = x_ref.shape[1]
     hidden = wup.shape[1]
+    wider = wup.shape[0]
     spans = x_ref.shape[2] // LANES
     base_row = part * SLOTS
     load_a = pltpu.make_async_copy(ma, mas, sems.at[0])
@@ -240,7 +246,11 @@
         load_a.wait()
         for k, ref in enumerate((wq, wk, wv, wo)):
             ref[...] = mas[:, k * width : (k + 1) * width].astype(BF16)
-        wup[...] = mas[:, 4 * width :].astype(BF16)
+        wup[0:width, :] = mas[:, 4 * width :].astype(BF16)
+        bias = wide[0:1, :]
+        high = bias.astype(BF16).astype(F32)
+        empty = jnp.zeros((wider - width - 2, hidden), F32)
+        wup[width:wider, :] = jnp.concatenate([high, bias - high, empty], axis=0).astype(BF16)
         load_b.wait()
         wr[...] = mbs[:, :width].astype(BF16)
         wdn[...] = mbs[:, width:].astype(BF16)
@@ -249,16 +259,10 @@
     for t in range(TILES):
         slots = hms[t * 64 : (t + 1) * 64, :]
         picked = jnp.dot(pick[...], slots, preferred_element_type=F32).astype(BF16)
-        for d in range(4):
-            spot = d * KEYS + t * KEYS_TILE
-            pats[spot : spot + KEYS_TILE, :] = picked[d * KEYS_TILE : (d + 1) * KEYS_TILE]
-    reduced = vrow(4)
-    for d in range(4):
-        reduced = reduced + jnp.dot(
-            pats[d * KEYS : (d + 1) * KEYS, :],
-            wr[d * width : (d + 1) * width, :],
-            preferred_element_type=F32,
+        pats[t * KEYS_TILE : (t + 1) * KEYS_TILE, :] = jnp.concatenate(
+            [picked[d * KEYS_TILE : (d + 1) * KEYS_TILE] for d in range(4)], axis=1
         )
+    reduced = jnp.dot(pats[...], wr[...], preferred_element_type=F32) + vrow(4)
     normal, inverse = normalize(reduced)
     nks[...] = normal
     rks[...] = inverse
@@ -295,7 +299,11 @@
         normal, inverse = normalize(middle)
         n2s[rows, :] = normal
         r2s[rows, :] = inverse
-        h2s[rows, :] = (normal * vrow(8) + vrow(9)).astype(BF16)
+        mask = msk[rows, :]
+        h2s[rows, 0:width] = ((normal * vrow(8) + vrow(9)) * mask).astype(BF16)
+        lane = lax.broadcasted_iota(jnp.int32, (64, wider - width), 1)
+        flag = jnp.where(lane < 2, mask[:, 0 : wider - width], 0.0)
+        h2s[rows, width:wider] = flag.astype(BF16)
         return carry
 
     lax.fori_loop(0, TILES, second_norm, 0, unroll=9)
@@ -305,18 +313,15 @@
         h2t[r] = jnp.transpose(h2s[rows, :])
     for ref in (tmp, xs):
         ref[...] = jnp.zeros(ref.shape, F32)
-    for ref in (hid_b, du_b):
+    for ref in (hid_c, du_c):
         ref[...] = jnp.zeros(ref.shape, BF16)
 
-    def spots(step):
-        group = lax.div(step, 3)
-        big = step - group * 3
-        return big, pl.ds(pl.multiple_of(big * 192, 64), 192), pl.ds(
-            pl.multiple_of(group * 256, 256), 256
-        )
-
-    def feed(step, u_ref, d_ref):
-        big, rows, cols = spots(step)
+    def columns(group):
+        return pl.ds(pl.multiple_of(group * 256, 256), 256)
+
+    def feed(group, big, u_ref, d_ref):
+        rows = slice(big * 192, (big + 1) * 192)
+        cols = columns(group)
 
         def up():
             u_ref[...] = jnp.dot(h2s[rows, :], wup[:, cols], preferred_element_type=F32)
@@ -326,14 +331,15 @@
 
         return [up, down]
 
-    def drain(step, hid_ref, du_ref):
-        big, rows, cols = spots(step)
+    def drain(group, big, hid_ref, du_ref):
+        rows = slice(big * 192, (big + 1) * 192)
+        cols = columns(group)
 
         def one():
             tmp[rows, :] += jnp.dot(hid_ref[...], wdn[cols, :], preferred_element_type=F32)
 
         def two():
-            xs[rows, :] += contract(du_ref[...], wup[:, cols], 1, 1)
+            xs[rows, :] += contract(du_ref[...], wup[0:width, cols], 1, 1)
 
         def three():
             gdn[:, cols] += jnp.dot(dmt[big], hid_ref[...], preferred_element_type=F32)
@@ -343,36 +349,33 @@
 
         return [one, two, three, four]
 
-    def mix(step, u_ref, d_ref, hid_ref, du_ref, extras):
-        big = lax.rem(step, 3)
+    def mix(group, u_ref, d_ref, hid_ref, du_ref, extras):
         extras = list(extras)
         for lane in range(2):
             local = slice(lane * LANES, (lane + 1) * LANES)
             cols = pl.ds(
-                pl.multiple_of(lax.div(step, 3) * 256 + lane * LANES, LANES), LANES
+                pl.multiple_of(group * 256 + lane * LANES, LANES), LANES
             )
-            bias_up = wide[0:1, cols]
             bias_dw = wide[1:2, cols]
             taps = [wide[2 + k : 3 + k, cols] for k in range(9)]
-            sums = [jnp.zeros((8, LANES), F32)] * 11
+            sums = [None] + [jnp.zeros((8, LANES), F32)] * 10
             for c in range(3):
                 rows = slice(c * 64, (c + 1) * 64)
-                mask = msk[pl.ds(pl.multiple_of(big * 192 + c * 64, 64), 64), 0:LANES]
                 sums = mix_unit(
-                    u_ref, d_ref, hid_ref, du_ref, rows, local, mask, bias_up, bias_dw, taps, sums
+                    u_ref, d_ref, hid_ref, du_ref, rows, local, bias_dw, taps, sums
                 )
                 if extras:
                     extras.pop(0)()
-            for k in range(11):
+            for k in range(1, 11):
                 acc[k * 8 : (k + 1) * 8, cols] += sums[k]
         for extra in extras:
             extra()
 
     def mix_unit(
-        u_ref, d_ref, hid_ref, du_ref, rows, local, mask, bias_up, bias_dw, taps, sums
+        u_ref, d_ref, hid_ref, du_ref, rows, local, bias_dw, taps, sums
     ):
         sums = list(sums)
-        ups = (u_ref[rows, local] + bias_up) * mask
+        ups = u_ref[rows, local]
         mid = [ups[i * 8 : (i + 1) * 8] for i in range(7)]
         shifted = [
             [pltpu.roll(v, 1, 0) for v in mid],
@@ -413,30 +416,33 @@
                     for b in range(3):
                         term = taps[3 * a + b] * back[b][i - a + 1]
                         du = term if du is None else du + term
-            du_rows.append(du * mask[i * 8 : (i + 1) * 8])
+            du_rows.append(du)
         du_low = jnp.concatenate(du_rows + [zero], axis=0).astype(BF16)
         du_ref[rows, local] = du_low
-        sums[0] = sums[0] + row_sums(du_low.astype(F32))
         return sums
 
-    steps = 3 * hidden // 256
-    even = (u_a, d_a, hid_a, du_a)
-    odd = (u_b, d_b, hid_b, du_b)
-    for piece in feed(0, *even[:2]):
-        piece()
-
-    def slot(step, own, other, ahead):
-        extras = feed(step + 1, *other[:2]) if ahead else []
-        mix(step, *own, extras + drain(jnp.maximum(step - 1, 0), *other[2:]))
-
-    def pair(number, carry):
-        slot(2 * number, even, odd, True)
-        slot(2 * number + 1, odd, even, True)
+    sets = (
+        (u_a, d_a, hid_a, du_a),
+        (u_b, d_b, hid_b, du_b),
+        (u_c, d_c, hid_c, du_c),
+    )
+    groups = hidden // 256
+    for big in range(2):
+        for piece in feed(0, big, *sets[big][:2]):
+            piece()
+
+    def group_step(group, carry):
+        after = jnp.minimum(group + 1, groups - 1)
+        before = jnp.maximum(group - 1, 0)
+        plans = ((group, 2, before, 2), (after, 0, group, 0), (after, 1, group, 1))
+        for big, (feed_group, feed_big, drain_group, drain_big) in enumerate(plans):
+            extras = drain(drain_group, drain_big, *sets[drain_big][2:])
+            later = feed(feed_group, feed_big, *sets[feed_big][:2])
+            mix(group, *sets[big], extras + later)
         return carry
 
-    lax.fori_loop(0, (steps - 1) // 2, pair, 0)
-    slot(steps - 1, even, odd, False)
-    for piece in drain(steps - 1, *even[2:]):
+    lax.fori_loop(0, groups, group_step, 0)
+    for piece in drain(groups - 1, 2, *sets[2][2:]):
         piece()
 
     def middle_rows(big, sums):
@@ -448,7 +454,7 @@
             rows = pl.ds(base + c * 64, 64)
             mask = msk[rows, :]
             outs.append(m1s[rows, :] + mask * (tmp[rows, :] + vrow(10)))
-            dout = xs[rows, :]
+            dout = xs[rows, :] * mask
             normal = n2s[rows, :]
             dmid = grads[c] + norm_back(dout, normal, r2s[rows, :], vrow(8))
             m1s[rows, :] = dmid
@@ -499,14 +505,13 @@
     add_small(5, row_sums(dout * normal))
     add_small(6, row_sums(dout))
     add_small(4, row_sums(ds.astype(F32)))
-    for d in range(4):
-        rows = slice(d * KEYS, (d + 1) * KEYS)
-        wide_rows = slice(d * width, (d + 1) * width)
-        gr[wide_rows, :] += contract(pats[rows, :], ds, 0, 0)
-        dps[rows, :] = contract(ds, wr[wide_rows, :], 1, 1).astype(BF16)
+    gr[...] += contract(ds, pats[...], 0, 0)
+    dps[...] = contract(ds, wr[...], 1, 1).astype(BF16)
     for t in range(TILES):
-        spots = [d * KEYS + t * KEYS_TILE for d in range(4)]
-        picked = jnp.concatenate([dps[spot : spot + KEYS_TILE, :] for spot in spots], axis=0)
+        back_rows = dps[t * KEYS_TILE : (t + 1) * KEYS_TILE, :]
+        picked = jnp.concatenate(
+            [back_rows[:, d * width : (d + 1) * width] for d in range(4)], axis=0
+        )
         tmp[t * 64 : (t + 1) * 64, :] = contract(pick[...], picked, 0, 0)
     xs[...] = contract(dqs[...], wq[...], 1, 1)
 
@@ -537,25 +542,26 @@
 
     @pl.when(g == pl.num_programs(0) - 1)
     def _():
-        for k in range(11):
+        gwd[0:1, :] = gup[width : width + 1, :]
+        for k in range(1, 11):
             gwd[k : k + 1, :] = jnp.sum(acc[k * 8 : (k + 1) * 8, :], axis=0, keepdims=True)
         rotate(
             order, gq, gk, gv, go, gup, gr, gdn, gsm, gwd, la, ra, lb, rb, wire,
-            codes, rows_m, mas, mbs, flat, per_block,
+            codes, rows_m, mas, rbt, flat, per_block,
         )
 
 
 def rotate(
     order, gq, gk, gv, go, gup, gr, gdn, gsm, gwd, la, ra, lb, rb, wire,
-    codes, rows_m, ras, rbs, flat, per_block,
+    codes, rows_m, ras, rbt, flat, per_block,
 ):
-    width, hidden = gup.shape
+    width, hidden = gq.shape[0], gup.shape[1]
     fill_codes(la, ra, lb, rb, codes, width)
 
     def dot(left, right):
         return jnp.dot(left, right, preferred_element_type=F32)
 
-    for k, parts in enumerate(((gq,), (gk, gv), (go,), (gup,))):
+    for k, parts in enumerate(((gq,), (gk, gv), (go,), (gup.at[0:width],))):
         first, count = SPANS_A[k]
         right = lane_matrix(codes, 6 + k, count * width)
         total = None
@@ -565,20 +571,25 @@
             total = piece if total is None else total + piece
         row_matrix(codes, k, rows_m, width)
         ras[:, first * width : (first + count) * width] = dot(rows_m[0:width, 0:width], total.astype(BF16))
-    row_matrix(codes, 4, rows_m, hidden)
-    part = dot(rows_m[...], gr[...].astype(BF16)).astype(BF16)
-    rbs[:, 0:width] = dot(part, lane_matrix(codes, 10, width))
-    row_matrix(codes, 5, rows_m, hidden)
-    part = contract(rows_m[...], gdn[...].astype(BF16), 1, 1).astype(BF16)
-    rbs[:, width : 2 * width] = dot(part, lane_matrix(codes, 11, width))
+    for k, grad in enumerate((gr, gdn)):
+        row_matrix(codes, 10 + k, rows_m, width)
+        right = rows_m[0:width, 0:width]
+        part = dot(right, grad[...].astype(BF16)).astype(BF16)
+        rbt[k * width : (k + 1) * width, :] = dot(part, lane_matrix(codes, 4 + k, hidden))
     count, tall, _ = wire.shape
     half = count // 2
     depth = 2 * flat.shape[0] // count
-    for first, (source, rows) in enumerate(((ras, width), (rbs, hidden))):
-        per_row = source.shape[1] // LANES
-        for j in range(per_row):
-            cols = slice(j * LANES, (j + 1) * LANES)
-            flat[pl.ds(j, rows, stride=per_row), :] = source[:, cols]
+    for first in range(2):
+        if first == 0:
+            per_row = ras.shape[1] // LANES
+            for j in range(per_row):
+                cols = slice(j * LANES, (j + 1) * LANES)
+                flat[pl.ds(j, width, stride=per_row), :] = ras[:, cols]
+        else:
+            per_row = rbt.shape[0] // LANES
+            for j in range(per_row):
+                rows = slice(j * LANES, (j + 1) * LANES)
+                flat[pl.ds(j, hidden, stride=per_row), :] = jnp.transpose(rbt[rows, :])
 
         def place(t, carry, first=first):
             spot = order[t] - first * half
@@ -630,7 +641,7 @@
     tall = (SLOTS, width)
     keys = (KEYS, width)
     scratch = [((width, width), BF16)] * 4 + [
-        ((width, hidden), BF16),
+        ((width + 16, hidden), BF16),
         ((hidden, width), BF16),
         ((hidden, width), BF16),
         ((16, hidden), F32),
@@ -638,8 +649,8 @@
         ((HEADS * KEYS_TILE, width), BF16),
     ]
     scratch += [((width, width), F32)] * 4 + [
+        ((width + 16, hidden), F32),
         ((width, hidden), F32),
-        ((hidden, width), F32),
         ((width, hidden), F32),
         ((16, width), F32),
         ((16, hidden), F32),
@@ -652,6 +663,7 @@
         ((rows, width), F32),
         ((16, hidden), jnp.int32),
         ((hidden, hidden), BF16),
+        ((2 * width, hidden), F32),
         ((total // 2, LANES), F32),
     ]
     scratch += [
@@ -662,7 +674,7 @@
         (tall, BF16),
         (tall, BF16),
         (tall, BF16),
-        (tall, BF16),
+        ((KEYS, hidden), BF16),
         (keys, BF16),
         (keys, F32),
         ((KEYS, 1), F32),
@@ -674,10 +686,14 @@
         (tall, F32),
         (tall, F32),
         ((SLOTS, 1), F32),
-        (tall, BF16),
+        ((SLOTS, width + 16), BF16),
         ((3, width, 192), BF16),
-        ((3, width, 192), BF16),
+        ((3, width + 16, 192), BF16),
         ((88, hidden), F32),
+        ((192, 256), F32),
+        ((192, 256), F32),
+        ((192, 256), BF16),
+        ((192, 256), BF16),
         ((192, 256), F32),
         ((192, 256), F32),
         ((192, 256), BF16),
@@ -692,7 +708,7 @@
         (tall, BF16),
         (keys, BF16),
         (keys, BF16),
-        (tall, BF16),
+        ((KEYS, hidden), BF16),
     ]
     smem = pl.BlockSpec(memory_space=pltpu.SMEM)
     anywhere = pl.BlockSpec(memory_space=pl.ANY)
@@ -781,7 +797,7 @@
 def restore_kernel(
     blocks, order, la, ra, lb, rb, steps, ma, mb, vp, vf, vsec, owned, first, second,
     na, nb, ca, cb, vg, vfn, vsn, nv, grad, first_new, second_new,
-    codes, rows_m, das, dbs, flat, wide_s, mas, mbs, cas, cbs, sems, per_block,
+    codes, rows_m, das, dbs, flat, wide_s, mas, mbs, cas, cbs, sbt, sems, per_block,
 ):
     width = ma.shape[0]
     hidden = mb.shape[0]
@@ -805,8 +821,8 @@
     base = width * per_row
     per_row = mb.shape[1] // LANES
     for j in range(per_row):
-        cols = slice(j * LANES, (j + 1) * LANES)
-        dbs[:, cols] = flat[pl.ds(base + j, hidden, stride=per_row), :].astype(BF16)
+        rows = slice(j * LANES, (j + 1) * LANES)
+        dbs[rows, :] = jnp.transpose(flat[pl.ds(base + j, hidden, stride=per_row), :]).astype(BF16)
 
     def dot(left, right):
         return jnp.dot(left, right, preferred_element_type=F32)
@@ -835,18 +851,17 @@
         update(mas, dot(part, rows_m[0:size, 0:size]), cas, slice(None), cols)
     send(mas, na, slice(0, width))
     send(cas, ca, slice(0, width))
-    parts = []
     for k in range(2):
-        cols = slice(k * width, (k + 1) * width)
-        parts.append(dot(lane_matrix(codes, 4 + k, hidden), dbs[:, cols]).astype(BF16))
-        row_matrix(codes, 10 + k, rows_m.at[k * 512 : k * 512 + 512, :], width)
+        rows = slice(k * width, (k + 1) * width)
+        part = dot(lane_matrix(codes, 10 + k, width), dbs[rows, :]).astype(BF16)
+        row_matrix(codes, 4 + k, rows_m, hidden)
+        sbt[rows, :] = dot(part, rows_m[...])
     load_b.wait()
-    for c in range(hidden // width):
-        rows = slice(c * width, (c + 1) * width)
-        for k in range(2):
-            right = rows_m[k * 512 : k * 512 + width, 0:width]
-            cols = slice(k * width, (k + 1) * width)
-            update(mbs, dot(parts[k][rows], right), cbs, rows, cols)
+    for c in range(hidden // 256):
+        rows = slice(c * 256, (c + 1) * 256)
+        for j in range(per_row):
+            cols = slice(j * LANES, (j + 1) * LANES)
+            update(mbs, jnp.transpose(sbt[cols, rows]), cbs, rows, cols)
         send(mbs, nb, rows)
         send(cbs, cb, rows)
     total = owned[...]
@@ -920,14 +935,15 @@
             pltpu.VMEM((16, hidden), jnp.int32),
             pltpu.VMEM((hidden, hidden), BF16),
             pltpu.VMEM(ma.shape, BF16),
-            pltpu.VMEM(mb.shape, BF16),
+            pltpu.VMEM((2 * width, hidden), BF16),
             pltpu.VMEM((total, LANES), F32),
             pltpu.VMEM((16, hidden), F32),
             pltpu.VMEM(ma.shape, F32),
             pltpu.VMEM(mb.shape, F32),
             pltpu.VMEM(ma.shape, BF16),
             pltpu.VMEM(mb.shape, BF16),
-            pltpu.SemaphoreType.DMA((4 + 2 * (hidden // width),)),
+            pltpu.VMEM((2 * width, hidden), F32),
+            pltpu.SemaphoreType.DMA((4 + 2 * (hidden // 256),)),
         ],
         compiler_params=pltpu.CompilerParams(vmem_limit_bytes=60 << 20),
     )(
@@ -943,7 +959,8 @@
     for _, _, order in plan:
         buffers.append(scratch[spot : spot + len(order)])
         spot += len(order)
-    rs_send, rs_recv, ag_send, ag_recv = scratch[spot:]
+    keeps = scratch[spot : spot + len(plan)]
+    rs_send, rs_recv, ag_send, ag_recv, local_sem = scratch[spot + len(plan) :]
     tok = lax.axis_index("tok")
     side = lax.axis_index("ch")
 
@@ -956,6 +973,14 @@
         return {"tok": tok + 2**axis - 2 ** (axis + 1) * mine(axis)}
 
     axes = [*reversed(range(bits)), "ch"]
+    loads = []
+    for c, (start, size, order) in enumerate(plan):
+        index = tuple(mine(a) if a == order[0] else slice(None) for a in axes)
+        copy = pltpu.make_async_copy(
+            wire.at[index + (pl.ds(start, size), slice(None))], keeps[c], local_sem.at[c]
+        )
+        copy.start()
+        loads.append(copy)
     barrier = pltpu.get_barrier_semaphore()
     for axis in axes:
         pl.semaphore_signal(barrier, inc=1, device_id=peer(axis), device_id_type=pl.DeviceIdType.MESH)
@@ -984,6 +1009,9 @@
         return copy
 
     def scatter_keep(c, s):
+        if s == 0:
+            loads[c].wait()
+            return keeps[c][...]
         axis = plan[c][2][s]
         return held[c][region(c, lambda a: mine(a) if a == axis else slice(None))]
 
@@ -1059,14 +1087,19 @@
     for _, size, order in plan:
         for s in range(len(order)):
             scratch.append(pltpu.VMEM((2,) * (len(order) - 1 - s) + (size, LANES), BF16))
+    for _, size, order in plan:
+        scratch.append(pltpu.VMEM((2,) * (len(order) - 1) + (size, LANES), BF16))
     for _ in range(4):
         scratch.append(pltpu.SemaphoreType.DMA((len(plan), bits + 1)))
+    scratch.append(pltpu.SemaphoreType.DMA((len(plan),)))
     shape = (2,) * (bits + 1) + (tall, LANES)
     block = jax.ShapeDtypeStruct((depth, LANES), F32)
     grad, every = pl.pallas_call(
         functools.partial(exchange_kernel, plan=plan, bits=bits, depth=depth),
         name="exchange",
-        in_specs=[vmem_spec()] * 3 + [pl.BlockSpec(memory_space=pltpu.SMEM)],
+        in_specs=[pl.BlockSpec(memory_space=pl.ANY)]
+        + [vmem_spec()] * 2
+        + [pl.BlockSpec(memory_space=pltpu.SMEM)],
         out_specs=[vmem_spec()] * 2,
         out_shape=[block, jax.ShapeDtypeStruct(shape, BF16)],
         scratch_shapes=scratch,

time: 178 us -> 173 us (0.972)
  Pallas kernels: 177 us -> 171 us
    pallas_call x1, Pallas kernels: 113 us -> 108 us  [run_block(): pl.pallas_call(functools.partial(block_kernel, per=per, per_block=per_blo...]
where the time goes in v6:
time: 173 us
  Pallas kernels  171 us (99%)
    pallas_call x1, Pallas kernels, run_block(): pl.pallas_call(functools.partial(block_kernel, per=per, per_block=per_blo...  108 us
    pallas_call x1, Pallas kernels, exchange_plan(): pl.pallas_call(functools.partial(exchange_kernel, plan=plan, bits=bits, d...  47.6 us
    pallas_call x1, Pallas kernels, restore_blocks(): pl.pallas_call(functools.partial(restore_kernel, per_block=per_block), na...  15.9 us

profile of v6, /device:TPU:0, one launch (start us, length us, event | category | flops | bytes accessed | tf_op | source)
XLA Modules:
  0.0 172.7 jit_solution(4755297287522195741)
XLA Ops:
  1.3 107.7 %block_step.1 = (bf16[2,320,1152]{2,1,0:T(8,128)(2,1)}, f32[2,320,1152]{2,1,0:T(8,128)}, bf16[32,416,128]{2,1,0:T(8,128)(2,1)}) custom-call(s32[4,9]{1,0:T(4,128)} %bitcast.26, s32[32]{0:T(128)} %order.3, bf16[2,320,1152]{2,1,0:T(8,128)(2,1)} %bitcast.16, bf16[2,320,1152]{2,1,0:T(8,128)(2,1)} %bitcast.17, f32[320,2560]{1,0:T(8,128)} %ma.3, f32[1280,640]{1,0:T(8,128)} %mb.3, ...), custom_call_target="tpu_custom_call" | custom-call | tf_op jit(solution)/shard_map/block_step/pallas_call | solution.py:720
  109.0 47.6 %exchange.1 = (f32[400,128]{1,0:T(8,128)}, bf16[2,2,2,2,2,416,128]{6,5,4,3,2,1,0:T(8,128)(2,1)}) custom-call(bf16[2,2,2,2,2,416,128]{6,5,4,3,2,1,0:T(8,128)(2,1)} %bitcast.14, f32[400,128]{1,0:T(8,128)} %bitcast.18, f32[400,128]{1,0:T(8,128)} %bitcast.20, s32[1]{0:T(128)S(6)} %copy.29.steps), custom_call_target="tpu_custom_call" | custom-call | tf_op jit(solution)/shard_map/exchange/pallas_call | solution.py:1097
  156.6 15.9 %restore.1 = (f32[320,2560]{1,0:T(8,128)}, f32[1280,640]{1,0:T(8,128)}, bf16[320,2560]{1,0:T(8,128)(2,1)}, bf16[1280,640]{1,0:T(8,128)(2,1)}, f32[55,320]{1,0:T(...) custom-call(bf16[32,416,128]{2,1,0:T(8,128)(2,1)} %bitcast.15, ...), custom_call_target="tpu_custom_call" | custom-call | tf_op jit(solution)/shard_map/restore/pallas_call | solution.py:917

commit v7 on v6

--- a/solution.py
+++ b/solution.py
@@ -313,9 +313,6 @@
         h2t[r] = jnp.transpose(h2s[rows, :])
     for ref in (tmp, xs):
         ref[...] = jnp.zeros(ref.shape, F32)
-    for ref in (hid_c, du_c):
-        ref[...] = jnp.zeros(ref.shape, BF16)
-
     def columns(group):
         return pl.ds(pl.multiple_of(group * 256, 256), 256)
 
@@ -431,17 +428,24 @@
         for piece in feed(0, big, *sets[big][:2]):
             piece()
 
-    def group_step(group, carry):
-        after = jnp.minimum(group + 1, groups - 1)
-        before = jnp.maximum(group - 1, 0)
-        plans = ((group, 2, before, 2), (after, 0, group, 0), (after, 1, group, 1))
+    def group_step(group, first, last):
+        after = group + 1 if first else jnp.minimum(group + 1, groups - 1)
+        plans = ((group, 2, group - 1, 2), (after, 0, group, 0), (after, 1, group, 1))
         for big, (feed_group, feed_big, drain_group, drain_big) in enumerate(plans):
-            extras = drain(drain_group, drain_big, *sets[drain_big][2:])
-            later = feed(feed_group, feed_big, *sets[feed_big][:2])
-            mix(group, *sets[big], extras + later)
+            extras = []
+            if big or not first:
+                extras += drain(drain_group, drain_big, *sets[drain_big][2:])
+            if not (big and last):
+                extras += feed(feed_group, feed_big, *sets[feed_big][:2])
+            mix(group, *sets[big], extras)
+
+    def group_pair(number, carry):
+        for k in range(2):
+            group_step(2 * number + k + 1, False, False)
         return carry
 
-    lax.fori_loop(0, groups, group_step, 0)
+    group_step(0, True, False)
+    lax.fori_loop(0, (groups - 1) // 2, group_pair, 0)
     for piece in drain(groups - 1, 2, *sets[2][2:]):
         piece()
 

time: 173 us -> 168 us (0.971)
  Pallas kernels: 171 us -> 166 us
    pallas_call x1, Pallas kernels: 108 us -> 102 us  [run_block(): pl.pallas_call(functools.partial(block_kernel, per=per, per_block=per_blo...]
where the time goes in v7:
time: 168 us; the launch traced here: 167 us
  Pallas kernels  166 us (99%)
    pallas_call x1, Pallas kernels, run_block(): pl.pallas_call(functools.partial(block_kernel, per=per, per_block=per_blo...  102 us
    pallas_call x1, Pallas kernels, exchange_plan(): pl.pallas_call(functools.partial(exchange_kernel, plan=plan, bits=bits, d...  47.6 us
    pallas_call x1, Pallas kernels, restore_blocks(): pl.pallas_call(functools.partial(restore_kernel, per_block=per_block), na...  16 us

profile of v7, /device:TPU:0, one launch (start us, length us, event | category | flops | bytes accessed | tf_op | source)
XLA Modules:
  0.0 167.5 jit_solution(11200002726306795110)
XLA Ops:
  1.3 102.5 %block_step.1 = (bf16[2,320,1152]{2,1,0:T(8,128)(2,1)}, f32[2,320,1152]{2,1,0:T(8,128)}, bf16[32,416,128]{2,1,0:T(8,128)(2,1)}) custom-call(s32[4,9]{1,0:T(4,128)} %bitcast.26, s32[32]{0:T(128)} %order.3, bf16[2,320,1152]{2,1,0:T(8,128)(2,1)} %bitcast.16, bf16[2,320,1152]{2,1,0:T(8,128)(2,1)} %bitcast.17, f32[320,2560]{1,0:T(8,128)} %ma.3, f32[1280,640]{1,0:T(8,128)} %mb.3, ...), custom_call_target="tpu_custom_call" | custom-call | tf_op jit(solution)/shard_map/block_step/pallas_call | solution.py:724
  103.8 47.6 %exchange.1 = (f32[400,128]{1,0:T(8,128)}, bf16[2,2,2,2,2,416,128]{6,5,4,3,2,1,0:T(8,128)(2,1)}) custom-call(bf16[2,2,2,2,2,416,128]{6,5,4,3,2,1,0:T(8,128)(2,1)} %bitcast.14, f32[400,128]{1,0:T(8,128)} %bitcast.18, f32[400,128]{1,0:T(8,128)} %bitcast.20, s32[1]{0:T(128)S(6)} %copy.29.steps), custom_call_target="tpu_custom_call" | custom-call | tf_op jit(solution)/shard_map/exchange/pallas_call | solution.py:1101
  151.4 16.0 %restore.1 = (f32[320,2560]{1,0:T(8,128)}, f32[1280,640]{1,0:T(8,128)}, bf16[320,2560]{1,0:T(8,128)(2,1)}, bf16[1280,640]{1,0:T(8,128)(2,1)}, f32[55,320]{1,0:T(...) custom-call(bf16[32,416,128]{2,1,0:T(8,128)(2,1)} %bitcast.15, ...), custom_call_target="tpu_custom_call" | custom-call | tf_op jit(solution)/shard_map/restore/pallas_call | solution.py:921
